TPU v7x, 32 devices: a whole 2x2x4 slice. The times are simulated.
32 devices in a mesh: groups: 2 (over x), hop: 16 (over z, y, core).
Axes of the slice: x: 2, y: 2, z: 4, core: 2. Of those that a mesh axis runs over, the one named last changes fastest.
Arguments:
- features: bfloat16 [131072, 384], P(('groups', 'hop')), parts along dimension 0, may hold values from -0.29882812 to 0.29882812
- targets: bfloat16 [131072, 384], P(('groups', 'hop')), parts along dimension 0, may hold values from -6 to 6
- row_index: int32 [32, 2, 3, 512], P(('groups', 'hop')), parts along dimension 0, may hold values from 0 to 4095
- hop_order: int32 [4, 16], P('groups'), parts along dimension 0, may hold values from 0 to 15, each once within a row
- weight_in: float32 [32, 384, 512], P(('groups', 'hop')), parts along dimension 0, may hold values from -0.3125 to 0.3125
- weight_out: float32 [32, 512, 384], P(('groups', 'hop')), parts along dimension 0, may hold values from -0.25 to 0.25
- moment_in: bfloat16 [32, 384, 512], P(('groups', 'hop')), parts along dimension 0, may hold values from -0.119628906 to 0.119628906
- moment_out: bfloat16 [32, 512, 384], P(('groups', 'hop')), parts along dimension 0, may hold values from -0.119628906 to 0.119628906
Outputs:
- new_weight_in: float32 [32, 384, 512], P(('groups', 'hop')), parts along dimension 0
- new_weight_out: float32 [32, 512, 384], P(('groups', 'hop')), parts along dimension 0
- new_moment_in: bfloat16 [32, 384, 512], P(('groups', 'hop')), parts along dimension 0
- new_moment_out: bfloat16 [32, 512, 384], P(('groups', 'hop')), parts along dimension 0
There are 2 independent parts, one for each index of `groups`. A program takes and returns all parts, laid end to end along the dimension named above; each array names one. Nothing has to cross between parts.
Inputs may be any that keep to these rules, and one draw needn't show every extreme that they name: `hop_order`: each row is a permutation of 0 to 15.
All inputs are finite; a program needn't handle non-finite values.
Results may differ from a plain program's by a relative error of at most 0.015.
Values may be sent and summed in bfloat16 or wider, within the bound.
No kernel may reach another device: no remote copies, remote signals or barrier semaphores. Data moves between devices by JAX's collectives and lax.ppermute only.
A program may use at most 64 MiB of HBM per device.

v0:
```python
import jax
import jax.numpy as jnp
from jax import lax
from jax.sharding import PartitionSpec as P

STEPS = 3
VISITS = 2


MOMENTUM = 0.9
LEARN_RATE = 0.1


def normal_cdf(values):
    return 0.5 * (1.0 + lax.erf(values * 0.7071067811865476))


def normal_pdf(values):
    return 0.3989422804014327 * jnp.exp(-0.5 * values * values)


def train_step(model, batch_x, batch_y):
    weight_in, weight_out, moment_in, moment_out = model
    cast_in = weight_in.astype(jnp.bfloat16)
    cast_out = weight_out.astype(jnp.bfloat16)
    preact = jnp.dot(batch_x, cast_in, preferred_element_type=jnp.float32)
    hidden = (preact * normal_cdf(preact)).astype(jnp.bfloat16)
    error_rows = (
        batch_x.astype(jnp.float32)
        + jnp.dot(hidden, cast_out, preferred_element_type=jnp.float32)
        - batch_y.astype(jnp.float32)
    )
    d_out = (error_rows / batch_x.shape[0]).astype(jnp.bfloat16)
    grad_out = lax.dot_general(
        hidden, d_out, (((0,), (0,)), ((), ())), preferred_element_type=jnp.float32
    )
    d_hidden = lax.dot_general(
        d_out, cast_out, (((1,), (1,)), ((), ())), preferred_element_type=jnp.float32
    )
    d_preact = (d_hidden * (normal_cdf(preact) + preact * normal_pdf(preact))).astype(jnp.bfloat16)
    grad_in = lax.dot_general(
        batch_x, d_preact, (((0,), (0,)), ((), ())), preferred_element_type=jnp.float32
    )
    moment_in = (MOMENTUM * moment_in.astype(jnp.float32) + grad_in).astype(jnp.bfloat16)
    moment_out = (MOMENTUM * moment_out.astype(jnp.float32) + grad_out).astype(jnp.bfloat16)
    weight_in = weight_in - LEARN_RATE * moment_in.astype(jnp.float32)
    weight_out = weight_out - LEARN_RATE * moment_out.astype(jnp.float32)
    return (weight_in, weight_out, moment_in, moment_out)


def invert(order):
    count = order.shape[0]
    places = jnp.arange(count, dtype=jnp.int32)
    matches = order[:, None] == places[None, :]
    return jnp.sum(jnp.where(matches, places[:, None], 0), axis=0)


def move_model(model, source, devices):
    shapes = [member.shape for member in model]
    first_in, first_out, second_in, second_out = [
        member.reshape(devices, 8, -1) for member in model
    ]
    held = (
        lax.all_to_all(first_in, "hop", split_axis=0, concat_axis=0, tiled=True),
        lax.all_to_all(first_out, "hop", split_axis=0, concat_axis=0, tiled=True),
    )
    left_part = jnp.take(held[0], source, axis=0)
    right_part = jnp.take(held[1], source, axis=0)
    held = (
        lax.all_to_all(second_in, "hop", split_axis=0, concat_axis=0, tiled=True),
        lax.all_to_all(second_out, "hop", split_axis=0, concat_axis=0, tiled=True),
    )
    settle_left_part = jnp.take(held[0], source, axis=0)
    settle_right_part = jnp.take(held[1], source, axis=0)
    moved = (
        lax.all_to_all(left_part, "hop", split_axis=0, concat_axis=0, tiled=True),
        lax.all_to_all(right_part, "hop", split_axis=0, concat_axis=0, tiled=True),
        lax.all_to_all(settle_left_part, "hop", split_axis=0, concat_axis=0, tiled=True),
        lax.all_to_all(settle_right_part, "hop", split_axis=0, concat_axis=0, tiled=True),
    )
    return tuple((member.reshape(shape) for member, shape in zip(moved, shapes)))


def move_batch(batch, source, devices):
    shape = batch[0].shape
    rows_x = batch[0].reshape(devices, 8, -1)
    rows_y = batch[1].reshape(devices, 8, -1)
    left_part = jnp.take(
        lax.all_to_all(rows_x, "hop", split_axis=0, concat_axis=0, tiled=True), source, axis=0
    )
    right_part = jnp.take(
        lax.all_to_all(rows_y, "hop", split_axis=0, concat_axis=0, tiled=True), source, axis=0
    )
    return (
        lax.all_to_all(left_part, "hop", split_axis=0, concat_axis=0, tiled=True).reshape(shape),
        lax.all_to_all(right_part, "hop", split_axis=0, concat_axis=0, tiled=True).reshape(shape),
    )


def on_device(
    features, targets, row_index, hop_order, weight_in, weight_out, moment_in, moment_out
):
    devices = lax.axis_size("hop")
    model = (weight_in[0], weight_out[0], moment_in[0], moment_out[0])
    placed = jnp.arange(devices, dtype=jnp.int32)
    batches = []
    for visit_index in range(VISITS):
        picks = row_index[0, visit_index].reshape(-1)
        batch = (jnp.take(features, picks, axis=0), jnp.take(targets, picks, axis=0))
        if visit_index > 0:
            batch = move_batch(batch, placed, devices)
        batches.append(batch)
        placed = jnp.take(hop_order[visit_index], placed, axis=0)
    batch_rows = row_index.shape[3]
    for visit_index in range(VISITS):
        for step_index in range(STEPS):
            start = step_index * batch_rows
            model = train_step(
                model,
                batches[visit_index][0][start : start + batch_rows],
                batches[visit_index][1][start : start + batch_rows],
            )
    model = move_model(model, invert(placed), devices)
    return (model[0][None], model[1][None], model[2][None], model[3][None])


def solution(mesh):
    in_specs = (
        P(("groups", "hop"), None),
        P(("groups", "hop"), None),
        P(("groups", "hop"), None, None, None),
        P("groups", None),
        P(("groups", "hop"), None, None),
        P(("groups", "hop"), None, None),
        P(("groups", "hop"), None, None),
        P(("groups", "hop"), None, None),
    )
    out_specs = (
        P(("groups", "hop"), None, None),
        P(("groups", "hop"), None, None),
        P(("groups", "hop"), None, None),
        P(("groups", "hop"), None, None),
    )
    return jax.shard_map(
        on_device, mesh=mesh, in_specs=in_specs, out_specs=out_specs, check_vma=False
    )
```

profile of v0, /device:TPU:1, one launch (start us, length us, event | category | flops | bytes accessed | tf_op | source)
XLA Modules:
  0.0 345.5 jit_solution(12835269164537412370)
XLA Ops:
  2.6 5.3 %gather_fusion.5 = bf16[1536,384]{1,0:T(8,128)(2,1)} fusion(bf16[4096,384]{1,0:T(8,128)(2,1)S(1)} %copy-done, s32[2048]{0:T(1024)S(1)} %pad_clamp_fusion), kind=kCustom, calls=%fused_computation.7.clone | custom fusion | bytes 2365440 | tf_op jit(solution)/shard_map/jit(_take)/gather | solution.py:109
  7.8 7.3 %gather_fusion.2 = bf16[1536,384]{1,0:T(8,128)(2,1)} fusion(bf16[4096,384]{1,0:T(8,128)(2,1)} %param.18, s32[2048]{0:T(1024)S(1)} %pad_clamp_fusion), kind=kCustom, calls=%fused_computation.6.clone | custom fusion | bytes 2365440 | tf_op jit(solution)/shard_map/jit(_take)/gather | solution.py:109
  15.2 3.5 %broadcast_select_fusion.2 = (bf16[1536,384]{1,0:T(8,128)(2,1)}, bf16[1536,384]{1,0:T(8,128)(2,1)}) fusion(bf16[1536,384]{1,0:T(8,128)(2,1)} %gather_fusion.5, pred[1536]{0:T(1024)(128)(4,1)S(1)} %compare_and_fusion, bf16[1536,384]{1,0:T(8,128)(2,1)} %gather_fusion.2), kind=kLoop, calls=%fused_computation.90 | loop fusion | flops 1179648 | bytes 4720128 | tf_op jit(solution)/shard_map/jit(_take)/select_n | solution.py:109
  18.6 3.3 reshape.66
  21.9 7.3 %all-to-all-start.2 = ((bf16[16,8,4608]{2,1,0:T(8,128)(2,1)}), bf16[16,8,4608]{2,1,0:T(8,128)(2,1)}, u32[]{:S(2)}, u32[]{:S(2)}) async-start(bf16[16,8,4608]{2,1,0:T(8,128)(2,1)} %reshape.66), calls=%async_computation.2 | async-start | bytes 2359296 | tf_op jit(solution)/shard_map/all_to_all | solution.py:92
  29.2 3.3 reshape.64
  32.5 22.4 %all-to-all-done.2 = bf16[16,8,4608]{2,1,0:T(8,128)(2,1)} async-done(((bf16[16,8,4608]{2,1,0:T(8,128)(2,1)}), bf16[16,8,4608]{2,1,0:T(8,128)(2,1)}, u32[]{:S(2)}, u32[]{:S(2)}) %all-to-all-start.2) | async-done | bytes 1179680 | tf_op jit(solution)/shard_map/all_to_all | solution.py:92
  54.9 6.9 %all-to-all-start = ((bf16[16,8,4608]{2,1,0:T(8,128)(2,1)}), bf16[16,8,4608]{2,1,0:T(8,128)(2,1)}, u32[]{:S(2)}, u32[]{:S(2)}) async-start(bf16[16,8,4608]{2,1,0:T(8,128)(2,1)} %reshape.64), calls=%async_computation | async-start | bytes 2359296 | tf_op jit(solution)/shard_map/all_to_all | solution.py:89
  61.9 5.3 %gather_fusion.1 = bf16[1536,384]{1,0:T(8,128)(2,1)} fusion(bf16[4096,384]{1,0:T(8,128)(2,1)S(1)} %copy-done, s32[2048]{0:T(1024)S(1)} %pad_clamp_fusion.1), kind=kCustom, calls=%fused_computation.5.clone | custom fusion | bytes 2365440 | tf_op jit(solution)/shard_map/jit(_take)/gather | solution.py:109
  67.2 7.3 %gather_fusion = bf16[1536,384]{1,0:T(8,128)(2,1)} fusion(bf16[4096,384]{1,0:T(8,128)(2,1)} %param.18, s32[2048]{0:T(1024)S(1)} %pad_clamp_fusion.1), kind=kCustom, calls=%fused_computation.clone | custom fusion | bytes 2365440 | tf_op jit(solution)/shard_map/jit(_take)/gather | solution.py:109
  77.2 10.3 %all-to-all-done = bf16[16,8,4608]{2,1,0:T(8,128)(2,1)} async-done(((bf16[16,8,4608]{2,1,0:T(8,128)(2,1)}), bf16[16,8,4608]{2,1,0:T(8,128)(2,1)}, u32[]{:S(2)}, u32[]{:S(2)}) %all-to-all-start) | async-done | bytes 1179680 | tf_op jit(solution)/shard_map/all_to_all | solution.py:89
  91.1 6.9 %all-to-all-start.1 = ((bf16[16,8,4608]{2,1,0:T(8,128)(2,1)}), bf16[16,8,4608]{2,1,0:T(8,128)(2,1)}, u32[]{:S(2)}, u32[]{:S(2)}) async-start(bf16[16,8,4608]{2,1,0:T(8,128)(2,1)} %get-tuple-element.24), calls=%async_computation.1 | async-start | bytes 2359296 | tf_op jit(solution)/shard_map/all_to_all | solution.py:95
  98.0 2.1 broadcast_select_fusion.4
  102.4 2.5 fusion.39
  108.6 2.2 fusion.44
  110.8 12.9 %all-to-all-done.1 = bf16[16,8,4608]{2,1,0:T(8,128)(2,1)} async-done(((bf16[16,8,4608]{2,1,0:T(8,128)(2,1)}), bf16[16,8,4608]{2,1,0:T(8,128)(2,1)}, u32[]{:S(2)}, u32[]{:S(2)}) %all-to-all-start.1) | async-done | bytes 1179680 | tf_op jit(solution)/shard_map/all_to_all | solution.py:95
  123.7 6.9 %all-to-all-start.3 = ((bf16[16,8,4608]{2,1,0:T(8,128)(2,1)}), bf16[16,8,4608]{2,1,0:T(8,128)(2,1)}, u32[]{:S(2)}, u32[]{:S(2)}) async-start(bf16[16,8,4608]{2,1,0:T(8,128)(2,1)} %get-tuple-element.23), calls=%async_computation.3 | async-start | bytes 2359296 | tf_op jit(solution)/shard_map/all_to_all | solution.py:96
  130.6 2.8 fusion.99
  133.4 3.5 %fusion.37 = f32[384,512]{1,0:T(8,128)} fusion(bf16[512,384]{1,0:T(8,128)(2,1)} %fusion.44, f32[512,512]{1,0:T(8,128)} %get-tuple-element.28, f32[384,512]{1,0:T(8,128)} %copy-done.5, bf16[1536,384]{1,0:T(8,128)(2,1)S(1)} %get-tuple-element.16, f32[512,384]{1,0:T(8,128)S(1)} %get-tuple-element.29), kind=kOutput, calls=%fused_computation.79 | convolution fusion | flops 406257664 | bytes 4194304 | tf_op jit(solution)/shard_map/dot_general | solution.py:41
  136.9 2.9 multiply_convert_fusion.3
  142.8 3.9 %multiply_subtract_fusion.7 = (f32[384,512]{1,0:T(8,128)S(1)}, f32[384,512]{1,0:T(8,128)}) fusion(f32[384,512]{1,0:T(8,128)} %fusion.37, f32[384,512]{1,0:T(8,128)} %copy-done.5, f32[1,384,512]{2,1,0:T(8,128)S(1)} %copy-done.2, bf16[512,384]{1,0:T(8,128)(2,1)} %copy-done.19, bf16[512,384]{1,0:T(8,128)(2,1)S(1)} %get-tuple-element.33, ...), kind=kOutput, calls=%fused_computation.141 | convolution fusion | flops 407240704 | bytes 6160384 | tf_op jit(solution)/shard_map/dot_general | solution.py:41
  146.7 3.3 reshape.65
  150.0 2.4 multiply_convert_fusion.2
  152.4 3.9 %all-to-all-done.3 = bf16[16,8,4608]{2,1,0:T(8,128)(2,1)} async-done(((bf16[16,8,4608]{2,1,0:T(8,128)(2,1)}), bf16[16,8,4608]{2,1,0:T(8,128)(2,1)}, u32[]{:S(2)}, u32[]{:S(2)}) %all-to-all-start.3) | async-done | bytes 1179680 | tf_op jit(solution)/shard_map/all_to_all | solution.py:96
  156.3 3.3 reshape.67
  162.8 2.5 fusion.33
  165.3 2.8 multiply_convert_fusion.1
  171.2 3.6 %fusion.31 = f32[384,512]{1,0:T(8,128)} fusion(bf16[512,384]{1,0:T(8,128)(2,1)} %copy-done.22, bf16[512,384]{1,0:T(8,128)(2,1)S(1)} %copy-done.21, f32[512,512]{1,0:T(8,128)} %get-tuple-element.42, f32[384,512]{1,0:T(8,128)} %copy-done.6, bf16[1536,384]{1,0:T(8,128)(2,1)} %reshape.65), kind=kOutput, calls=%fused_computation.73 | convolution fusion | flops 406061056 | bytes 3801088 | tf_op jit(solution)/shard_map/dot_general | solution.py:41
  174.8 2.9 multiply_convert_fusion
  180.8 2.0 reshape.71
  182.8 6.9 %all-to-all-start.10 = ((bf16[16,8,1536]{2,1,0:T(8,128)(2,1)}), bf16[16,8,1536]{2,1,0:T(8,128)(2,1)}, u32[]{:S(2)}, u32[]{:S(2)}) async-start(bf16[16,8,1536]{2,1,0:T(8,128)(2,1)} %reshape.71), calls=%async_computation.10 | async-start | bytes 786432 | tf_op jit(solution)/shard_map/all_to_all | solution.py:71
  189.7 3.8 %multiply_subtract_fusion.1 = (f32[384,512]{1,0:T(8,128)}, bf16[384,512]{1,0:T(8,128)(2,1)}) fusion(f32[384,512]{1,0:T(8,128)} %fusion.31, f32[384,512]{1,0:T(8,128)S(1)} %get-tuple-element.35, f32[384,512]{1,0:T(8,128)} %copy-done.6, bf16[512,384]{1,0:T(8,128)(2,1)S(1)} %fusion.40, f32[512,512]{1,0:T(8,128)} %get-tuple-element.48, ...), kind=kOutput, calls=%fused_computation.135 | convolution fusion | flops 407437312 | bytes 6160384 | tf_op jit(solution)/shard_map/dot_general | solution.py:41
  193.5 2.0 reshape.70
  195.5 6.1 %all-to-all-done.10 = bf16[16,8,1536]{2,1,0:T(8,128)(2,1)} async-done(((bf16[16,8,1536]{2,1,0:T(8,128)(2,1)}), bf16[16,8,1536]{2,1,0:T(8,128)(2,1)}, u32[]{:S(2)}, u32[]{:S(2)}) %all-to-all-start.10) | async-done | bytes 393248 | tf_op jit(solution)/shard_map/all_to_all | solution.py:71
  201.7 3.7 %all-to-all-start.8 = ((bf16[16,8,1536]{2,1,0:T(8,128)(2,1)}), bf16[16,8,1536]{2,1,0:T(8,128)(2,1)S(1)}, u32[]{:S(2)}, u32[]{:S(2)}) async-start(bf16[16,8,1536]{2,1,0:T(8,128)(2,1)} %reshape.70), calls=%async_computation.8 | async-start | bytes 786432 | tf_op jit(solution)/shard_map/all_to_all | solution.py:70
  206.4 10.9 %all-to-all-done.8 = bf16[16,8,1536]{2,1,0:T(8,128)(2,1)S(1)} async-done(((bf16[16,8,1536]{2,1,0:T(8,128)(2,1)}), bf16[16,8,1536]{2,1,0:T(8,128)(2,1)S(1)}, u32[]{:S(2)}, u32[]{:S(2)}) %all-to-all-start.8) | async-done | bytes 393248 | tf_op jit(solution)/shard_map/all_to_all | solution.py:70
  217.4 3.8 %all-to-all-start.6 = ((f32[16,8,1536]{2,1,0:T(8,128)}), f32[16,8,1536]{2,1,0:T(8,128)S(1)}, u32[]{:S(2)}, u32[]{:S(2)}) async-start(f32[16,8,1536]{2,1,0:T(8,128)} %reshape.69), calls=%async_computation.6 | async-start | bytes 1572864 | tf_op jit(solution)/shard_map/all_to_all | solution.py:65
  222.3 17.5 %all-to-all-done.6 = f32[16,8,1536]{2,1,0:T(8,128)S(1)} async-done(((f32[16,8,1536]{2,1,0:T(8,128)}), f32[16,8,1536]{2,1,0:T(8,128)S(1)}, u32[]{:S(2)}, u32[]{:S(2)}) %all-to-all-start.6) | async-done | bytes 786464 | tf_op jit(solution)/shard_map/all_to_all | solution.py:65
  239.8 5.4 %all-to-all-start.4 = ((f32[16,8,1536]{2,1,0:T(8,128)}), f32[16,8,1536]{2,1,0:T(8,128)S(1)}, u32[]{:S(2)}, u32[]{:S(2)}) async-start(f32[16,8,1536]{2,1,0:T(8,128)} %reshape.68), calls=%async_computation.4 | async-start | bytes 1572864 | tf_op jit(solution)/shard_map/all_to_all | solution.py:64
  249.1 14.8 %all-to-all-done.4 = f32[16,8,1536]{2,1,0:T(8,128)S(1)} async-done(((f32[16,8,1536]{2,1,0:T(8,128)}), f32[16,8,1536]{2,1,0:T(8,128)S(1)}, u32[]{:S(2)}, u32[]{:S(2)}) %all-to-all-start.4) | async-done | bytes 786464 | tf_op jit(solution)/shard_map/all_to_all | solution.py:64
  263.9 17.1 %all_to_all.60 = bf16[16,8,1536]{2,1,0:T(8,128)(2,1)S(1)} all-to-all(bf16[16,8,1536]{2,1,0:T(8,128)(2,1)S(1)} %get-tuple-element.20), channel_id=1, replica_groups=mesh['groups'=2,'hop'=16] {'hop'}, dimensions={0} | all-to-all | bytes 786432 | tf_op jit(solution)/shard_map/all_to_all | solution.py:78
  281.0 3.7 %all-to-all-start.11 = ((bf16[16,8,1536]{2,1,0:T(8,128)(2,1)}), bf16[16,8,1536]{2,1,0:T(8,128)(2,1)S(1)}, u32[]{:S(2)}, u32[]{:S(2)}) async-start(bf16[16,8,1536]{2,1,0:T(8,128)(2,1)} %get-tuple-element.19), calls=%async_computation.11 | async-start | bytes 786432 | tf_op jit(solution)/shard_map/all_to_all | solution.py:79
  287.0 9.6 %all-to-all-done.11 = bf16[16,8,1536]{2,1,0:T(8,128)(2,1)S(1)} async-done(((bf16[16,8,1536]{2,1,0:T(8,128)(2,1)}), bf16[16,8,1536]{2,1,0:T(8,128)(2,1)S(1)}, u32[]{:S(2)}, u32[]{:S(2)}) %all-to-all-start.11) | async-done | bytes 393248 | tf_op jit(solution)/shard_map/all_to_all | solution.py:79
  296.7 24.2 %all_to_all.61 = f32[16,8,1536]{2,1,0:T(8,128)} all-to-all(f32[16,8,1536]{2,1,0:T(8,128)S(1)} %get-tuple-element.22), channel_id=1, replica_groups=mesh['groups'=2,'hop'=16] {'hop'}, dimensions={0} | all-to-all | bytes 1572864 | tf_op jit(solution)/shard_map/all_to_all | solution.py:76
  320.9 4.2 %all-to-all-start.7 = ((f32[16,8,1536]{2,1,0:T(8,128)}), f32[16,8,1536]{2,1,0:T(8,128)}, u32[]{:S(2)}, u32[]{:S(2)}) async-start(f32[16,8,1536]{2,1,0:T(8,128)} %get-tuple-element.21), calls=%async_computation.7 | async-start | bytes 1572864 | tf_op jit(solution)/shard_map/all_to_all | solution.py:77
  327.0 2.3 broadcast_in_dim_reshape.12
  329.3 13.9 %all-to-all-done.7 = f32[16,8,1536]{2,1,0:T(8,128)} async-done(((f32[16,8,1536]{2,1,0:T(8,128)}), f32[16,8,1536]{2,1,0:T(8,128)}, u32[]{:S(2)}, u32[]{:S(2)}) %all-to-all-start.7) | async-done | bytes 786464 | tf_op jit(solution)/shard_map/all_to_all | solution.py:77
  343.2 2.2 broadcast_in_dim_reshape.13
  (94 shorter events, 36.5 us)
Async XLA Ops:
  0.6 1.9 copy-start
  21.9 33.0 %all-to-all-start.2 = ((bf16[16,8,4608]{2,1,0:T(8,128)(2,1)}), bf16[16,8,4608]{2,1,0:T(8,128)(2,1)}, u32[]{:S(2)}, u32[]{:S(2)}) async-start(bf16[16,8,4608]{2,1,0:T(8,128)(2,1)} %reshape.66), calls=%async_computation.2 | async-start | bytes 2359296 | tf_op jit(solution)/shard_map/all_to_all | solution.py:92
  54.9 32.6 %all-to-all-start = ((bf16[16,8,4608]{2,1,0:T(8,128)(2,1)}), bf16[16,8,4608]{2,1,0:T(8,128)(2,1)}, u32[]{:S(2)}, u32[]{:S(2)}) async-start(bf16[16,8,4608]{2,1,0:T(8,128)(2,1)} %reshape.64), calls=%async_computation | async-start | bytes 2359296 | tf_op jit(solution)/shard_map/all_to_all | solution.py:89
  67.2 7.3 %copy-start.23 = (s32[2,16]{1,0:T(2,128)S(1)}, s32[2,16]{1,0:T(2,128)}, u32[]{:S(2)}) copy-start(s32[2,16]{1,0:T(2,128)} %param.21) | copy-start | bytes 388
  91.1 32.6 %all-to-all-start.1 = ((bf16[16,8,4608]{2,1,0:T(8,128)(2,1)}), bf16[16,8,4608]{2,1,0:T(8,128)(2,1)}, u32[]{:S(2)}, u32[]{:S(2)}) async-start(bf16[16,8,4608]{2,1,0:T(8,128)(2,1)} %get-tuple-element.24), calls=%async_computation.1 | async-start | bytes 2359296 | tf_op jit(solution)/shard_map/all_to_all | solution.py:95
  98.0 2.1 copy-start.2
  100.1 1.5 copy-start.10
  100.1 39.7 %copy-start.4 = (bf16[1536,384]{1,0:T(8,128)(2,1)}, bf16[1536,384]{1,0:T(8,128)(2,1)S(1)}, u32[]{:S(2)}) copy-start(bf16[1536,384]{1,0:T(8,128)(2,1)S(1)} %get-tuple-element.16) | copy-start | bytes 3538948
  100.2 1.7 copy-start.11
  101.6 0.8 copy-start.8
  104.9 0.9 copy-start.5
  105.8 1.4 copy-start.9
  105.8 1.4 copy-start.12
  105.8 1.4 copy-start.20
  107.2 1.4 copy-start.7
  123.7 32.6 %all-to-all-start.3 = ((bf16[16,8,4608]{2,1,0:T(8,128)(2,1)}), bf16[16,8,4608]{2,1,0:T(8,128)(2,1)}, u32[]{:S(2)}, u32[]{:S(2)}) async-start(bf16[16,8,4608]{2,1,0:T(8,128)(2,1)} %get-tuple-element.23), calls=%async_computation.3 | async-start | bytes 2359296 | tf_op jit(solution)/shard_map/all_to_all | solution.py:96
  139.8 1.6 copy-start.18
  141.4 1.5 copy-start.19
  159.6 1.7 copy-start.15
  165.3 2.8 copy-start.6
  165.3 2.8 copy-start.21
  168.1 1.7 copy-start.16
  169.7 1.5 copy-start.22
  171.2 3.6 %copy-start.3 = (bf16[1536,384]{1,0:T(8,128)(2,1)S(1)}, bf16[1536,384]{1,0:T(8,128)(2,1)}, u32[]{:S(2)}) copy-start(bf16[1536,384]{1,0:T(8,128)(2,1)} %reshape.65) | copy-start | bytes 3538948
  177.7 1.6 copy-start.17
  182.8 18.9 %all-to-all-start.10 = ((bf16[16,8,1536]{2,1,0:T(8,128)(2,1)}), bf16[16,8,1536]{2,1,0:T(8,128)(2,1)}, u32[]{:S(2)}, u32[]{:S(2)}) async-start(bf16[16,8,1536]{2,1,0:T(8,128)(2,1)} %reshape.71), calls=%async_computation.10 | async-start | bytes 786432 | tf_op jit(solution)/shard_map/all_to_all | solution.py:71
  193.5 11.9 %copy-start.13 = (f32[512,384]{1,0:T(8,128)S(1)}, f32[512,384]{1,0:T(8,128)}, u32[]{:S(2)}) copy-start(f32[512,384]{1,0:T(8,128)} %get-tuple-element.49) | copy-start | bytes 2359300
  201.7 15.7 %all-to-all-start.8 = ((bf16[16,8,1536]{2,1,0:T(8,128)(2,1)}), bf16[16,8,1536]{2,1,0:T(8,128)(2,1)S(1)}, u32[]{:S(2)}, u32[]{:S(2)}) async-start(bf16[16,8,1536]{2,1,0:T(8,128)(2,1)} %reshape.70), calls=%async_computation.8 | async-start | bytes 786432 | tf_op jit(solution)/shard_map/all_to_all | solution.py:70
  206.4 14.8 %copy-start.14 = (f32[384,512]{1,0:T(8,128)S(1)}, f32[384,512]{1,0:T(8,128)}, u32[]{:S(2)}) copy-start(f32[384,512]{1,0:T(8,128)} %get-tuple-element.51) | copy-start | bytes 2359300
  217.4 22.5 %all-to-all-start.6 = ((f32[16,8,1536]{2,1,0:T(8,128)}), f32[16,8,1536]{2,1,0:T(8,128)S(1)}, u32[]{:S(2)}, u32[]{:S(2)}) async-start(f32[16,8,1536]{2,1,0:T(8,128)} %reshape.69), calls=%async_computation.6 | async-start | bytes 1572864 | tf_op jit(solution)/shard_map/all_to_all | solution.py:65
  239.8 24.0 %all-to-all-start.4 = ((f32[16,8,1536]{2,1,0:T(8,128)}), f32[16,8,1536]{2,1,0:T(8,128)S(1)}, u32[]{:S(2)}, u32[]{:S(2)}) async-start(f32[16,8,1536]{2,1,0:T(8,128)} %reshape.68), calls=%async_computation.4 | async-start | bytes 1572864 | tf_op jit(solution)/shard_map/all_to_all | solution.py:64
  281.0 15.7 %all-to-all-start.11 = ((bf16[16,8,1536]{2,1,0:T(8,128)(2,1)}), bf16[16,8,1536]{2,1,0:T(8,128)(2,1)S(1)}, u32[]{:S(2)}, u32[]{:S(2)}) async-start(bf16[16,8,1536]{2,1,0:T(8,128)(2,1)} %get-tuple-element.19), calls=%async_computation.11 | async-start | bytes 786432 | tf_op jit(solution)/shard_map/all_to_all | solution.py:79
  320.9 22.4 %all-to-all-start.7 = ((f32[16,8,1536]{2,1,0:T(8,128)}), f32[16,8,1536]{2,1,0:T(8,128)}, u32[]{:S(2)}, u32[]{:S(2)}) async-start(f32[16,8,1536]{2,1,0:T(8,128)} %get-tuple-element.21), calls=%async_computation.7 | async-start | bytes 1572864 | tf_op jit(solution)/shard_map/all_to_all | solution.py:77
  327.0 18.5 %copy-start.1 = (bf16[4096,384]{1,0:T(8,128)(2,1)S(1)}, bf16[4096,384]{1,0:T(8,128)(2,1)}, u32[]{:S(2)}) copy-start(bf16[4096,384]{1,0:T(8,128)(2,1)} %param.19) | copy-start | bytes 9437188
where the time goes:
time: 348 us; the launch traced here: 345 us
  waiting for transfers between devices  122 us (35%)
  local copies, waits for them, and re-layouts  62.6 us (18%)
  starting transfers between devices  56 us (16%)
  matrix products  52.8 us (15%)
  blocking collectives  41.3 us (12%)
  other arithmetic  9.41 us (3%)
    all_to_all x1, blocking collectives, move_model(): lax.all_to_all(left_part, 'hop', split_axis=0, concat_axis=0, tiled=True)  24.2 us
    all_to_all x1, waiting for transfers between devices, move_batch(): lax.all_to_all(rows_y, 'hop', split_axis=0, concat_axis=0, tiled=True)  22.4 us
    dot_general x6, matrix products, train_step(): lax.dot_general(batch_x, d_preact, (((0,), (0,)), ((), ())), preferred_el...  19.8 us
    all_to_all x1, waiting for transfers between devices, move_model(): lax.all_to_all(first_out, 'hop', split_axis=0, concat_axis=0, tiled=True)  17.5 us
    all_to_all x1, blocking collectives, move_model(): lax.all_to_all(settle_left_part, 'hop', split_axis=0, concat_axis=0, tile...  17.1 us
    all_to_all x1, waiting for transfers between devices, move_model(): lax.all_to_all(first_in, 'hop', split_axis=0, concat_axis=0, tiled=True)  14.8 us
    gather x2, local copies, waits for them, and re-layouts, on_device(): jnp.take(features, picks, axis=0)  14.7 us
    all_to_all x1, waiting for transfers between devices, move_model(): lax.all_to_all(right_part, 'hop', split_axis=0, concat_axis=0, tiled=True)  13.9 us
  transfers between devices with their start and end apart: 10, of which 10 were waited for; matrix products, arithmetic and copies ran while one was open for 20% of the time, Pallas kernels for 0%

commit v1 on v0

v1 whole, which is shorter than its diff:
```python
import functools

import jax
import jax.numpy as jnp
from jax import lax
from jax.experimental import pallas as pl
from jax.experimental.pallas import tpu as pltpu
from jax.sharding import PartitionSpec as P

MOMENTUM = 0.9
LEARN_RATE = 0.1
SUB, LANE = 8, 128
F32, BF16 = jnp.float32, jnp.bfloat16
HALF_ROOT = 0.7071067811865476
PDF_SCALE = 0.3989422804014327


def tiles_of(shape):
    rows, cols = shape[-2:]
    return [
        (row * SUB, col * LANE) for row in range(rows // SUB) for col in range(cols // LANE)
    ]


def tile_slots(shapes, devices):
    slots, base = [], 0
    for shape in shapes:
        tiles = tiles_of(shape)
        if len(tiles) % devices:
            raise ValueError("uneven tiles")
        each = len(tiles) // devices
        slots.append(
            [(index // each, base + index % each, *tile) for index, tile in enumerate(tiles)]
        )
        base += each
    return slots, base


def pack(refs, slots, packed_ref):
    for ref, places in zip(refs, slots):
        for chunk, slot, row, col in places:
            packed_ref[chunk, slot] = ref[row : row + SUB, col : col + LANE].astype(
                packed_ref.dtype
            )


def unpack(packed_ref, slots, refs):
    for ref, places in zip(refs, slots):
        for chunk, slot, row, col in places:
            ref[row : row + SUB, col : col + LANE] = packed_ref[chunk, slot].astype(ref.dtype)


def train_step(x_ref, y_ref, win, wout, min_, mout, hid, dout, dpre, block):
    rows = x_ref.shape[0]
    cast_in = win[...].astype(BF16)
    cast_out = wout[...].astype(BF16)
    for start in range(0, rows, block):
        part = slice(start, start + block)
        batch_x = x_ref[part, :]
        preact = jnp.dot(batch_x, cast_in, preferred_element_type=F32)
        cdf = 0.5 * (1.0 + lax.erf(preact * HALF_ROOT))
        pdf = PDF_SCALE * jnp.exp(-0.5 * preact * preact)
        hidden = (preact * cdf).astype(BF16)
        hid[part, :] = hidden
        error = (
            batch_x.astype(F32)
            + jnp.dot(hidden, cast_out, preferred_element_type=F32)
            - y_ref[part, :].astype(F32)
        )
        d_out = (error * (1.0 / rows)).astype(BF16)
        dout[part, :] = d_out
        d_hidden = lax.dot_general(
            d_out, cast_out, (((1,), (1,)), ((), ())), preferred_element_type=F32
        )
        dpre[part, :] = (d_hidden * (cdf + preact * pdf)).astype(BF16)
    over_rows = (((0,), (0,)), ((), ()))
    grad = lax.dot_general(hid[...], dout[...], over_rows, preferred_element_type=F32)
    moment = (MOMENTUM * mout[...].astype(F32) + grad).astype(BF16)
    mout[...] = moment
    wout[...] = wout[...] - LEARN_RATE * moment.astype(F32)
    grad = lax.dot_general(x_ref[...], dpre[...], over_rows, preferred_element_type=F32)
    moment = (MOMENTUM * min_[...].astype(F32) + grad).astype(BF16)
    min_[...] = moment
    win[...] = win[...] - LEARN_RATE * moment.astype(F32)


def visit_kernel(slots, packed_input, block, *refs):
    if packed_input:
        x_ref, y_ref, arrived, sent, *scratch = refs
    else:
        x_ref, y_ref, *model, sent = refs[:7]
        scratch = refs[7:]
    state, work = scratch[:4], scratch[4:]
    step = pl.program_id(0)

    @pl.when(step == 0)
    def _():
        if packed_input:
            unpack(arrived, slots, state)
        else:
            for held, given in zip(state, model):
                held[...] = given[...]

    train_step(x_ref, y_ref, *state, *work, block)

    @pl.when(step == pl.num_programs(0) - 1)
    def _():
        pack(state, slots, sent)


def whole(shape):
    return pl.BlockSpec(shape, lambda step: (0,) * len(shape))


def visit(batch_x, batch_y, model, shapes, steps, slots, packed_shape):
    rows, width = batch_x.shape[0] // steps, batch_x.shape[1]
    hidden = shapes[0][1]
    packed_input = len(model) == 1
    batch_spec = pl.BlockSpec((rows, width), lambda step: (step, 0))
    flops = steps * 10 * rows * width * hidden
    return pl.pallas_call(
        functools.partial(visit_kernel, slots, packed_input, rows // 4),
        grid=(steps,),
        in_specs=[batch_spec, batch_spec] + [whole(member.shape) for member in model],
        out_specs=whole(packed_shape),
        out_shape=jax.ShapeDtypeStruct(packed_shape, BF16),
        scratch_shapes=[
            pltpu.VMEM(shapes[0], F32),
            pltpu.VMEM(shapes[1], F32),
            pltpu.VMEM(shapes[2], BF16),
            pltpu.VMEM(shapes[3], BF16),
            pltpu.VMEM((rows, hidden), BF16),
            pltpu.VMEM((rows, width), BF16),
            pltpu.VMEM((rows, hidden), BF16),
        ],
        cost_estimate=pl.CostEstimate(
            flops=flops,
            bytes_accessed=4 * batch_x.size + 8 * width * hidden * 4,
            transcendentals=2 * steps * rows * hidden,
        ),
        name="visit",
    )(batch_x, batch_y, *model)


def reorder_kernel(source_ref, packed_ref, out_ref, sems):
    count = out_ref.shape[0]
    copies = [
        pltpu.make_async_copy(packed_ref.at[source_ref[slot]], out_ref.at[slot], sems.at[slot])
        for slot in range(count)
    ]
    for copy in copies:
        copy.start()
    for copy in copies:
        copy.wait()


def reorder(packed, source):
    return pl.pallas_call(
        reorder_kernel,
        in_specs=[
            pl.BlockSpec(memory_space=pltpu.SMEM),
            pl.BlockSpec(memory_space=pl.ANY),
        ],
        out_specs=pl.BlockSpec(memory_space=pltpu.VMEM),
        out_shape=jax.ShapeDtypeStruct(packed.shape, packed.dtype),
        scratch_shapes=[pltpu.SemaphoreType.DMA((packed.shape[0],))],
        name="reorder",
    )(source, packed)


def unpack_kernel(slots, packed_ref, *out_refs):
    unpack(packed_ref, slots, out_refs)


def invert(order):
    count = order.shape[0]
    places = jnp.arange(count, dtype=jnp.int32)
    matches = order[:, None] == places[None, :]
    return jnp.sum(jnp.where(matches, places[:, None], 0), axis=0).astype(jnp.int32)


def exchange(packed):
    return lax.all_to_all(packed, "hop", split_axis=0, concat_axis=0, tiled=True)


def move(packed, source):
    return exchange(reorder(exchange(packed), source))


def on_device(
    features, targets, row_index, hop_order, weight_in, weight_out, moment_in, moment_out
):
    devices = lax.axis_size("hop")
    model = (weight_in[0], weight_out[0], moment_in[0], moment_out[0])
    shapes = [member.shape for member in model]
    slots, depth = tile_slots(shapes, devices)
    packed_shape = (devices, depth, SUB, LANE)
    _, visits, steps, _ = row_index.shape
    sources = [invert(hop_order[visit_index]) for visit_index in range(visits)]
    held = model
    for visit_index in range(visits):
        picks = row_index[0, visit_index].reshape(-1)
        batch_x = features.at[picks].get(mode="promise_in_bounds")
        batch_y = targets.at[picks].get(mode="promise_in_bounds")
        packed = visit(batch_x, batch_y, held, shapes, steps, slots, packed_shape)
        held = (move(packed, sources[visit_index]),)
    outs = pl.pallas_call(
        functools.partial(unpack_kernel, slots),
        out_shape=[jax.ShapeDtypeStruct(m.shape, m.dtype) for m in model],
        name="unpack",
    )(held[0])
    return tuple(member[None] for member in outs)


def solution(mesh):
    split = P(("groups", "hop"), None, None)
    in_specs = (
        P(("groups", "hop"), None),
        P(("groups", "hop"), None),
        P(("groups", "hop"), None, None, None),
        P("groups", None),
        split,
        split,
        split,
        split,
    )
    return jax.shard_map(
        on_device, mesh=mesh, in_specs=in_specs, out_specs=(split,) * 4, check_vma=False
    )
```

time: 348 us -> 214 us (0.61)
  matrix products: 52.8 us -> 0 us
  waiting for transfers between devices: 122 us -> 83.7 us
  local copies, waits for them, and re-layouts: 62.6 us -> 27 us
  Pallas kernels: 0 us -> 31.3 us
  starting transfers between devices: 56 us -> 24.7 us
  other arithmetic: 9.41 us -> 1.26 us
  blocking collectives: 41.3 us -> 45.1 us
    dot_general x24 -> x0, matrix products: 52.8 us -> none  [the longest x6 19.8 us: train_step(): lax.dot_general(batch_x, d_preact, (((0,), (0,)), ((), ())), preferred_el...]
    all_to_all x10 -> x3, waiting for transfers between devices: 122 us -> 83.7 us  [exchange(): lax.all_to_all(packed, 'hop', split_axis=0, concat_axis=0, tiled=True)]
    all_to_all x10 -> x3, starting transfers between devices: 56 us -> 24.7 us  [exchange(): lax.all_to_all(packed, 'hop', split_axis=0, concat_axis=0, tiled=True)]
    pallas_call x0 -> x5, Pallas kernels: none -> 31.3 us  [the longest x2 21.6 us: visit(): pl.pallas_call(functools.partial(visit_kernel, slots, packed_input, rows...]
    reshape x8 -> x0, local copies, waits for them, and re-layouts: 19.3 us -> none  [the longest x4 6.16 us: move_model(): member.reshape(devices, 8, -1)]
    select_n x9 -> x2, other arithmetic: 9.25 us -> 0.05 us  [on_device(): batch_x = features.at[picks].get(mode='promise_in_bounds')]
    gather x12 -> x4, local copies, waits for them, and re-layouts: 33.7 us -> 25.2 us  [the longest x2 14.6 us: on_device(): batch_x = features.at[picks].get(mode='promise_in_bounds')]
    another operation x6 -> x0, local copies, waits for them, and re-layouts: 6.5 us -> none  [the longest x4 6.48 us: on_device(): return (model[0][None], model[1][None], model[2][None], model[3][None])]
  transfers between devices with their start and end apart: 10 -> 3, of which waited for: 10 -> 3; matrix products, arithmetic and copies ran while one was open for 20% -> 6% of each run, Pallas kernels for 0% -> 0%
where the time goes in v1:
time: 214 us
  waiting for transfers between devices  83.7 us (39%)
  blocking collectives  45.1 us (21%)
  Pallas kernels  31.3 us (15%)
  local copies, waits for them, and re-layouts  27 us (13%)
  starting transfers between devices  24.7 us (12%)
    all_to_all x3, waiting for transfers between devices, exchange(): lax.all_to_all(packed, 'hop', split_axis=0, concat_axis=0, tiled=True)  83.7 us
    all_to_all x1, blocking collectives, exchange(): lax.all_to_all(packed, 'hop', split_axis=0, concat_axis=0, tiled=True)  45.1 us
    all_to_all x3, starting transfers between devices, exchange(): lax.all_to_all(packed, 'hop', split_axis=0, concat_axis=0, tiled=True)  24.7 us
    pallas_call x2, Pallas kernels, visit(): pl.pallas_call(functools.partial(visit_kernel, slots, packed_input, rows...  21.6 us
    gather x2, local copies, waits for them, and re-layouts, on_device(): batch_x = features.at[picks].get(mode='promise_in_bounds')  14.6 us
    gather x2, local copies, waits for them, and re-layouts, on_device(): batch_y = targets.at[picks].get(mode='promise_in_bounds')  10.6 us
    pallas_call x2, Pallas kernels, reorder(): pl.pallas_call(reorder_kernel, in_specs=[pl.BlockSpec(memory_space=pltpu....  6.81 us
  transfers between devices with their start and end apart: 3, of which 3 were waited for; matrix products, arithmetic and copies ran while one was open for 6% of the time, Pallas kernels for 0%

profile of v1, /device:TPU:1, one launch (start us, length us, event | category | flops | bytes accessed | tf_op | source)
XLA Modules:
  0.0 213.8 jit_solution(14984436011410221332)
XLA Ops:
  0.6 0.0 copy-start
  0.6 0.9 fusion.2
  1.6 1.0 copy-done
  2.6 5.3 %gather_fusion.3 = bf16[1536,384]{1,0:T(8,128)(2,1)} fusion(bf16[4096,384]{1,0:T(8,128)(2,1)S(1)} %copy-done, s32[2048]{0:T(1024)S(1)} %pad_clamp_fusion), kind=kCustom, calls=%fused_computation.3 | custom fusion | bytes 2365440 | tf_op jit(solution)/shard_map/gather | solution.py:204
  7.9 7.3 %gather_fusion.2 = bf16[1536,384]{1,0:T(8,128)(2,1)} fusion(bf16[4096,384]{1,0:T(8,128)(2,1)} %param.8, s32[2048]{0:T(1024)S(1)} %pad_clamp_fusion), kind=kCustom, calls=%fused_computation.2 | custom fusion | bytes 2365440 | tf_op jit(solution)/shard_map/gather | solution.py:203
  15.1 10.9 %visit.2 = bf16[16,48,8,128]{3,2,1,0:T(8,128)(2,1)} custom-call(bf16[1536,384]{1,0:T(8,128)(2,1)} %gather_fusion.2, bf16[1536,384]{1,0:T(8,128)(2,1)} %gather_fusion.3, f32[384,512]{1,0:T(8,128)} %bitcast.16, f32[512,384]{1,0:T(8,128)} %bitcast.17, bf16[384,512]{1,0:T(8,128)(2,1)} %bitcast.20, bf16[512,384]{1,0:T(8,128)(2,1)} %bitcast.21), custom_call_target="tpu_custom_call" | custom-call | flops 3019898880 | bytes 8650752 | tf_op jit(solution)/shard_map/visit/pallas_call | solution.py:121
  26.1 0.0 copy-start.1
  26.1 7.5 %all-to-all-start = ((bf16[16,48,8,128]{3,2,1,0:T(8,128)(2,1)}), bf16[16,48,8,128]{3,2,1,0:T(8,128)(2,1)}, u32[]{:S(2)}, u32[]{:S(2)}) async-start(bf16[16,48,8,128]{3,2,1,0:T(8,128)(2,1)} %visit.2), calls=%async_computation | async-start | bytes 3145728 | tf_op jit(solution)/shard_map/all_to_all | solution.py:183
  33.6 0.0 copy-done.1
  33.6 0.6 select_reduce_fusion.source_ref
  34.2 31.9 %all-to-all-done.packed_ref = bf16[16,48,8,128]{3,2,1,0:T(8,128)(2,1)} async-done(((bf16[16,48,8,128]{3,2,1,0:T(8,128)(2,1)}), bf16[16,48,8,128]{3,2,1,0:T(8,128)(2,1)}, u32[]{:S(2)}, u32[]{:S(2)}) %all-to-all-start) | async-done | bytes 1572896 | tf_op jit(solution)/shard_map/all_to_all | solution.py:183
  66.1 3.4 %reorder.2 = bf16[16,48,8,128]{3,2,1,0:T(8,128)(2,1)} custom-call(s32[16]{0:T(128)} %select_reduce_fusion.source_ref, bf16[16,48,8,128]{3,2,1,0:T(8,128)(2,1)} %all-to-all-done.packed_ref), custom_call_target="tpu_custom_call" | custom-call | tf_op jit(solution)/shard_map/reorder/pallas_call | solution.py:158
  69.5 8.6 %all-to-all-start.1 = ((bf16[16,48,8,128]{3,2,1,0:T(8,128)(2,1)}), bf16[16,48,8,128]{3,2,1,0:T(8,128)(2,1)}, u32[]{:S(2)}, u32[]{:S(2)}) async-start(bf16[16,48,8,128]{3,2,1,0:T(8,128)(2,1)} %reorder.2), calls=%async_computation.1 | async-start | bytes 3145728 | tf_op jit(solution)/shard_map/all_to_all | solution.py:183
  78.1 5.3 %gather_fusion.1 = bf16[1536,384]{1,0:T(8,128)(2,1)} fusion(bf16[4096,384]{1,0:T(8,128)(2,1)S(1)} %copy-done, s32[2048]{0:T(1024)S(1)} %pad_clamp_fusion.1), kind=kCustom, calls=%fused_computation.1 | custom fusion | bytes 2365440 | tf_op jit(solution)/shard_map/gather | solution.py:204
  83.4 7.3 %gather_fusion = bf16[1536,384]{1,0:T(8,128)(2,1)} fusion(bf16[4096,384]{1,0:T(8,128)(2,1)} %param.8, s32[2048]{0:T(1024)S(1)} %pad_clamp_fusion.1), kind=kCustom, calls=%fused_computation | custom fusion | bytes 2365440 | tf_op jit(solution)/shard_map/gather | solution.py:203
  90.7 19.9 %all-to-all-done.1.refs_2_ = bf16[16,48,8,128]{3,2,1,0:T(8,128)(2,1)} async-done(((bf16[16,48,8,128]{3,2,1,0:T(8,128)(2,1)}), bf16[16,48,8,128]{3,2,1,0:T(8,128)(2,1)}, u32[]{:S(2)}, u32[]{:S(2)}) %all-to-all-start.1) | async-done | bytes 1572896 | tf_op jit(solution)/shard_map/all_to_all | solution.py:183
  110.5 10.7 %visit.3 = bf16[16,48,8,128]{3,2,1,0:T(8,128)(2,1)} custom-call(bf16[1536,384]{1,0:T(8,128)(2,1)} %gather_fusion, bf16[1536,384]{1,0:T(8,128)(2,1)} %gather_fusion.1, bf16[16,48,8,128]{3,2,1,0:T(8,128)(2,1)} %all-to-all-done.1.refs_2_), custom_call_target="tpu_custom_call" | custom-call | flops 3019898880 | bytes 8650752 | tf_op jit(solution)/shard_map/visit/pallas_call | solution.py:121
  121.2 8.6 %all-to-all-start.2 = ((bf16[16,48,8,128]{3,2,1,0:T(8,128)(2,1)}), bf16[16,48,8,128]{3,2,1,0:T(8,128)(2,1)}, u32[]{:S(2)}, u32[]{:S(2)}) async-start(bf16[16,48,8,128]{3,2,1,0:T(8,128)(2,1)} %visit.3), calls=%async_computation.2 | async-start | bytes 3145728 | tf_op jit(solution)/shard_map/all_to_all | solution.py:183
  129.9 0.6 select_reduce_fusion.1.source_ref
  130.5 31.9 %all-to-all-done.2.packed_ref = bf16[16,48,8,128]{3,2,1,0:T(8,128)(2,1)} async-done(((bf16[16,48,8,128]{3,2,1,0:T(8,128)(2,1)}), bf16[16,48,8,128]{3,2,1,0:T(8,128)(2,1)}, u32[]{:S(2)}, u32[]{:S(2)}) %all-to-all-start.2) | async-done | bytes 1572896 | tf_op jit(solution)/shard_map/all_to_all | solution.py:183
  162.4 3.4 %reorder.3 = bf16[16,48,8,128]{3,2,1,0:T(8,128)(2,1)} custom-call(s32[16]{0:T(128)} %select_reduce_fusion.1.source_ref, bf16[16,48,8,128]{3,2,1,0:T(8,128)(2,1)} %all-to-all-done.2.packed_ref), custom_call_target="tpu_custom_call" | custom-call | tf_op jit(solution)/shard_map/reorder/pallas_call | solution.py:158
  165.8 45.1 %all_to_all.20.packed_ref = bf16[16,48,8,128]{3,2,1,0:T(8,128)(2,1)} all-to-all(bf16[16,48,8,128]{3,2,1,0:T(8,128)(2,1)} %reorder.3), channel_id=1, replica_groups=mesh['groups'=2,'hop'=16] {'hop'}, dimensions={0} | all-to-all | bytes 3145728 | tf_op jit(solution)/shard_map/all_to_all | solution.py:183
  210.9 2.9 %unpack.1 = (f32[384,512]{1,0:T(8,128)}, f32[512,384]{1,0:T(8,128)}, bf16[384,512]{1,0:T(8,128)(2,1)}, bf16[512,384]{1,0:T(8,128)(2,1)}) custom-call(bf16[16,48,8,128]{3,2,1,0:T(8,128)(2,1)} %all_to_all.20.packed_ref), custom_call_target="tpu_custom_call" | custom-call | tf_op jit(solution)/shard_map/unpack/pallas_call | solution.py:207
  (5 shorter events, 0.1 us)
Async XLA Ops:
  0.6 1.9 copy-start
  26.1 7.5 %copy-start.1 = (s32[2,16]{1,0:T(2,128)S(1)}, s32[2,16]{1,0:T(2,128)}, u32[]{:S(2)}) copy-start(s32[2,16]{1,0:T(2,128)} %param.11) | copy-start | bytes 388
  26.1 40.0 %all-to-all-start = ((bf16[16,48,8,128]{3,2,1,0:T(8,128)(2,1)}), bf16[16,48,8,128]{3,2,1,0:T(8,128)(2,1)}, u32[]{:S(2)}, u32[]{:S(2)}) async-start(bf16[16,48,8,128]{3,2,1,0:T(8,128)(2,1)} %visit.2), calls=%async_computation | async-start | bytes 3145728 | tf_op jit(solution)/shard_map/all_to_all | solution.py:183
  69.5 41.1 %all-to-all-start.1 = ((bf16[16,48,8,128]{3,2,1,0:T(8,128)(2,1)}), bf16[16,48,8,128]{3,2,1,0:T(8,128)(2,1)}, u32[]{:S(2)}, u32[]{:S(2)}) async-start(bf16[16,48,8,128]{3,2,1,0:T(8,128)(2,1)} %reorder.2), calls=%async_computation.1 | async-start | bytes 3145728 | tf_op jit(solution)/shard_map/all_to_all | solution.py:183
  121.2 41.1 %all-to-all-start.2 = ((bf16[16,48,8,128]{3,2,1,0:T(8,128)(2,1)}), bf16[16,48,8,128]{3,2,1,0:T(8,128)(2,1)}, u32[]{:S(2)}, u32[]{:S(2)}) async-start(bf16[16,48,8,128]{3,2,1,0:T(8,128)(2,1)} %visit.3), calls=%async_computation.2 | async-start | bytes 3145728 | tf_op jit(solution)/shard_map/all_to_all | solution.py:183

commit v2 on v1

v2 whole, which is shorter than its diff:
```python
import functools

import jax
import jax.numpy as jnp
from jax import lax
from jax.experimental import pallas as pl
from jax.experimental.pallas import tpu as pltpu
from jax.sharding import PartitionSpec as P


MOMENTUM = 0.9
LEARN_RATE = 0.1
SUB, LANE = 8, 128
F32, BF16 = jnp.float32, jnp.bfloat16
HALF_ROOT = 0.7071067811865476
PDF_SCALE = 0.3989422804014327


def tile_slots(shapes, pieces):
    slots, base = [], 0
    for rows, cols in shapes:
        tiles = [(row, col) for row in range(0, rows, SUB) for col in range(0, cols, LANE)]
        if len(tiles) % pieces:
            raise ValueError("uneven tiles")
        each = len(tiles) // pieces
        slots.append(
            [(index // each, base + index % each, *tile) for index, tile in enumerate(tiles)]
        )
        base += each
    return slots, base


def pack(refs, slots, packed_ref):
    for ref, places in zip(refs, slots):
        for piece, slot, row, col in places:
            packed_ref[piece, slot] = ref[row : row + SUB, col : col + LANE].astype(
                packed_ref.dtype
            )


def unpack(packed_ref, slots, refs):
    for ref, places in zip(refs, slots):
        for piece, slot, row, col in places:
            ref[row : row + SUB, col : col + LANE] = packed_ref[piece, slot].astype(ref.dtype)


def collect(me_ref, piece_refs, packed_ref, sems):
    chip = me_ref[0] // 2
    return [
        pltpu.make_async_copy(ref, packed_ref.at[chip ^ k], sems.at[k])
        for k, ref in enumerate(piece_refs)
    ]


def scatter(me_ref, packed_ref, piece_refs, sems):
    chip = me_ref[0] // 2
    return [
        pltpu.make_async_copy(packed_ref.at[chip ^ k], ref, sems.at[k])
        for k, ref in enumerate(piece_refs)
    ]


def train_step(x_ref, y_ref, win, wout, min_, mout, hid, dout, dpre, block):
    rows = x_ref.shape[0]
    cast_in = win[...].astype(BF16)
    cast_out = wout[...].astype(BF16)
    for start in range(0, rows, block):
        part = slice(start, start + block)
        batch_x = x_ref[part, :]
        preact = jnp.dot(batch_x, cast_in, preferred_element_type=F32)
        cdf = 0.5 * (1.0 + lax.erf(preact * HALF_ROOT))
        pdf = PDF_SCALE * jnp.exp(-0.5 * preact * preact)
        hidden = (preact * cdf).astype(BF16)
        hid[part, :] = hidden
        error = (
            batch_x.astype(F32)
            + jnp.dot(hidden, cast_out, preferred_element_type=F32)
            - y_ref[part, :].astype(F32)
        )
        d_out = (error * (1.0 / rows)).astype(BF16)
        dout[part, :] = d_out
        d_hidden = lax.dot_general(
            d_out, cast_out, (((1,), (1,)), ((), ())), preferred_element_type=F32
        )
        dpre[part, :] = (d_hidden * (cdf + preact * pdf)).astype(BF16)
    over_rows = (((0,), (0,)), ((), ()))
    grad = lax.dot_general(hid[...], dout[...], over_rows, preferred_element_type=F32)
    moment = (MOMENTUM * mout[...].astype(F32) + grad).astype(BF16)
    mout[...] = moment
    wout[...] = wout[...] - LEARN_RATE * moment.astype(F32)
    grad = lax.dot_general(x_ref[...], dpre[...], over_rows, preferred_element_type=F32)
    moment = (MOMENTUM * min_[...].astype(F32) + grad).astype(BF16)
    min_[...] = moment
    win[...] = win[...] - LEARN_RATE * moment.astype(F32)


def visit_kernel(slots, pieces, packed_input, block, *refs):
    inputs = 2 * pieces if packed_input else 4
    me_ref, x_ref, y_ref = refs[:3]
    given = refs[3 : 3 + inputs]
    sent = refs[3 + inputs : 3 + inputs + 2 * pieces]
    scratch = refs[3 + inputs + 2 * pieces :]
    state, work = scratch[:4], scratch[4:7]
    packed, sems = scratch[7:9], scratch[9]
    step = pl.program_id(0)
    halves = [(slots[:2], state[:2]), (slots[2:], state[2:])]

    @pl.when(step == 0)
    def _():
        if packed_input:
            copies = [
                collect(me_ref, given[half * pieces :][:pieces], packed[half], sems.at[half])
                for half in range(2)
            ]
            for copy in copies[0] + copies[1]:
                copy.start()
            for half, (places, held) in enumerate(halves):
                for copy in copies[half]:
                    copy.wait()
                unpack(packed[half], places, held)
        else:
            for held, ref in zip(state, given):
                held[...] = ref[...]

    train_step(x_ref, y_ref, *state, *work, block)

    @pl.when(step == pl.num_programs(0) - 1)
    def _():
        copies = []
        for half, (places, held) in enumerate(halves):
            pack(held, places, packed[half])
            own = scatter(me_ref, packed[half], sent[half * pieces :][:pieces], sems.at[half])
            for copy in own:
                copy.start()
            copies += own
        for copy in copies:
            copy.wait()


def whole(shape):
    return pl.BlockSpec(shape, lambda step: (0,) * len(shape))


SCALARS = pl.BlockSpec(memory_space=pltpu.SMEM)
ANYWHERE = pl.BlockSpec(memory_space=pl.ANY)


def visit(me, batch_x, batch_y, model, shapes, steps, slots, piece_shape, pieces):
    rows, width = batch_x.shape[0] // steps, batch_x.shape[1]
    hidden = shapes[0][1]
    packed_input = len(model) > 4
    batch_spec = pl.BlockSpec((rows, width), lambda step: (step, 0))
    model_specs = [ANYWHERE if packed_input else whole(member.shape) for member in model]
    outs = pl.pallas_call(
        functools.partial(visit_kernel, slots, pieces, packed_input, rows // 4),
        grid=(steps,),
        in_specs=[SCALARS, batch_spec, batch_spec] + model_specs,
        out_specs=[ANYWHERE] * (2 * pieces),
        out_shape=[jax.ShapeDtypeStruct(piece_shape, BF16)] * (2 * pieces),
        scratch_shapes=[
            pltpu.VMEM(shapes[0], F32),
            pltpu.VMEM(shapes[1], F32),
            pltpu.VMEM(shapes[2], BF16),
            pltpu.VMEM(shapes[3], BF16),
            pltpu.VMEM((rows, hidden), BF16),
            pltpu.VMEM((rows, width), BF16),
            pltpu.VMEM((rows, hidden), BF16),
            pltpu.VMEM((pieces, *piece_shape), BF16),
            pltpu.VMEM((pieces, *piece_shape), BF16),
            pltpu.SemaphoreType.DMA((2, pieces)),
        ],
        cost_estimate=pl.CostEstimate(
            flops=steps * 10 * rows * width * hidden,
            bytes_accessed=4 * batch_x.size + 8 * width * hidden * 4,
            transcendentals=2 * steps * rows * hidden,
        ),
        name="visit",
    )(me, batch_x, batch_y, *model)
    return outs[:pieces], outs[pieces:]


def route_kernel(pieces, me_ref, source_ref, own_ref, partner_ref, *refs):
    out_refs, sems = refs[:pieces], refs[pieces]
    chip, core = me_ref[0] // 2, me_ref[0] % 2
    for k, out_ref in enumerate(out_refs):
        source = source_ref[2 * (chip ^ k) + core]
        place = chip ^ (source // 2)

        @pl.when(source % 2 == core)
        def _():
            pltpu.make_async_copy(own_ref.at[place], out_ref, sems.at[k]).start()

        @pl.when(source % 2 != core)
        def _():
            pltpu.make_async_copy(partner_ref.at[place], out_ref, sems.at[k]).start()

    for k, out_ref in enumerate(out_refs):
        pltpu.make_async_copy(own_ref.at[0], out_ref, sems.at[k]).wait()


def route(me, source, own, partner):
    pieces = own.shape[0]
    in_vmem = pl.BlockSpec(memory_space=pltpu.VMEM)
    return pl.pallas_call(
        functools.partial(route_kernel, pieces),
        in_specs=[SCALARS, SCALARS, in_vmem, in_vmem],
        out_specs=[ANYWHERE] * pieces,
        out_shape=[jax.ShapeDtypeStruct(own.shape[1:], own.dtype)] * pieces,
        scratch_shapes=[pltpu.SemaphoreType.DMA((pieces,))],
        cost_estimate=pl.CostEstimate(
            flops=0, bytes_accessed=4 * own.size, transcendentals=0
        ),
        name="route",
    )(me, source, own, partner)


def unpack_kernel(slots, pieces, me_ref, *refs):
    given, outs, (packed, sems) = refs[:pieces], refs[pieces:-2], refs[-2:]
    copies = collect(me_ref, given, packed, sems)
    for copy in copies:
        copy.start()
    for copy in copies:
        copy.wait()
    unpack(packed, slots, outs)


def unpacked(me, given, slots, outs):
    pieces = len(given)
    return pl.pallas_call(
        functools.partial(unpack_kernel, slots, pieces),
        in_specs=[SCALARS] + [ANYWHERE] * pieces,
        out_shape=[jax.ShapeDtypeStruct(shape, dtype) for shape, dtype in outs],
        scratch_shapes=[
            pltpu.VMEM((pieces, *given[0].shape), BF16),
            pltpu.SemaphoreType.DMA((pieces,)),
        ],
        name="unpack",
    )(me, *given)


def invert(order):
    count = order.shape[0]
    places = jnp.arange(count, dtype=jnp.int32)
    matches = order[:, None] == places[None, :]
    return jnp.sum(jnp.where(matches, places[:, None], 0), axis=0).astype(jnp.int32)


def spread(parts, devices):
    moved = [None] * len(parts)
    moved[0] = parts[0]
    for k in sorted(range(1, len(parts)), reverse=True):
        moved[k] = lax.ppermute(parts[k], "hop", [(i, i ^ (2 * k)) for i in range(devices)])
    return moved


def move(parts, me, source, devices):
    own = spread(parts, devices)
    own = jnp.stack(own)
    partner = lax.ppermute(own, "hop", [(i, i ^ 1) for i in range(devices)])
    routed = route(me, source, own, partner)
    return spread(routed, devices)


def on_device(
    features, targets, row_index, hop_order, weight_in, weight_out, moment_in, moment_out
):
    devices = lax.axis_size("hop")
    me = lax.axis_index("hop").astype(jnp.int32).reshape(1)
    model = (weight_in[0], weight_out[0], moment_in[0], moment_out[0])
    shapes = [member.shape for member in model]
    pieces = devices // 2
    slots, depth = tile_slots(shapes[:2], pieces)
    piece_shape = (depth, SUB, LANE)
    _, visits, steps, _ = row_index.shape
    sources = [invert(hop_order[visit_index]) for visit_index in range(visits)]
    held = model
    for visit_index in range(visits):
        picks = row_index[0, visit_index].reshape(-1)
        batch_x = features.at[picks].get(mode="promise_in_bounds")
        batch_y = targets.at[picks].get(mode="promise_in_bounds")
        weights, moments = visit(
            me, batch_x, batch_y, held, shapes, steps, slots * 2, piece_shape, pieces
        )
        source = sources[visit_index]
        weights = move(weights, me, source, devices)
        moments = move(moments, me, source, devices)
        held = (*weights, *moments)
    outs = unpacked(me, weights, slots, [(m.shape, m.dtype) for m in model[:2]])
    outs += unpacked(me, moments, slots, [(m.shape, m.dtype) for m in model[2:]])
    return tuple(member[None] for member in outs)


def solution(mesh):
    split = P(("groups", "hop"), None, None)
    in_specs = (
        P(("groups", "hop"), None),
        P(("groups", "hop"), None),
        P(("groups", "hop"), None, None, None),
        P("groups", None),
        split,
        split,
        split,
        split,
    )
    return jax.shard_map(
        on_device, mesh=mesh, in_specs=in_specs, out_specs=(split,) * 4, check_vma=False
    )
```

time: 214 us -> 265 us (1.24); the launches traced: 214 us -> 259 us
  starting transfers between devices: 24.7 us -> 109 us
  blocking collectives: 45.1 us -> 0 us
  local copies, waits for them, and re-layouts: 27 us -> 43 us
  waiting for transfers between devices: 83.7 us -> 68.4 us
  Pallas kernels: 31.3 us -> 36.6 us
    ppermute x0 -> x60, starting transfers between devices: none -> 109 us  [the longest x56 79.1 us: spread(): lax.ppermute(parts[k], 'hop', [(i, i ^ 2 * k) for i in range(devices)])]
    all_to_all x3 -> x0, waiting for transfers between devices: 83.7 us -> none  [exchange(): lax.all_to_all(packed, 'hop', split_axis=0, concat_axis=0, tiled=True)]
    ppermute x0 -> x60, waiting for transfers between devices: none -> 68.4 us  [the longest x56 68.4 us: spread(): lax.ppermute(parts[k], 'hop', [(i, i ^ 2 * k) for i in range(devices)])]
    all_to_all x1 -> x0, blocking collectives: 45.1 us -> none  [exchange(): lax.all_to_all(packed, 'hop', split_axis=0, concat_axis=0, tiled=True)]
    all_to_all x3 -> x0, starting transfers between devices: 24.7 us -> none  [exchange(): lax.all_to_all(packed, 'hop', split_axis=0, concat_axis=0, tiled=True)]
    unnamed x4 -> x78, local copies, waits for them, and re-layouts: 0.99 us -> 15.6 us
    pallas_call x5 -> x8, Pallas kernels: 31.3 us -> 36.6 us  [the longest x2 22.6 us: visit(): pl.pallas_call(functools.partial(visit_kernel, slots, pieces, packed_inpu...]
  transfers between devices with their start and end apart: 3 -> 60, of which waited for: 3 -> 17; matrix products, arithmetic and copies ran while one was open for 6% -> 11% of each run, Pallas kernels for 0% -> 4%
where the time goes in v2:
time: 265 us; the launch traced here: 259 us
  starting transfers between devices  109 us (41%)
  waiting for transfers between devices  68.4 us (26%)
  local copies, waits for them, and re-layouts  43 us (16%)
  Pallas kernels  36.6 us (14%)
    ppermute x56, starting transfers between devices, spread(): lax.ppermute(parts[k], 'hop', [(i, i ^ 2 * k) for i in range(devices)])  79.1 us
    ppermute x56, waiting for transfers between devices, spread(): lax.ppermute(parts[k], 'hop', [(i, i ^ 2 * k) for i in range(devices)])  68.4 us
    ppermute x4, starting transfers between devices, move(): partner = lax.ppermute(own, 'hop', [(i, i ^ 1) for i in range(devices)])  29.8 us
    pallas_call x2, Pallas kernels, visit(): pl.pallas_call(functools.partial(visit_kernel, slots, pieces, packed_inpu...  22.6 us
    unnamed x78, local copies, waits for them, and re-layouts  15.6 us
    gather x2, local copies, waits for them, and re-layouts, on_device(): batch_x = features.at[picks].get(mode='promise_in_bounds')  14.6 us
    gather x2, local copies, waits for them, and re-layouts, on_device(): batch_y = targets.at[picks].get(mode='promise_in_bounds')  10.6 us
    pallas_call x4, Pallas kernels, route(): pl.pallas_call(functools.partial(route_kernel, pieces), in_specs=[SCALARS...  9.35 us
  transfers between devices with their start and end apart: 60, of which 17 were waited for; matrix products, arithmetic and copies ran while one was open for 11% of the time, Pallas kernels for 4%

profile of v2, /device:TPU:1, one launch (start us, length us, event | category | flops | bytes accessed | tf_op | source)
XLA Modules:
  0.0 259.4 jit_solution(7153622731367411442)
XLA Ops:
  2.6 5.3 %gather_fusion.3 = bf16[1536,384]{1,0:T(8,128)(2,1)} fusion(bf16[4096,384]{1,0:T(8,128)(2,1)S(1)} %copy-done, s32[2048]{0:T(1024)S(1)} %pad_clamp_fusion), kind=kCustom, calls=%fused_computation.3 | custom fusion | bytes 2365440 | tf_op jit(solution)/shard_map/gather | solution.py:280
  7.8 7.3 %gather_fusion.2 = bf16[1536,384]{1,0:T(8,128)(2,1)} fusion(bf16[4096,384]{1,0:T(8,128)(2,1)} %param.8, s32[2048]{0:T(1024)S(1)} %pad_clamp_fusion), kind=kCustom, calls=%fused_computation.2 | custom fusion | bytes 2365440 | tf_op jit(solution)/shard_map/gather | solution.py:279
  15.1 11.0 %visit.2 = (bf16[48,8,128]{2,1,0:T(8,128)(2,1)}, bf16[48,8,128]{2,1,0:T(8,128)(2,1)}, bf16[48,8,128]{2,1,0:T(8,128)(2,1)}, bf16[48,8,128]{2,1,0:T(8,128)(2,1)}, ...) custom-call(s32[1]{0:T(128)} %bitcast.refs_0_.me_ref, ...), custom_call_target="tpu_custom_call" | custom-call | flops 3019898880 | bytes 8650752 | tf_op jit(solution)/shard_map/visit/pallas_call | solution.py:154
  26.2 2.1 collective-permute-start
  29.6 2.4 collective-permute-start.3
  35.5 3.4 %collective-permute-start.5 = (bf16[48,8,128]{2,1,0:T(8,128)(2,1)}, bf16[48,8,128]{2,1,0:T(8,128)(2,1)S(1)}, u32[]{:S(2)}, u32[]{:S(2)}) collective-permute-start(bf16[48,8,128]{2,1,0:T(8,128)(2,1)} %get-tuple-element.78), channel_id=1, source_target_pairs={{0,12},{1,13},{2,14},{3,15},{4,8},{5,9},{6,10},{7,11},{8,4},{9,5},... | collective-permute-start | bytes 294920 | tf_op jit(solution)/shard_map/ppermute | solution.py:252
  40.4 3.1 %collective-permute-done.15 = bf16[48,8,128]{2,1,0:T(8,128)(2,1)S(1)} collective-permute-done((bf16[48,8,128]{2,1,0:T(8,128)(2,1)}, bf16[48,8,128]{2,1,0:T(8,128)(2,1)S(1)}, u32[]{:S(2)}, u32[]{:S(2)}) %collective-permute-start.15) | collective-permute-done | bytes 98336 | tf_op jit(solution)/shard_map/ppermute | solution.py:252
  43.5 3.7 %collective-permute-done.16 = bf16[48,8,128]{2,1,0:T(8,128)(2,1)S(1)} collective-permute-done((bf16[48,8,128]{2,1,0:T(8,128)(2,1)}, bf16[48,8,128]{2,1,0:T(8,128)(2,1)S(1)}, u32[]{:S(2)}, u32[]{:S(2)}) %collective-permute-start.16) | collective-permute-done | bytes 98336 | tf_op jit(solution)/shard_map/ppermute | solution.py:252
  47.4 5.3 %collective-permute-done.17 = bf16[48,8,128]{2,1,0:T(8,128)(2,1)S(1)} collective-permute-done((bf16[48,8,128]{2,1,0:T(8,128)(2,1)}, bf16[48,8,128]{2,1,0:T(8,128)(2,1)S(1)}, u32[]{:S(2)}, u32[]{:S(2)}) %collective-permute-start.17) | collective-permute-done | bytes 98336 | tf_op jit(solution)/shard_map/ppermute | solution.py:252
  52.7 5.2 %collective-permute-done.18 = bf16[48,8,128]{2,1,0:T(8,128)(2,1)S(1)} collective-permute-done((bf16[48,8,128]{2,1,0:T(8,128)(2,1)S(1)}, bf16[48,8,128]{2,1,0:T(8,128)(2,1)S(1)}, u32[]{:S(2)}, u32[]{:S(2)}) %collective-permute-start.18) | collective-permute-done | bytes 98336 | tf_op jit(solution)/shard_map/ppermute | solution.py:252
  57.9 6.7 %collective-permute-done.19 = bf16[48,8,128]{2,1,0:T(8,128)(2,1)S(1)} collective-permute-done((bf16[48,8,128]{2,1,0:T(8,128)(2,1)S(1)}, bf16[48,8,128]{2,1,0:T(8,128)(2,1)S(1)}, u32[]{:S(2)}, u32[]{:S(2)}) %collective-permute-start.19) | collective-permute-done | bytes 98336 | tf_op jit(solution)/shard_map/ppermute | solution.py:252
  66.3 3.8 %collective-permute-done.20 = bf16[48,8,128]{2,1,0:T(8,128)(2,1)S(1)} collective-permute-done((bf16[48,8,128]{2,1,0:T(8,128)(2,1)S(1)}, bf16[48,8,128]{2,1,0:T(8,128)(2,1)S(1)}, u32[]{:S(2)}, u32[]{:S(2)}) %collective-permute-start.20) | collective-permute-done | bytes 98336 | tf_op jit(solution)/shard_map/ppermute | solution.py:252
  70.1 2.5 collective-permute-start.21
  72.6 3.8 %collective-permute-done.21 = bf16[48,8,128]{2,1,0:T(8,128)(2,1)S(1)} collective-permute-done((bf16[48,8,128]{2,1,0:T(8,128)(2,1)S(1)}, bf16[48,8,128]{2,1,0:T(8,128)(2,1)S(1)}, u32[]{:S(2)}, u32[]{:S(2)}) %collective-permute-start.21) | collective-permute-done | bytes 98336 | tf_op jit(solution)/shard_map/ppermute | solution.py:252
  76.4 2.5 collective-permute-start.6
  79.7 9.2 %collective-permute-start.22 = (bf16[8,48,8,128]{3,2,1,0:T(8,128)(2,1)S(1)}, bf16[8,48,8,128]{3,2,1,0:T(8,128)(2,1)}, u32[]{:S(2)}, u32[]{:S(2)}) collective-permute-start(bf16[8,48,8,128]{3,2,1,0:T(8,128)(2,1)S(1)} %bitcast_dynamic-update-slice_fusion.16.own_ref), channel_id=1, source_target_pairs={{0,1},{1,0},{2,3},{3,2},{4,5},{5,4},{6,7},{7,6},{8,9},{9,8},{10,11... | collective-permute-start | bytes 2359304 | tf_op jit(solution)/shard_map/ppermute | solution.py:259
  92.2 2.9 %collective-permute-start.7 = (bf16[8,48,8,128]{3,2,1,0:T(8,128)(2,1)}, bf16[8,48,8,128]{3,2,1,0:T(8,128)(2,1)}, u32[]{:S(2)}, u32[]{:S(2)}) collective-permute-start(bf16[8,48,8,128]{3,2,1,0:T(8,128)(2,1)} %bitcast_dynamic-update-slice_fusion.24.own_ref), channel_id=1, source_target_pairs={{0,1},{1,0},{2,3},{3,2},{4,5},{5,4},{6,7},{7,6},{8,9},{9,8},{10,11... | collective-permute-start | bytes 2359304 | tf_op jit(solution)/shard_map/ppermute | solution.py:259
  95.8 2.3 route.5
  98.7 2.1 collective-permute-start.25
  103.5 2.3 route.4
  107.2 2.6 %collective-permute-start.29 = (bf16[48,8,128]{2,1,0:T(8,128)(2,1)}, bf16[48,8,128]{2,1,0:T(8,128)(2,1)S(1)}, u32[]{:S(2)}, u32[]{:S(2)}) collective-permute-start(bf16[48,8,128]{2,1,0:T(8,128)(2,1)} %get-tuple-element.103), channel_id=1, source_target_pairs={{0,14},{1,15},{2,12},{3,13},{4,10},{5,11},{6,8},{7,9},{8,6},{9,7},... | collective-permute-start | bytes 294920 | tf_op jit(solution)/shard_map/ppermute | solution.py:252
  110.4 5.5 %collective-permute-done.27.refs_16_ = bf16[48,8,128]{2,1,0:T(8,128)(2,1)} collective-permute-done((bf16[48,8,128]{2,1,0:T(8,128)(2,1)}, bf16[48,8,128]{2,1,0:T(8,128)(2,1)}, u32[]{:S(2)}, u32[]{:S(2)}) %collective-permute-start.27) | collective-permute-done | bytes 98336 | tf_op jit(solution)/shard_map/ppermute | solution.py:252
  115.9 3.7 %collective-permute-start.11 = (bf16[48,8,128]{2,1,0:T(8,128)(2,1)}, bf16[48,8,128]{2,1,0:T(8,128)(2,1)}, u32[]{:S(2)}, u32[]{:S(2)}) collective-permute-start(bf16[48,8,128]{2,1,0:T(8,128)(2,1)} %get-tuple-element.84), channel_id=1, source_target_pairs={{0,8},{1,9},{2,10},{3,11},{4,12},{5,13},{6,14},{7,15},{8,0},{9,1},... | collective-permute-start | bytes 294920 | tf_op jit(solution)/shard_map/ppermute | solution.py:252
  119.6 2.9 %collective-permute-start.12 = (bf16[48,8,128]{2,1,0:T(8,128)(2,1)}, bf16[48,8,128]{2,1,0:T(8,128)(2,1)}, u32[]{:S(2)}, u32[]{:S(2)}) collective-permute-start(bf16[48,8,128]{2,1,0:T(8,128)(2,1)} %get-tuple-element.85), channel_id=1, source_target_pairs={{0,10},{1,11},{2,8},{3,9},{4,14},{5,15},{6,12},{7,13},{8,2},{9,3},... | collective-permute-start | bytes 294920 | tf_op jit(solution)/shard_map/ppermute | solution.py:252
  125.9 5.3 %gather_fusion.1 = bf16[1536,384]{1,0:T(8,128)(2,1)} fusion(bf16[4096,384]{1,0:T(8,128)(2,1)S(1)} %copy-done, s32[2048]{0:T(1024)S(1)} %pad_clamp_fusion.1), kind=kCustom, calls=%fused_computation.1 | custom fusion | bytes 2365440 | tf_op jit(solution)/shard_map/gather | solution.py:280
  131.2 7.3 %gather_fusion = bf16[1536,384]{1,0:T(8,128)(2,1)} fusion(bf16[4096,384]{1,0:T(8,128)(2,1)} %param.8, s32[2048]{0:T(1024)S(1)} %pad_clamp_fusion.1), kind=kCustom, calls=%fused_computation | custom fusion | bytes 2365440 | tf_op jit(solution)/shard_map/gather | solution.py:279
  138.5 11.6 %visit.3 = (bf16[48,8,128]{2,1,0:T(8,128)(2,1)}, bf16[48,8,128]{2,1,0:T(8,128)(2,1)}, bf16[48,8,128]{2,1,0:T(8,128)(2,1)}, bf16[48,8,128]{2,1,0:T(8,128)(2,1)}, ...) custom-call(s32[1]{0:T(128)} %bitcast.refs_0_.me_ref, ...), custom_call_target="tpu_custom_call" | custom-call | flops 3019898880 | bytes 8650752 | tf_op jit(solution)/shard_map/visit/pallas_call | solution.py:154
  153.1 3.0 %collective-permute-start.34 = (bf16[48,8,128]{2,1,0:T(8,128)(2,1)}, bf16[48,8,128]{2,1,0:T(8,128)(2,1)S(1)}, u32[]{:S(2)}, u32[]{:S(2)}) collective-permute-start(bf16[48,8,128]{2,1,0:T(8,128)(2,1)} %get-tuple-element.109), channel_id=1, source_target_pairs={{0,10},{1,11},{2,8},{3,9},{4,14},{5,15},{6,12},{7,13},{8,2},{9,3},... | collective-permute-start | bytes 294920 | tf_op jit(solution)/shard_map/ppermute | solution.py:252
  161.7 2.7 %collective-permute-done.45 = bf16[48,8,128]{2,1,0:T(8,128)(2,1)S(1)} collective-permute-done((bf16[48,8,128]{2,1,0:T(8,128)(2,1)}, bf16[48,8,128]{2,1,0:T(8,128)(2,1)S(1)}, u32[]{:S(2)}, u32[]{:S(2)}) %collective-permute-start.45) | collective-permute-done | bytes 98336 | tf_op jit(solution)/shard_map/ppermute | solution.py:252
  164.4 4.0 %collective-permute-done.46 = bf16[48,8,128]{2,1,0:T(8,128)(2,1)S(1)} collective-permute-done((bf16[48,8,128]{2,1,0:T(8,128)(2,1)}, bf16[48,8,128]{2,1,0:T(8,128)(2,1)S(1)}, u32[]{:S(2)}, u32[]{:S(2)}) %collective-permute-start.46) | collective-permute-done | bytes 98336 | tf_op jit(solution)/shard_map/ppermute | solution.py:252
  169.6 3.3 %collective-permute-done.47 = bf16[48,8,128]{2,1,0:T(8,128)(2,1)S(1)} collective-permute-done((bf16[48,8,128]{2,1,0:T(8,128)(2,1)}, bf16[48,8,128]{2,1,0:T(8,128)(2,1)S(1)}, u32[]{:S(2)}, u32[]{:S(2)}) %collective-permute-start.47) | collective-permute-done | bytes 98336 | tf_op jit(solution)/shard_map/ppermute | solution.py:252
  174.8 2.5 collective-permute-done.48
  177.4 2.7 %collective-permute-start.49 = (bf16[48,8,128]{2,1,0:T(8,128)(2,1)S(1)}, bf16[48,8,128]{2,1,0:T(8,128)(2,1)S(1)}, u32[]{:S(2)}, u32[]{:S(2)}) collective-permute-start(bf16[48,8,128]{2,1,0:T(8,128)(2,1)S(1)} %copy-done.17), channel_id=1, source_target_pairs={{0,10},{1,11},{2,8},{3,9},{4,14},{5,15},{6,12},{7,13},{8,2},{9,3},... | collective-permute-start | bytes 294920 | tf_op jit(solution)/shard_map/ppermute | solution.py:252
  180.1 2.5 collective-permute-done.49
  182.6 4.5 %collective-permute-start.50 = (bf16[48,8,128]{2,1,0:T(8,128)(2,1)S(1)}, bf16[48,8,128]{2,1,0:T(8,128)(2,1)S(1)}, u32[]{:S(2)}, u32[]{:S(2)}) collective-permute-start(bf16[48,8,128]{2,1,0:T(8,128)(2,1)S(1)} %copy-done.14), channel_id=1, source_target_pairs={{0,12},{1,13},{2,14},{3,15},{4,8},{5,9},{6,10},{7,11},{8,4},{9,5},... | collective-permute-start | bytes 294920 | tf_op jit(solution)/shard_map/ppermute | solution.py:252
  191.0 4.4 %collective-permute-done.51 = bf16[48,8,128]{2,1,0:T(8,128)(2,1)S(1)} collective-permute-done((bf16[48,8,128]{2,1,0:T(8,128)(2,1)S(1)}, bf16[48,8,128]{2,1,0:T(8,128)(2,1)S(1)}, u32[]{:S(2)}, u32[]{:S(2)}) %collective-permute-start.51) | collective-permute-done | bytes 98336 | tf_op jit(solution)/shard_map/ppermute | solution.py:252
  198.2 16.9 %collective-permute-start.52 = (bf16[8,48,8,128]{3,2,1,0:T(8,128)(2,1)S(1)}, bf16[8,48,8,128]{3,2,1,0:T(8,128)(2,1)}, u32[]{:S(2)}, u32[]{:S(2)}) collective-permute-start(bf16[8,48,8,128]{3,2,1,0:T(8,128)(2,1)S(1)} %bitcast_dynamic-update-slice_fusion.own_ref), channel_id=1, source_target_pairs={{0,1},{1,0},{2,3},{3,2},{4,5},{5,4},{6,7},{7,6},{8,9},{9,8},{10,11... | collective-permute-start | bytes 2359304 | tf_op jit(solution)/shard_map/ppermute | solution.py:259
  219.7 2.3 route.7
  222.2 2.6 collective-permute-start.55
  227.0 2.3 route.6
  229.3 3.1 %collective-permute-start.58 = (bf16[48,8,128]{2,1,0:T(8,128)(2,1)}, bf16[48,8,128]{2,1,0:T(8,128)(2,1)}, u32[]{:S(2)}, u32[]{:S(2)}) collective-permute-start(bf16[48,8,128]{2,1,0:T(8,128)(2,1)} %get-tuple-element.136), channel_id=1, source_target_pairs={{0,12},{1,13},{2,14},{3,15},{4,8},{5,9},{6,10},{7,11},{8,4},{9,5},... | collective-permute-start | bytes 294920 | tf_op jit(solution)/shard_map/ppermute | solution.py:252
  233.9 5.9 %collective-permute-done.57.refs_5_ = bf16[48,8,128]{2,1,0:T(8,128)(2,1)} collective-permute-done((bf16[48,8,128]{2,1,0:T(8,128)(2,1)}, bf16[48,8,128]{2,1,0:T(8,128)(2,1)}, u32[]{:S(2)}, u32[]{:S(2)}) %collective-permute-start.57) | collective-permute-done | bytes 98336 | tf_op jit(solution)/shard_map/ppermute | solution.py:252
  240.4 3.2 %collective-permute-start.41 = (bf16[48,8,128]{2,1,0:T(8,128)(2,1)}, bf16[48,8,128]{2,1,0:T(8,128)(2,1)}, u32[]{:S(2)}, u32[]{:S(2)}) collective-permute-start(bf16[48,8,128]{2,1,0:T(8,128)(2,1)} %get-tuple-element.116), channel_id=1, source_target_pairs={{0,8},{1,9},{2,10},{3,11},{4,12},{5,13},{6,14},{7,15},{8,0},{9,1},... | collective-permute-start | bytes 294920 | tf_op jit(solution)/shard_map/ppermute | solution.py:252
  243.7 3.2 %collective-permute-start.42 = (bf16[48,8,128]{2,1,0:T(8,128)(2,1)}, bf16[48,8,128]{2,1,0:T(8,128)(2,1)}, u32[]{:S(2)}, u32[]{:S(2)}) collective-permute-start(bf16[48,8,128]{2,1,0:T(8,128)(2,1)} %get-tuple-element.117), channel_id=1, source_target_pairs={{0,10},{1,11},{2,8},{3,9},{4,14},{5,15},{6,12},{7,13},{8,2},{9,3},... | collective-permute-start | bytes 294920 | tf_op jit(solution)/shard_map/ppermute | solution.py:252
  248.5 2.3 collective-permute-start.44
  250.9 2.2 unpack.3
  253.1 3.7 %collective-permute-done.42.refs_5_ = bf16[48,8,128]{2,1,0:T(8,128)(2,1)} collective-permute-done((bf16[48,8,128]{2,1,0:T(8,128)(2,1)}, bf16[48,8,128]{2,1,0:T(8,128)(2,1)}, u32[]{:S(2)}, u32[]{:S(2)}) %collective-permute-start.42) | collective-permute-done | bytes 98336 | tf_op jit(solution)/shard_map/ppermute | solution.py:252
  256.8 2.5 unpack.2
  (174 shorter events, 52.3 us)
Async XLA Ops:
  26.2 9.3 %collective-permute-start = (bf16[48,8,128]{2,1,0:T(8,128)(2,1)}, bf16[48,8,128]{2,1,0:T(8,128)(2,1)S(1)}, u32[]{:S(2)}, u32[]{:S(2)}) collective-permute-start(bf16[48,8,128]{2,1,0:T(8,128)(2,1)} %get-tuple-element.73), channel_id=1, source_target_pairs={{0,2},{1,3},{2,0},{3,1},{4,6},{5,7},{6,4},{7,5},{8,10},{9,11},{10,... | collective-permute-start | bytes 294920 | tf_op jit(solution)/shard_map/ppermute | solution.py:252
  28.3 11.2 %collective-permute-start.1 = (bf16[48,8,128]{2,1,0:T(8,128)(2,1)}, bf16[48,8,128]{2,1,0:T(8,128)(2,1)S(1)}, u32[]{:S(2)}, u32[]{:S(2)}) collective-permute-start(bf16[48,8,128]{2,1,0:T(8,128)(2,1)} %get-tuple-element.74), channel_id=1, source_target_pairs={{0,4},{1,5},{2,6},{3,7},{4,0},{5,1},{6,2},{7,3},{8,12},{9,13},{10,... | collective-permute-start | bytes 294920 | tf_op jit(solution)/shard_map/ppermute | solution.py:252
  29.6 49.3 %collective-permute-start.2 = (bf16[48,8,128]{2,1,0:T(8,128)(2,1)}, bf16[48,8,128]{2,1,0:T(8,128)(2,1)S(1)}, u32[]{:S(2)}, u32[]{:S(2)}) collective-permute-start(bf16[48,8,128]{2,1,0:T(8,128)(2,1)} %get-tuple-element.75), channel_id=1, source_target_pairs={{0,6},{1,7},{2,4},{3,5},{4,2},{5,3},{6,0},{7,1},{8,14},{9,15},{10,... | collective-permute-start | bytes 294920 | tf_op jit(solution)/shard_map/ppermute | solution.py:252
  29.6 60.0 %collective-permute-start.3 = (bf16[48,8,128]{2,1,0:T(8,128)(2,1)}, bf16[48,8,128]{2,1,0:T(8,128)(2,1)S(1)}, u32[]{:S(2)}, u32[]{:S(2)}) collective-permute-start(bf16[48,8,128]{2,1,0:T(8,128)(2,1)} %get-tuple-element.76), channel_id=1, source_target_pairs={{0,8},{1,9},{2,10},{3,11},{4,12},{5,13},{6,14},{7,15},{8,0},{9,1},... | collective-permute-start | bytes 294920 | tf_op jit(solution)/shard_map/ppermute | solution.py:252
  32.0 58.3 %collective-permute-start.4 = (bf16[48,8,128]{2,1,0:T(8,128)(2,1)}, bf16[48,8,128]{2,1,0:T(8,128)(2,1)S(1)}, u32[]{:S(2)}, u32[]{:S(2)}) collective-permute-start(bf16[48,8,128]{2,1,0:T(8,128)(2,1)} %get-tuple-element.77), channel_id=1, source_target_pairs={{0,10},{1,11},{2,8},{3,9},{4,14},{5,15},{6,12},{7,13},{8,2},{9,3},... | collective-permute-start | bytes 294920 | tf_op jit(solution)/shard_map/ppermute | solution.py:252
  35.5 55.5 %collective-permute-start.5 = (bf16[48,8,128]{2,1,0:T(8,128)(2,1)}, bf16[48,8,128]{2,1,0:T(8,128)(2,1)S(1)}, u32[]{:S(2)}, u32[]{:S(2)}) collective-permute-start(bf16[48,8,128]{2,1,0:T(8,128)(2,1)} %get-tuple-element.78), channel_id=1, source_target_pairs={{0,12},{1,13},{2,14},{3,15},{4,8},{5,9},{6,10},{7,11},{8,4},{9,5},... | collective-permute-start | bytes 294920 | tf_op jit(solution)/shard_map/ppermute | solution.py:252
  57.9 6.7 %collective-permute-start.19 = (bf16[48,8,128]{2,1,0:T(8,128)(2,1)S(1)}, bf16[48,8,128]{2,1,0:T(8,128)(2,1)S(1)}, u32[]{:S(2)}, u32[]{:S(2)}) collective-permute-start(bf16[48,8,128]{2,1,0:T(8,128)(2,1)S(1)} %copy-done.22), channel_id=1, source_target_pairs={{0,10},{1,11},{2,8},{3,9},{4,14},{5,15},{6,12},{7,13},{8,2},{9,3},... | collective-permute-start | bytes 294920 | tf_op jit(solution)/shard_map/ppermute | solution.py:252
  76.4 15.2 %collective-permute-start.6 = (bf16[48,8,128]{2,1,0:T(8,128)(2,1)S(1)}, bf16[48,8,128]{2,1,0:T(8,128)(2,1)S(1)}, u32[]{:S(2)}, u32[]{:S(2)}) collective-permute-start(bf16[48,8,128]{2,1,0:T(8,128)(2,1)S(1)} %copy-done.9), channel_id=1, source_target_pairs={{0,14},{1,15},{2,12},{3,13},{4,10},{5,11},{6,8},{7,9},{8,6},{9,7},... | collective-permute-start | bytes 294920 | tf_op jit(solution)/shard_map/ppermute | solution.py:252
  79.7 16.0 %collective-permute-start.22 = (bf16[8,48,8,128]{3,2,1,0:T(8,128)(2,1)S(1)}, bf16[8,48,8,128]{3,2,1,0:T(8,128)(2,1)}, u32[]{:S(2)}, u32[]{:S(2)}) collective-permute-start(bf16[8,48,8,128]{3,2,1,0:T(8,128)(2,1)S(1)} %bitcast_dynamic-update-slice_fusion.16.own_ref), channel_id=1, source_target_pairs={{0,1},{1,0},{2,3},{3,2},{4,5},{5,4},{6,7},{7,6},{8,9},{9,8},{10,11... | collective-permute-start | bytes 2359304 | tf_op jit(solution)/shard_map/ppermute | solution.py:259
  92.2 9.2 %collective-permute-start.7 = (bf16[8,48,8,128]{3,2,1,0:T(8,128)(2,1)}, bf16[8,48,8,128]{3,2,1,0:T(8,128)(2,1)}, u32[]{:S(2)}, u32[]{:S(2)}) collective-permute-start(bf16[8,48,8,128]{3,2,1,0:T(8,128)(2,1)} %bitcast_dynamic-update-slice_fusion.24.own_ref), channel_id=1, source_target_pairs={{0,1},{1,0},{2,3},{3,2},{4,5},{5,4},{6,7},{7,6},{8,9},{9,8},{10,11... | collective-permute-start | bytes 2359304 | tf_op jit(solution)/shard_map/ppermute | solution.py:259
  98.1 7.7 %collective-permute-start.23 = (bf16[48,8,128]{2,1,0:T(8,128)(2,1)}, bf16[48,8,128]{2,1,0:T(8,128)(2,1)S(1)}, u32[]{:S(2)}, u32[]{:S(2)}) collective-permute-start(bf16[48,8,128]{2,1,0:T(8,128)(2,1)} %get-tuple-element.97), channel_id=1, source_target_pairs={{0,2},{1,3},{2,0},{3,1},{4,6},{5,7},{6,4},{7,5},{8,10},{9,11},{10,... | collective-permute-start | bytes 294920 | tf_op jit(solution)/shard_map/ppermute | solution.py:252
  98.7 8.5 %collective-permute-start.24 = (bf16[48,8,128]{2,1,0:T(8,128)(2,1)}, bf16[48,8,128]{2,1,0:T(8,128)(2,1)S(1)}, u32[]{:S(2)}, u32[]{:S(2)}) collective-permute-start(bf16[48,8,128]{2,1,0:T(8,128)(2,1)} %get-tuple-element.98), channel_id=1, source_target_pairs={{0,4},{1,5},{2,6},{3,7},{4,0},{5,1},{6,2},{7,3},{8,12},{9,13},{10,... | collective-permute-start | bytes 294920 | tf_op jit(solution)/shard_map/ppermute | solution.py:252
  98.7 11.1 %collective-permute-start.25 = (bf16[48,8,128]{2,1,0:T(8,128)(2,1)}, bf16[48,8,128]{2,1,0:T(8,128)(2,1)S(1)}, u32[]{:S(2)}, u32[]{:S(2)}) collective-permute-start(bf16[48,8,128]{2,1,0:T(8,128)(2,1)} %get-tuple-element.99), channel_id=1, source_target_pairs={{0,6},{1,7},{2,4},{3,5},{4,2},{5,3},{6,0},{7,1},{8,14},{9,15},{10,... | collective-permute-start | bytes 294920 | tf_op jit(solution)/shard_map/ppermute | solution.py:252
  100.8 9.5 %collective-permute-start.26 = (bf16[48,8,128]{2,1,0:T(8,128)(2,1)}, bf16[48,8,128]{2,1,0:T(8,128)(2,1)}, u32[]{:S(2)}, u32[]{:S(2)}) collective-permute-start(bf16[48,8,128]{2,1,0:T(8,128)(2,1)} %get-tuple-element.100), channel_id=1, source_target_pairs={{0,8},{1,9},{2,10},{3,11},{4,12},{5,13},{6,14},{7,15},{8,0},{9,1},... | collective-permute-start | bytes 294920 | tf_op jit(solution)/shard_map/ppermute | solution.py:252
  101.4 14.5 %collective-permute-start.27 = (bf16[48,8,128]{2,1,0:T(8,128)(2,1)}, bf16[48,8,128]{2,1,0:T(8,128)(2,1)}, u32[]{:S(2)}, u32[]{:S(2)}) collective-permute-start(bf16[48,8,128]{2,1,0:T(8,128)(2,1)} %get-tuple-element.101), channel_id=1, source_target_pairs={{0,10},{1,11},{2,8},{3,9},{4,14},{5,15},{6,12},{7,13},{8,2},{9,3},... | collective-permute-start | bytes 294920 | tf_op jit(solution)/shard_map/ppermute | solution.py:252
  105.8 10.1 %collective-permute-start.28 = (bf16[48,8,128]{2,1,0:T(8,128)(2,1)}, bf16[48,8,128]{2,1,0:T(8,128)(2,1)S(1)}, u32[]{:S(2)}, u32[]{:S(2)}) collective-permute-start(bf16[48,8,128]{2,1,0:T(8,128)(2,1)} %get-tuple-element.102), channel_id=1, source_target_pairs={{0,12},{1,13},{2,14},{3,15},{4,8},{5,9},{6,10},{7,11},{8,4},{9,5},... | collective-permute-start | bytes 294920 | tf_op jit(solution)/shard_map/ppermute | solution.py:252
  107.2 12.4 %collective-permute-start.29 = (bf16[48,8,128]{2,1,0:T(8,128)(2,1)}, bf16[48,8,128]{2,1,0:T(8,128)(2,1)S(1)}, u32[]{:S(2)}, u32[]{:S(2)}) collective-permute-start(bf16[48,8,128]{2,1,0:T(8,128)(2,1)} %get-tuple-element.103), channel_id=1, source_target_pairs={{0,14},{1,15},{2,12},{3,13},{4,10},{5,11},{6,8},{7,9},{8,6},{9,7},... | collective-permute-start | bytes 294920 | tf_op jit(solution)/shard_map/ppermute | solution.py:252
  109.8 12.8 %collective-permute-start.8 = (bf16[48,8,128]{2,1,0:T(8,128)(2,1)}, bf16[48,8,128]{2,1,0:T(8,128)(2,1)S(1)}, u32[]{:S(2)}, u32[]{:S(2)}) collective-permute-start(bf16[48,8,128]{2,1,0:T(8,128)(2,1)} %get-tuple-element.81), channel_id=1, source_target_pairs={{0,2},{1,3},{2,0},{3,1},{4,6},{5,7},{6,4},{7,5},{8,10},{9,11},{10,... | collective-permute-start | bytes 294920 | tf_op jit(solution)/shard_map/ppermute | solution.py:252
  110.3 13.6 %collective-permute-start.9 = (bf16[48,8,128]{2,1,0:T(8,128)(2,1)}, bf16[48,8,128]{2,1,0:T(8,128)(2,1)S(1)}, u32[]{:S(2)}, u32[]{:S(2)}) collective-permute-start(bf16[48,8,128]{2,1,0:T(8,128)(2,1)} %get-tuple-element.82), channel_id=1, source_target_pairs={{0,4},{1,5},{2,6},{3,7},{4,0},{5,1},{6,2},{7,3},{8,12},{9,13},{10,... | collective-permute-start | bytes 294920 | tf_op jit(solution)/shard_map/ppermute | solution.py:252
  115.9 22.6 %collective-permute-start.10 = (bf16[48,8,128]{2,1,0:T(8,128)(2,1)}, bf16[48,8,128]{2,1,0:T(8,128)(2,1)}, u32[]{:S(2)}, u32[]{:S(2)}) collective-permute-start(bf16[48,8,128]{2,1,0:T(8,128)(2,1)} %get-tuple-element.83), channel_id=1, source_target_pairs={{0,6},{1,7},{2,4},{3,5},{4,2},{5,3},{6,0},{7,1},{8,14},{9,15},{10,... | collective-permute-start | bytes 294920 | tf_op jit(solution)/shard_map/ppermute | solution.py:252
  115.9 22.6 %collective-permute-start.11 = (bf16[48,8,128]{2,1,0:T(8,128)(2,1)}, bf16[48,8,128]{2,1,0:T(8,128)(2,1)}, u32[]{:S(2)}, u32[]{:S(2)}) collective-permute-start(bf16[48,8,128]{2,1,0:T(8,128)(2,1)} %get-tuple-element.84), channel_id=1, source_target_pairs={{0,8},{1,9},{2,10},{3,11},{4,12},{5,13},{6,14},{7,15},{8,0},{9,1},... | collective-permute-start | bytes 294920 | tf_op jit(solution)/shard_map/ppermute | solution.py:252
  119.6 18.9 %collective-permute-start.12 = (bf16[48,8,128]{2,1,0:T(8,128)(2,1)}, bf16[48,8,128]{2,1,0:T(8,128)(2,1)}, u32[]{:S(2)}, u32[]{:S(2)}) collective-permute-start(bf16[48,8,128]{2,1,0:T(8,128)(2,1)} %get-tuple-element.85), channel_id=1, source_target_pairs={{0,10},{1,11},{2,8},{3,9},{4,14},{5,15},{6,12},{7,13},{8,2},{9,3},... | collective-permute-start | bytes 294920 | tf_op jit(solution)/shard_map/ppermute | solution.py:252
  122.5 15.9 %collective-permute-start.13 = (bf16[48,8,128]{2,1,0:T(8,128)(2,1)}, bf16[48,8,128]{2,1,0:T(8,128)(2,1)}, u32[]{:S(2)}, u32[]{:S(2)}) collective-permute-start(bf16[48,8,128]{2,1,0:T(8,128)(2,1)} %get-tuple-element.86), channel_id=1, source_target_pairs={{0,12},{1,13},{2,14},{3,15},{4,8},{5,9},{6,10},{7,11},{8,4},{9,5},... | collective-permute-start | bytes 294920 | tf_op jit(solution)/shard_map/ppermute | solution.py:252
  123.9 14.6 %collective-permute-start.14 = (bf16[48,8,128]{2,1,0:T(8,128)(2,1)}, bf16[48,8,128]{2,1,0:T(8,128)(2,1)}, u32[]{:S(2)}, u32[]{:S(2)}) collective-permute-start(bf16[48,8,128]{2,1,0:T(8,128)(2,1)} %get-tuple-element.87), channel_id=1, source_target_pairs={{0,14},{1,15},{2,12},{3,13},{4,10},{5,11},{6,8},{7,9},{8,6},{9,7},... | collective-permute-start | bytes 294920 | tf_op jit(solution)/shard_map/ppermute | solution.py:252
  150.2 8.4 %collective-permute-start.30 = (bf16[48,8,128]{2,1,0:T(8,128)(2,1)}, bf16[48,8,128]{2,1,0:T(8,128)(2,1)S(1)}, u32[]{:S(2)}, u32[]{:S(2)}) collective-permute-start(bf16[48,8,128]{2,1,0:T(8,128)(2,1)} %get-tuple-element.105), channel_id=1, source_target_pairs={{0,2},{1,3},{2,0},{3,1},{4,6},{5,7},{6,4},{7,5},{8,10},{9,11},{10,... | collective-permute-start | bytes 294920 | tf_op jit(solution)/shard_map/ppermute | solution.py:252
  151.5 9.3 %collective-permute-start.31 = (bf16[48,8,128]{2,1,0:T(8,128)(2,1)}, bf16[48,8,128]{2,1,0:T(8,128)(2,1)S(1)}, u32[]{:S(2)}, u32[]{:S(2)}) collective-permute-start(bf16[48,8,128]{2,1,0:T(8,128)(2,1)} %get-tuple-element.106), channel_id=1, source_target_pairs={{0,4},{1,5},{2,6},{3,7},{4,0},{5,1},{6,2},{7,3},{8,12},{9,13},{10,... | collective-permute-start | bytes 294920 | tf_op jit(solution)/shard_map/ppermute | solution.py:252
  151.5 45.9 %collective-permute-start.32 = (bf16[48,8,128]{2,1,0:T(8,128)(2,1)}, bf16[48,8,128]{2,1,0:T(8,128)(2,1)S(1)}, u32[]{:S(2)}, u32[]{:S(2)}) collective-permute-start(bf16[48,8,128]{2,1,0:T(8,128)(2,1)} %get-tuple-element.107), channel_id=1, source_target_pairs={{0,6},{1,7},{2,4},{3,5},{4,2},{5,3},{6,0},{7,1},{8,14},{9,15},{10,... | collective-permute-start | bytes 294920 | tf_op jit(solution)/shard_map/ppermute | solution.py:252
  152.9 62.9 %collective-permute-start.33 = (bf16[48,8,128]{2,1,0:T(8,128)(2,1)}, bf16[48,8,128]{2,1,0:T(8,128)(2,1)S(1)}, u32[]{:S(2)}, u32[]{:S(2)}) collective-permute-start(bf16[48,8,128]{2,1,0:T(8,128)(2,1)} %get-tuple-element.108), channel_id=1, source_target_pairs={{0,8},{1,9},{2,10},{3,11},{4,12},{5,13},{6,14},{7,15},{8,0},{9,1},... | collective-permute-start | bytes 294920 | tf_op jit(solution)/shard_map/ppermute | solution.py:252
  153.1 63.3 %collective-permute-start.34 = (bf16[48,8,128]{2,1,0:T(8,128)(2,1)}, bf16[48,8,128]{2,1,0:T(8,128)(2,1)S(1)}, u32[]{:S(2)}, u32[]{:S(2)}) collective-permute-start(bf16[48,8,128]{2,1,0:T(8,128)(2,1)} %get-tuple-element.109), channel_id=1, source_target_pairs={{0,10},{1,11},{2,8},{3,9},{4,14},{5,15},{6,12},{7,13},{8,2},{9,3},... | collective-permute-start | bytes 294920 | tf_op jit(solution)/shard_map/ppermute | solution.py:252
  158.6 58.4 %collective-permute-start.35 = (bf16[48,8,128]{2,1,0:T(8,128)(2,1)}, bf16[48,8,128]{2,1,0:T(8,128)(2,1)S(1)}, u32[]{:S(2)}, u32[]{:S(2)}) collective-permute-start(bf16[48,8,128]{2,1,0:T(8,128)(2,1)} %get-tuple-element.110), channel_id=1, source_target_pairs={{0,12},{1,13},{2,14},{3,15},{4,8},{5,9},{6,10},{7,11},{8,4},{9,5},... | collective-permute-start | bytes 294920 | tf_op jit(solution)/shard_map/ppermute | solution.py:252
  182.6 6.6 %collective-permute-start.50 = (bf16[48,8,128]{2,1,0:T(8,128)(2,1)S(1)}, bf16[48,8,128]{2,1,0:T(8,128)(2,1)S(1)}, u32[]{:S(2)}, u32[]{:S(2)}) collective-permute-start(bf16[48,8,128]{2,1,0:T(8,128)(2,1)S(1)} %copy-done.14), channel_id=1, source_target_pairs={{0,12},{1,13},{2,14},{3,15},{4,8},{5,9},{6,10},{7,11},{8,4},{9,5},... | collective-permute-start | bytes 294920 | tf_op jit(solution)/shard_map/ppermute | solution.py:252
  195.5 22.2 %collective-permute-start.36 = (bf16[48,8,128]{2,1,0:T(8,128)(2,1)S(1)}, bf16[48,8,128]{2,1,0:T(8,128)(2,1)S(1)}, u32[]{:S(2)}, u32[]{:S(2)}) collective-permute-start(bf16[48,8,128]{2,1,0:T(8,128)(2,1)S(1)} %copy-done.8), channel_id=1, source_target_pairs={{0,14},{1,15},{2,12},{3,13},{4,10},{5,11},{6,8},{7,9},{8,6},{9,7},... | collective-permute-start | bytes 294920 | tf_op jit(solution)/shard_map/ppermute | solution.py:252
  198.2 21.5 %collective-permute-start.52 = (bf16[8,48,8,128]{3,2,1,0:T(8,128)(2,1)S(1)}, bf16[8,48,8,128]{3,2,1,0:T(8,128)(2,1)}, u32[]{:S(2)}, u32[]{:S(2)}) collective-permute-start(bf16[8,48,8,128]{3,2,1,0:T(8,128)(2,1)S(1)} %bitcast_dynamic-update-slice_fusion.own_ref), channel_id=1, source_target_pairs={{0,1},{1,0},{2,3},{3,2},{4,5},{5,4},{6,7},{7,6},{8,9},{9,8},{10,11... | collective-permute-start | bytes 2359304 | tf_op jit(solution)/shard_map/ppermute | solution.py:259
  218.4 7.2 %collective-permute-start.37 = (bf16[8,48,8,128]{3,2,1,0:T(8,128)(2,1)}, bf16[8,48,8,128]{3,2,1,0:T(8,128)(2,1)}, u32[]{:S(2)}, u32[]{:S(2)}) collective-permute-start(bf16[8,48,8,128]{3,2,1,0:T(8,128)(2,1)} %bitcast_dynamic-update-slice_fusion.8.own_ref), channel_id=1, source_target_pairs={{0,1},{1,0},{2,3},{3,2},{4,5},{5,4},{6,7},{7,6},{8,9},{9,8},{10,11... | collective-permute-start | bytes 2359304 | tf_op jit(solution)/shard_map/ppermute | solution.py:259
  222.1 7.2 %collective-permute-start.53 = (bf16[48,8,128]{2,1,0:T(8,128)(2,1)}, bf16[48,8,128]{2,1,0:T(8,128)(2,1)S(1)}, u32[]{:S(2)}, u32[]{:S(2)}) collective-permute-start(bf16[48,8,128]{2,1,0:T(8,128)(2,1)} %get-tuple-element.131), channel_id=1, source_target_pairs={{0,2},{1,3},{2,0},{3,1},{4,6},{5,7},{6,4},{7,5},{8,10},{9,11},{10,... | collective-permute-start | bytes 294920 | tf_op jit(solution)/shard_map/ppermute | solution.py:252
  222.2 10.2 %collective-permute-start.54 = (bf16[48,8,128]{2,1,0:T(8,128)(2,1)}, bf16[48,8,128]{2,1,0:T(8,128)(2,1)S(1)}, u32[]{:S(2)}, u32[]{:S(2)}) collective-permute-start(bf16[48,8,128]{2,1,0:T(8,128)(2,1)} %get-tuple-element.132), channel_id=1, source_target_pairs={{0,4},{1,5},{2,6},{3,7},{4,0},{5,1},{6,2},{7,3},{8,12},{9,13},{10,... | collective-permute-start | bytes 294920 | tf_op jit(solution)/shard_map/ppermute | solution.py:252
  222.2 11.5 %collective-permute-start.55 = (bf16[48,8,128]{2,1,0:T(8,128)(2,1)}, bf16[48,8,128]{2,1,0:T(8,128)(2,1)S(1)}, u32[]{:S(2)}, u32[]{:S(2)}) collective-permute-start(bf16[48,8,128]{2,1,0:T(8,128)(2,1)} %get-tuple-element.133), channel_id=1, source_target_pairs={{0,6},{1,7},{2,4},{3,5},{4,2},{5,3},{6,0},{7,1},{8,14},{9,15},{10,... | collective-permute-start | bytes 294920 | tf_op jit(solution)/shard_map/ppermute | solution.py:252
  224.8 9.1 %collective-permute-start.56 = (bf16[48,8,128]{2,1,0:T(8,128)(2,1)}, bf16[48,8,128]{2,1,0:T(8,128)(2,1)S(1)}, u32[]{:S(2)}, u32[]{:S(2)}) collective-permute-start(bf16[48,8,128]{2,1,0:T(8,128)(2,1)} %get-tuple-element.134), channel_id=1, source_target_pairs={{0,8},{1,9},{2,10},{3,11},{4,12},{5,13},{6,14},{7,15},{8,0},{9,1},... | collective-permute-start | bytes 294920 | tf_op jit(solution)/shard_map/ppermute | solution.py:252
  225.5 14.3 %collective-permute-start.57 = (bf16[48,8,128]{2,1,0:T(8,128)(2,1)}, bf16[48,8,128]{2,1,0:T(8,128)(2,1)}, u32[]{:S(2)}, u32[]{:S(2)}) collective-permute-start(bf16[48,8,128]{2,1,0:T(8,128)(2,1)} %get-tuple-element.135), channel_id=1, source_target_pairs={{0,10},{1,11},{2,8},{3,9},{4,14},{5,15},{6,12},{7,13},{8,2},{9,3},... | collective-permute-start | bytes 294920 | tf_op jit(solution)/shard_map/ppermute | solution.py:252
  229.3 11.1 %collective-permute-start.58 = (bf16[48,8,128]{2,1,0:T(8,128)(2,1)}, bf16[48,8,128]{2,1,0:T(8,128)(2,1)}, u32[]{:S(2)}, u32[]{:S(2)}) collective-permute-start(bf16[48,8,128]{2,1,0:T(8,128)(2,1)} %get-tuple-element.136), channel_id=1, source_target_pairs={{0,12},{1,13},{2,14},{3,15},{4,8},{5,9},{6,10},{7,11},{8,4},{9,5},... | collective-permute-start | bytes 294920 | tf_op jit(solution)/shard_map/ppermute | solution.py:252
  232.4 11.2 %collective-permute-start.59 = (bf16[48,8,128]{2,1,0:T(8,128)(2,1)}, bf16[48,8,128]{2,1,0:T(8,128)(2,1)}, u32[]{:S(2)}, u32[]{:S(2)}) collective-permute-start(bf16[48,8,128]{2,1,0:T(8,128)(2,1)} %get-tuple-element.137), channel_id=1, source_target_pairs={{0,14},{1,15},{2,12},{3,13},{4,10},{5,11},{6,8},{7,9},{8,6},{9,7},... | collective-permute-start | bytes 294920 | tf_op jit(solution)/shard_map/ppermute | solution.py:252
  233.8 13.1 %collective-permute-start.38 = (bf16[48,8,128]{2,1,0:T(8,128)(2,1)}, bf16[48,8,128]{2,1,0:T(8,128)(2,1)}, u32[]{:S(2)}, u32[]{:S(2)}) collective-permute-start(bf16[48,8,128]{2,1,0:T(8,128)(2,1)} %get-tuple-element.113), channel_id=1, source_target_pairs={{0,2},{1,3},{2,0},{3,1},{4,6},{5,7},{6,4},{7,5},{8,10},{9,11},{10,... | collective-permute-start | bytes 294920 | tf_op jit(solution)/shard_map/ppermute | solution.py:252
  233.9 14.7 %collective-permute-start.39 = (bf16[48,8,128]{2,1,0:T(8,128)(2,1)}, bf16[48,8,128]{2,1,0:T(8,128)(2,1)}, u32[]{:S(2)}, u32[]{:S(2)}) collective-permute-start(bf16[48,8,128]{2,1,0:T(8,128)(2,1)} %get-tuple-element.114), channel_id=1, source_target_pairs={{0,4},{1,5},{2,6},{3,7},{4,0},{5,1},{6,2},{7,3},{8,12},{9,13},{10,... | collective-permute-start | bytes 294920 | tf_op jit(solution)/shard_map/ppermute | solution.py:252
  239.8 13.3 %collective-permute-start.40 = (bf16[48,8,128]{2,1,0:T(8,128)(2,1)}, bf16[48,8,128]{2,1,0:T(8,128)(2,1)}, u32[]{:S(2)}, u32[]{:S(2)}) collective-permute-start(bf16[48,8,128]{2,1,0:T(8,128)(2,1)} %get-tuple-element.115), channel_id=1, source_target_pairs={{0,6},{1,7},{2,4},{3,5},{4,2},{5,3},{6,0},{7,1},{8,14},{9,15},{10,... | collective-permute-start | bytes 294920 | tf_op jit(solution)/shard_map/ppermute | solution.py:252
  240.4 12.7 %collective-permute-start.41 = (bf16[48,8,128]{2,1,0:T(8,128)(2,1)}, bf16[48,8,128]{2,1,0:T(8,128)(2,1)}, u32[]{:S(2)}, u32[]{:S(2)}) collective-permute-start(bf16[48,8,128]{2,1,0:T(8,128)(2,1)} %get-tuple-element.116), channel_id=1, source_target_pairs={{0,8},{1,9},{2,10},{3,11},{4,12},{5,13},{6,14},{7,15},{8,0},{9,1},... | collective-permute-start | bytes 294920 | tf_op jit(solution)/shard_map/ppermute | solution.py:252
  243.7 13.1 %collective-permute-start.42 = (bf16[48,8,128]{2,1,0:T(8,128)(2,1)}, bf16[48,8,128]{2,1,0:T(8,128)(2,1)}, u32[]{:S(2)}, u32[]{:S(2)}) collective-permute-start(bf16[48,8,128]{2,1,0:T(8,128)(2,1)} %get-tuple-element.117), channel_id=1, source_target_pairs={{0,10},{1,11},{2,8},{3,9},{4,14},{5,15},{6,12},{7,13},{8,2},{9,3},... | collective-permute-start | bytes 294920 | tf_op jit(solution)/shard_map/ppermute | solution.py:252
  246.9 9.9 %collective-permute-start.43 = (bf16[48,8,128]{2,1,0:T(8,128)(2,1)}, bf16[48,8,128]{2,1,0:T(8,128)(2,1)}, u32[]{:S(2)}, u32[]{:S(2)}) collective-permute-start(bf16[48,8,128]{2,1,0:T(8,128)(2,1)} %get-tuple-element.118), channel_id=1, source_target_pairs={{0,12},{1,13},{2,14},{3,15},{4,8},{5,9},{6,10},{7,11},{8,4},{9,5},... | collective-permute-start | bytes 294920 | tf_op jit(solution)/shard_map/ppermute | solution.py:252
  248.5 8.3 %collective-permute-start.44 = (bf16[48,8,128]{2,1,0:T(8,128)(2,1)}, bf16[48,8,128]{2,1,0:T(8,128)(2,1)}, u32[]{:S(2)}, u32[]{:S(2)}) collective-permute-start(bf16[48,8,128]{2,1,0:T(8,128)(2,1)} %get-tuple-element.119), channel_id=1, source_target_pairs={{0,14},{1,15},{2,12},{3,13},{4,10},{5,11},{6,8},{7,9},{8,6},{9,7},... | collective-permute-start | bytes 294920 | tf_op jit(solution)/shard_map/ppermute | solution.py:252
  (37 other events, 641.3 us)

commit v3 on v1

--- a/solution.py
+++ b/solution.py
@@ -10,9 +10,79 @@
 MOMENTUM = 0.9
 LEARN_RATE = 0.1
 SUB, LANE = 8, 128
+MIB = 1 << 20
+FETCH_BLOCKS, UNROLL, UNPACK_BLOCKS = 4, 16, 4
 F32, BF16 = jnp.float32, jnp.bfloat16
 HALF_ROOT = 0.7071067811865476
 PDF_SCALE = 0.3989422804014327
+
+
+def fetch_kernel(visit_index, picks_ref, x_ref, y_ref, x_out, y_out, held, table, picked, sems):
+    count, width = x_ref.shape
+    block, lanes = count // FETCH_BLOCKS, width // LANE
+    copies = []
+    for part in range(FETCH_BLOCKS):
+        place = pl.ds(part * block, block)
+        for side, ref in enumerate((x_ref, y_ref)):
+            copies.append(
+                pltpu.make_async_copy(
+                    ref.at[place], held.at[side, place], sems.at[FETCH_BLOCKS * side + part]
+                )
+            )
+            copies[-1].start()
+    for part in range(FETCH_BLOCKS):
+        for side in range(2):
+            copies[2 * part + side].wait()
+            for lane in range(lanes):
+                place = pl.ds(part * block * SUB + side * lanes + lane, block, stride=SUB)
+                table[place, :] = held[
+                    side, part * block : (part + 1) * block, lane * LANE : (lane + 1) * LANE
+                ].astype(F32)
+    _, _, steps, rows = picks_ref.shape
+    for step in range(steps):
+
+        @pl.loop(0, rows // UNROLL)
+        def _(group):
+            for offset in range(UNROLL):
+                row = group * UNROLL + offset
+                pick = picks_ref[0, visit_index, step, row]
+                source = pl.multiple_of(pick * SUB, SUB)
+                target = pl.multiple_of((step * rows + row) * SUB, SUB)
+                picked[pl.ds(target, SUB), :] = table[pl.ds(source, SUB), :]
+
+    for side, ref in enumerate((x_out, y_out)):
+        for lane in range(lanes):
+            place = pl.ds(side * lanes + lane, steps * rows, stride=SUB)
+            ref[:, lane * LANE : (lane + 1) * LANE] = picked[place, :].astype(ref.dtype)
+
+
+def fetch(features, targets, row_index, visit_index):
+    count, width = features.shape
+    _, _, steps, rows = row_index.shape
+    if 2 * width > SUB * LANE or count % FETCH_BLOCKS or rows % UNROLL:
+        raise ValueError("sizes")
+    total = steps * rows
+    return pl.pallas_call(
+        functools.partial(fetch_kernel, visit_index),
+        in_specs=[
+            pl.BlockSpec(memory_space=pltpu.SMEM),
+            pl.BlockSpec(memory_space=pl.ANY),
+            pl.BlockSpec(memory_space=pl.ANY),
+        ],
+        out_specs=[pl.BlockSpec(memory_space=pltpu.VMEM)] * 2,
+        out_shape=[jax.ShapeDtypeStruct((total, width), features.dtype)] * 2,
+        scratch_shapes=[
+            pltpu.VMEM((2, count, width), features.dtype),
+            pltpu.VMEM((count * SUB, LANE), F32),
+            pltpu.VMEM((total * SUB, LANE), F32),
+            pltpu.SemaphoreType.DMA((2 * FETCH_BLOCKS,)),
+        ],
+        compiler_params=pltpu.CompilerParams(vmem_limit_bytes=57 * MIB),
+        cost_estimate=pl.CostEstimate(
+            flops=0, bytes_accessed=4 * count * width, transcendentals=0
+        ),
+        name="fetch",
+    )(row_index, features, targets)
 
 
 def tiles_of(shape):
@@ -138,15 +208,15 @@
             bytes_accessed=4 * batch_x.size + 8 * width * hidden * 4,
             transcendentals=2 * steps * rows * hidden,
         ),
+        compiler_params=pltpu.CompilerParams(vmem_limit_bytes=28 * MIB),
         name="visit",
     )(batch_x, batch_y, *model)
 
 
 def reorder_kernel(source_ref, packed_ref, out_ref, sems):
-    count = out_ref.shape[0]
     copies = [
         pltpu.make_async_copy(packed_ref.at[source_ref[slot]], out_ref.at[slot], sems.at[slot])
-        for slot in range(count)
+        for slot in range(out_ref.shape[0])
     ]
     for copy in copies:
         copy.start()
@@ -159,13 +229,31 @@
         reorder_kernel,
         in_specs=[
             pl.BlockSpec(memory_space=pltpu.SMEM),
-            pl.BlockSpec(memory_space=pl.ANY),
-        ],
-        out_specs=pl.BlockSpec(memory_space=pltpu.VMEM),
+            pl.BlockSpec(memory_space=pltpu.VMEM),
+        ],
+        out_specs=pl.BlockSpec(memory_space=pl.ANY),
         out_shape=jax.ShapeDtypeStruct(packed.shape, packed.dtype),
         scratch_shapes=[pltpu.SemaphoreType.DMA((packed.shape[0],))],
+        compiler_params=pltpu.CompilerParams(vmem_limit_bytes=8 * MIB),
         name="reorder",
     )(source, packed)
+
+
+def unpack_blocks(packed, outs, devices):
+    blocks = UNPACK_BLOCKS if devices % UNPACK_BLOCKS == 0 else 1
+    parts = [(shape[0] // blocks, shape[1]) for shape, _ in outs]
+    slots, _ = tile_slots(parts, devices // blocks)
+    return pl.pallas_call(
+        functools.partial(unpack_kernel, slots),
+        grid=(blocks,),
+        in_specs=[
+            pl.BlockSpec((devices // blocks, *packed.shape[1:]), lambda block: (block, 0, 0, 0))
+        ],
+        out_specs=[pl.BlockSpec(part, lambda block: (block, 0)) for part in parts],
+        out_shape=[jax.ShapeDtypeStruct(shape, dtype) for shape, dtype in outs],
+        compiler_params=pltpu.CompilerParams(vmem_limit_bytes=16 * MIB),
+        name="unpack",
+    )(packed)
 
 
 def unpack_kernel(slots, packed_ref, *out_refs):
@@ -199,16 +287,10 @@
     sources = [invert(hop_order[visit_index]) for visit_index in range(visits)]
     held = model
     for visit_index in range(visits):
-        picks = row_index[0, visit_index].reshape(-1)
-        batch_x = features.at[picks].get(mode="promise_in_bounds")
-        batch_y = targets.at[picks].get(mode="promise_in_bounds")
+        batch_x, batch_y = fetch(features, targets, row_index, visit_index)
         packed = visit(batch_x, batch_y, held, shapes, steps, slots, packed_shape)
         held = (move(packed, sources[visit_index]),)
-    outs = pl.pallas_call(
-        functools.partial(unpack_kernel, slots),
-        out_shape=[jax.ShapeDtypeStruct(m.shape, m.dtype) for m in model],
-        name="unpack",
-    )(held[0])
+    outs = unpack_blocks(held[0], [(m.shape, m.dtype) for m in model], devices)
     return tuple(member[None] for member in outs)
 
 

time: 214 us -> 211 us (0.986)
  local copies, waits for them, and re-layouts: 27 us -> 6.41 us
  Pallas kernels: 31.3 us -> 49.1 us
    gather x4 -> x0, local copies, waits for them, and re-layouts: 25.2 us -> none  [the longest x2 14.6 us: on_device(): batch_x = features.at[picks].get(mode='promise_in_bounds')]
    pallas_call x1 -> x3, Pallas kernels: 2.85 us -> 26.3 us  [the longest x2 24.5 us: fetch(): pl.pallas_call(functools.partial(fetch_kernel, visit_index), in_specs=[pl...]
    unnamed x4 -> x19, local copies, waits for them, and re-layouts: 0.99 us -> 6.41 us
    pallas_call x2, Pallas kernels: 21.6 us -> 18.1 us  [visit(): pl.pallas_call(functools.partial(visit_kernel, slots, packed_input, rows...]
    pallas_call x2, Pallas kernels: 6.81 us -> 4.61 us  [reorder(): pl.pallas_call(reorder_kernel, in_specs=[pl.BlockSpec(memory_space=pltpu....]
  transfers between devices with their start and end apart: 3 -> 3, of which waited for: 3 -> 3; matrix products, arithmetic and copies ran while one was open for 6% -> 0% of each run, Pallas kernels for 0% -> 6%
where the time goes in v3:
time: 211 us; the launch traced here: 210 us
  waiting for transfers between devices  84.6 us (40%)
  Pallas kernels  49.1 us (23%)
  blocking collectives  44.8 us (21%)
  starting transfers between devices  24.6 us (12%)
  local copies, waits for them, and re-layouts  6.41 us (3%)
    all_to_all x3, waiting for transfers between devices, exchange(): lax.all_to_all(packed, 'hop', split_axis=0, concat_axis=0, tiled=True)  84.6 us
    all_to_all x1, blocking collectives, exchange(): lax.all_to_all(packed, 'hop', split_axis=0, concat_axis=0, tiled=True)  44.8 us
    all_to_all x3, starting transfers between devices, exchange(): lax.all_to_all(packed, 'hop', split_axis=0, concat_axis=0, tiled=True)  24.6 us
    pallas_call x2, Pallas kernels, fetch(): pl.pallas_call(functools.partial(fetch_kernel, visit_index), in_specs=[pl...  24.5 us
    pallas_call x2, Pallas kernels, visit(): pl.pallas_call(functools.partial(visit_kernel, slots, packed_input, rows...  18.1 us
    unnamed x19, local copies, waits for them, and re-layouts  6.41 us
    pallas_call x2, Pallas kernels, reorder(): pl.pallas_call(reorder_kernel, in_specs=[pl.BlockSpec(memory_space=pltpu....  4.61 us
  transfers between devices with their start and end apart: 3, of which 3 were waited for; matrix products, arithmetic and copies ran while one was open for 0% of the time, Pallas kernels for 6%

profile of v3, /device:TPU:1, one launch (start us, length us, event | category | flops | bytes accessed | tf_op | source)
XLA Modules:
  0.0 210.5 jit_solution(13833629114976405616)
XLA Ops:
  0.6 1.3 copy.14.picks_ref
  1.9 0.0 copy-start.4
  1.9 0.0 copy-start.5
  2.0 0.0 copy-start.6
  2.0 0.0 copy-start.7
  2.0 12.1 %fetch.3 = (bf16[1536,384]{1,0:T(8,128)(2,1)}, bf16[1536,384]{1,0:T(8,128)(2,1)}) custom-call(s32[1,2,3,512]{3,2,1,0:T(4,128)} %copy.14.picks_ref, bf16[4096,384]{1,0:T(8,128)(2,1)} %x_ref.3, bf16[4096,384]{1,0:T(8,128)(2,1)} %y_ref.3), custom_call_target="tpu_custom_call" | custom-call | bytes 6291456 | tf_op jit(solution)/shard_map/fetch/pallas_call | solution.py:65
  14.0 0.0 copy-done.4
  14.1 0.0 copy-done.5
  14.1 0.0 copy-done.6
  14.1 0.0 copy-done.7
  14.1 0.0 copy-start.2
  14.1 1.3 copy-done.2
  15.4 0.0 copy-start.3
  15.4 1.3 copy-done.3
  16.6 9.1 %visit.2 = bf16[16,48,8,128]{3,2,1,0:T(8,128)(2,1)} custom-call(bf16[1536,384]{1,0:T(8,128)(2,1)S(1)} %copy-done.2, bf16[1536,384]{1,0:T(8,128)(2,1)S(1)} %copy-done.3, f32[384,512]{1,0:T(8,128)S(1)} %bitcast.12, f32[512,384]{1,0:T(8,128)S(1)} %bitcast.13, bf16[384,512]{1,0:T(8,128)(2,1)S(1)} %bitcast.14, bf16[512,384]{1,0:T(8,128)(2,1)S(1)} %bitcast.15), custom_call_target="tpu_custom_call" | custom-call | flops 3019898880 | bytes 8650752 | tf_op jit(solution)/shard_map/visit/pallas_call | solution.py:191
  25.7 0.0 copy-start.8
  25.7 7.5 %all-to-all-start = ((bf16[16,48,8,128]{3,2,1,0:T(8,128)(2,1)}), bf16[16,48,8,128]{3,2,1,0:T(8,128)(2,1)S(1)}, u32[]{:S(2)}, u32[]{:S(2)}) async-start(bf16[16,48,8,128]{3,2,1,0:T(8,128)(2,1)} %visit.2), calls=%async_computation | async-start | bytes 3145728 | tf_op jit(solution)/shard_map/all_to_all | solution.py:271
  33.2 0.0 copy-done.8
  33.2 0.1 select_reduce_fusion.source_ref
  33.3 32.3 %all-to-all-done.packed_ref = bf16[16,48,8,128]{3,2,1,0:T(8,128)(2,1)S(1)} async-done(((bf16[16,48,8,128]{3,2,1,0:T(8,128)(2,1)}), bf16[16,48,8,128]{3,2,1,0:T(8,128)(2,1)S(1)}, u32[]{:S(2)}, u32[]{:S(2)}) %all-to-all-start) | async-done | bytes 1572896 | tf_op jit(solution)/shard_map/all_to_all | solution.py:271
  65.6 1.8 reorder.2
  67.4 8.6 %all-to-all-start.1 = ((bf16[16,48,8,128]{3,2,1,0:T(8,128)(2,1)}), bf16[16,48,8,128]{3,2,1,0:T(8,128)(2,1)S(1)}, u32[]{:S(2)}, u32[]{:S(2)}) async-start(bf16[16,48,8,128]{3,2,1,0:T(8,128)(2,1)} %reorder.2), calls=%async_computation.1 | async-start | bytes 3145728 | tf_op jit(solution)/shard_map/all_to_all | solution.py:271
  76.0 12.4 %fetch.2 = (bf16[1536,384]{1,0:T(8,128)(2,1)}, bf16[1536,384]{1,0:T(8,128)(2,1)}) custom-call(s32[1,2,3,512]{3,2,1,0:T(4,128)} %copy.14.picks_ref, bf16[4096,384]{1,0:T(8,128)(2,1)} %x_ref.3, bf16[4096,384]{1,0:T(8,128)(2,1)} %y_ref.3), custom_call_target="tpu_custom_call" | custom-call | bytes 6291456 | tf_op jit(solution)/shard_map/fetch/pallas_call | solution.py:65
  88.4 20.0 %all-to-all-done.1.refs_2_ = bf16[16,48,8,128]{3,2,1,0:T(8,128)(2,1)S(1)} async-done(((bf16[16,48,8,128]{3,2,1,0:T(8,128)(2,1)}), bf16[16,48,8,128]{3,2,1,0:T(8,128)(2,1)S(1)}, u32[]{:S(2)}, u32[]{:S(2)}) %all-to-all-start.1) | async-done | bytes 1572896 | tf_op jit(solution)/shard_map/all_to_all | solution.py:271
  108.4 0.0 copy-start
  108.4 1.3 copy-done
  109.7 0.0 copy-start.1
  109.7 1.3 copy-done.1
  110.9 9.1 %visit.3 = bf16[16,48,8,128]{3,2,1,0:T(8,128)(2,1)} custom-call(bf16[1536,384]{1,0:T(8,128)(2,1)S(1)} %copy-done, bf16[1536,384]{1,0:T(8,128)(2,1)S(1)} %copy-done.1, bf16[16,48,8,128]{3,2,1,0:T(8,128)(2,1)S(1)} %all-to-all-done.1.refs_2_), custom_call_target="tpu_custom_call" | custom-call | flops 3019898880 | bytes 8650752 | tf_op jit(solution)/shard_map/visit/pallas_call | solution.py:191
  120.0 8.6 %all-to-all-start.2 = ((bf16[16,48,8,128]{3,2,1,0:T(8,128)(2,1)}), bf16[16,48,8,128]{3,2,1,0:T(8,128)(2,1)S(1)}, u32[]{:S(2)}, u32[]{:S(2)}) async-start(bf16[16,48,8,128]{3,2,1,0:T(8,128)(2,1)} %visit.3), calls=%async_computation.2 | async-start | bytes 3145728 | tf_op jit(solution)/shard_map/all_to_all | solution.py:271
  128.6 0.1 select_reduce_fusion.1.source_ref
  128.7 32.3 %all-to-all-done.2.packed_ref = bf16[16,48,8,128]{3,2,1,0:T(8,128)(2,1)S(1)} async-done(((bf16[16,48,8,128]{3,2,1,0:T(8,128)(2,1)}), bf16[16,48,8,128]{3,2,1,0:T(8,128)(2,1)S(1)}, u32[]{:S(2)}, u32[]{:S(2)}) %all-to-all-start.2) | async-done | bytes 1572896 | tf_op jit(solution)/shard_map/all_to_all | solution.py:271
  161.0 2.8 %reorder.3 = bf16[16,48,8,128]{3,2,1,0:T(8,128)(2,1)S(1)} custom-call(s32[16]{0:T(128)S(1)} %select_reduce_fusion.1.source_ref, bf16[16,48,8,128]{3,2,1,0:T(8,128)(2,1)S(1)} %all-to-all-done.2.packed_ref), custom_call_target="tpu_custom_call" | custom-call | tf_op jit(solution)/shard_map/reorder/pallas_call | solution.py:228
  163.8 44.8 %all_to_all.20.packed_ref = bf16[16,48,8,128]{3,2,1,0:T(8,128)(2,1)S(1)} all-to-all(bf16[16,48,8,128]{3,2,1,0:T(8,128)(2,1)S(1)} %reorder.3), channel_id=1, replica_groups=mesh['groups'=2,'hop'=16] {'hop'}, dimensions={0} | all-to-all | bytes 3145728 | tf_op jit(solution)/shard_map/all_to_all | solution.py:271
  208.6 1.9 unpack.1
  (1 shorter events, 0.0 us)
Async XLA Ops:
  1.9 12.1 %copy-start.4 = (f32[1,384,512]{2,1,0:T(8,128)S(1)}, f32[1,384,512]{2,1,0:T(8,128)}, u32[]{:S(2)}) copy-start(f32[1,384,512]{2,1,0:T(8,128)} %param.12) | copy-start | bytes 2359300
  1.9 12.1 %copy-start.5 = (f32[1,512,384]{2,1,0:T(8,128)S(1)}, f32[1,512,384]{2,1,0:T(8,128)}, u32[]{:S(2)}) copy-start(f32[1,512,384]{2,1,0:T(8,128)} %param.13) | copy-start | bytes 2359300
  2.0 12.1 %copy-start.6 = (bf16[1,384,512]{2,1,0:T(8,128)(2,1)S(1)}, bf16[1,384,512]{2,1,0:T(8,128)(2,1)}, u32[]{:S(2)}) copy-start(bf16[1,384,512]{2,1,0:T(8,128)(2,1)} %param.14) | copy-start | bytes 1179652
  2.0 12.1 %copy-start.7 = (bf16[1,512,384]{2,1,0:T(8,128)(2,1)S(1)}, bf16[1,512,384]{2,1,0:T(8,128)(2,1)}, u32[]{:S(2)}) copy-start(bf16[1,512,384]{2,1,0:T(8,128)(2,1)} %param.15) | copy-start | bytes 1179652
  14.1 1.3 copy-start.2
  15.4 1.3 copy-start.3
  25.7 7.5 %copy-start.8 = (s32[2,16]{1,0:T(2,128)S(1)}, s32[2,16]{1,0:T(2,128)}, u32[]{:S(2)}) copy-start(s32[2,16]{1,0:T(2,128)} %param.11) | copy-start | bytes 388
  25.7 39.9 %all-to-all-start = ((bf16[16,48,8,128]{3,2,1,0:T(8,128)(2,1)}), bf16[16,48,8,128]{3,2,1,0:T(8,128)(2,1)S(1)}, u32[]{:S(2)}, u32[]{:S(2)}) async-start(bf16[16,48,8,128]{3,2,1,0:T(8,128)(2,1)} %visit.2), calls=%async_computation | async-start | bytes 3145728 | tf_op jit(solution)/shard_map/all_to_all | solution.py:271
  67.4 41.0 %all-to-all-start.1 = ((bf16[16,48,8,128]{3,2,1,0:T(8,128)(2,1)}), bf16[16,48,8,128]{3,2,1,0:T(8,128)(2,1)S(1)}, u32[]{:S(2)}, u32[]{:S(2)}) async-start(bf16[16,48,8,128]{3,2,1,0:T(8,128)(2,1)} %reorder.2), calls=%async_computation.1 | async-start | bytes 3145728 | tf_op jit(solution)/shard_map/all_to_all | solution.py:271
  108.4 1.3 copy-start
  109.7 1.3 copy-start.1
  120.0 41.0 %all-to-all-start.2 = ((bf16[16,48,8,128]{3,2,1,0:T(8,128)(2,1)}), bf16[16,48,8,128]{3,2,1,0:T(8,128)(2,1)S(1)}, u32[]{:S(2)}, u32[]{:S(2)}) async-start(bf16[16,48,8,128]{3,2,1,0:T(8,128)(2,1)} %visit.3), calls=%async_computation.2 | async-start | bytes 3145728 | tf_op jit(solution)/shard_map/all_to_all | solution.py:271

commit v4 on v3

--- a/solution.py
+++ b/solution.py
@@ -11,78 +11,96 @@
 LEARN_RATE = 0.1
 SUB, LANE = 8, 128
 MIB = 1 << 20
+STRIDE = SUB + 1
 FETCH_BLOCKS, UNROLL, UNPACK_BLOCKS = 4, 16, 4
+FIRST_MIB, FETCH_MIB, LATER_MIB = 58, 58, 28
 F32, BF16 = jnp.float32, jnp.bfloat16
 HALF_ROOT = 0.7071067811865476
 PDF_SCALE = 0.3989422804014327
 
 
-def fetch_kernel(visit_index, picks_ref, x_ref, y_ref, x_out, y_out, held, table, picked, sems):
-    count, width = x_ref.shape
-    block, lanes = count // FETCH_BLOCKS, width // LANE
+def table_copies(x_ref, y_ref, held, sems):
+    count = x_ref.shape[0]
+    block = count // FETCH_BLOCKS
     copies = []
     for part in range(FETCH_BLOCKS):
         place = pl.ds(part * block, block)
         for side, ref in enumerate((x_ref, y_ref)):
             copies.append(
-                pltpu.make_async_copy(
-                    ref.at[place], held.at[side, place], sems.at[FETCH_BLOCKS * side + part]
-                )
+                pltpu.make_async_copy(ref.at[place], held.at[side, place], sems.at[2 * part + side])
             )
-            copies[-1].start()
+    return copies
+
+
+def build_table(copies, held, table):
+    _, count, width = held.shape
+    block, lanes = count // FETCH_BLOCKS, width // LANE
     for part in range(FETCH_BLOCKS):
         for side in range(2):
             copies[2 * part + side].wait()
             for lane in range(lanes):
-                place = pl.ds(part * block * SUB + side * lanes + lane, block, stride=SUB)
+                place = pl.ds(part * block * STRIDE + side * lanes + lane, block, stride=STRIDE)
                 table[place, :] = held[
                     side, part * block : (part + 1) * block, lane * LANE : (lane + 1) * LANE
                 ].astype(F32)
-    _, _, steps, rows = picks_ref.shape
-    for step in range(steps):
-
-        @pl.loop(0, rows // UNROLL)
-        def _(group):
-            for offset in range(UNROLL):
-                row = group * UNROLL + offset
-                pick = picks_ref[0, visit_index, step, row]
-                source = pl.multiple_of(pick * SUB, SUB)
-                target = pl.multiple_of((step * rows + row) * SUB, SUB)
-                picked[pl.ds(target, SUB), :] = table[pl.ds(source, SUB), :]
-
-    for side, ref in enumerate((x_out, y_out)):
+
+
+def pick_rows(picks_ref, step, visit_index, table, picked, outs, first):
+    rows = picks_ref.shape[3]
+
+    @pl.loop(0, rows // UNROLL)
+    def _(group):
+        for offset in range(UNROLL):
+            row = group * UNROLL + offset
+            pick = picks_ref[0, step, visit_index, row]
+            picked[pl.ds(row * STRIDE, SUB), :] = table[pl.ds(pick * STRIDE, SUB), :]
+
+    lanes = outs[0].shape[1] // LANE
+    for side, ref in enumerate(outs):
         for lane in range(lanes):
-            place = pl.ds(side * lanes + lane, steps * rows, stride=SUB)
-            ref[:, lane * LANE : (lane + 1) * LANE] = picked[place, :].astype(ref.dtype)
-
-
-def fetch(features, targets, row_index, visit_index):
+            place = pl.ds(side * lanes + lane, rows, stride=STRIDE)
+            ref[first : first + rows, lane * LANE : (lane + 1) * LANE] = picked[place, :].astype(
+                ref.dtype
+            )
+
+
+def table_scratch(features, rows):
     count, width = features.shape
-    _, _, steps, rows = row_index.shape
     if 2 * width > SUB * LANE or count % FETCH_BLOCKS or rows % UNROLL:
         raise ValueError("sizes")
-    total = steps * rows
+    return [
+        pltpu.VMEM((2, count, width), features.dtype),
+        pltpu.VMEM((count * STRIDE, LANE), F32),
+        pltpu.VMEM((rows * STRIDE, LANE), F32),
+        pltpu.SemaphoreType.DMA((2 * FETCH_BLOCKS,)),
+    ]
+
+
+def fetch_kernel(visit_index, picks_ref, x_ref, y_ref, x_out, y_out, held, table, picked, sems):
+    _, steps, _, rows = picks_ref.shape
+    copies = table_copies(x_ref, y_ref, held, sems)
+    for copy in copies:
+        copy.start()
+    build_table(copies, held, table)
+    for step in range(steps):
+        pick_rows(picks_ref, step, visit_index, table, picked, (x_out, y_out), step * rows)
+
+
+def fetch(features, targets, picks, visit_index):
+    count, width = features.shape
+    _, steps, _, rows = picks.shape
     return pl.pallas_call(
         functools.partial(fetch_kernel, visit_index),
-        in_specs=[
-            pl.BlockSpec(memory_space=pltpu.SMEM),
-            pl.BlockSpec(memory_space=pl.ANY),
-            pl.BlockSpec(memory_space=pl.ANY),
-        ],
+        in_specs=[SCALARS, ANYWHERE, ANYWHERE],
         out_specs=[pl.BlockSpec(memory_space=pltpu.VMEM)] * 2,
-        out_shape=[jax.ShapeDtypeStruct((total, width), features.dtype)] * 2,
-        scratch_shapes=[
-            pltpu.VMEM((2, count, width), features.dtype),
-            pltpu.VMEM((count * SUB, LANE), F32),
-            pltpu.VMEM((total * SUB, LANE), F32),
-            pltpu.SemaphoreType.DMA((2 * FETCH_BLOCKS,)),
-        ],
-        compiler_params=pltpu.CompilerParams(vmem_limit_bytes=57 * MIB),
+        out_shape=[jax.ShapeDtypeStruct((steps * rows, width), features.dtype)] * 2,
+        scratch_shapes=table_scratch(features, rows),
+        compiler_params=pltpu.CompilerParams(vmem_limit_bytes=FETCH_MIB * MIB),
         cost_estimate=pl.CostEstimate(
             flops=0, bytes_accessed=4 * count * width, transcendentals=0
         ),
         name="fetch",
-    )(row_index, features, targets)
+    )(picks, features, targets)
 
 
 def tiles_of(shape):
@@ -154,22 +172,13 @@
     win[...] = win[...] - LEARN_RATE * moment.astype(F32)
 
 
-def visit_kernel(slots, packed_input, block, *refs):
-    if packed_input:
-        x_ref, y_ref, arrived, sent, *scratch = refs
-    else:
-        x_ref, y_ref, *model, sent = refs[:7]
-        scratch = refs[7:]
+def later_visit_kernel(slots, block, x_ref, y_ref, arrived, sent, *scratch):
     state, work = scratch[:4], scratch[4:]
     step = pl.program_id(0)
 
     @pl.when(step == 0)
     def _():
-        if packed_input:
-            unpack(arrived, slots, state)
-        else:
-            for held, given in zip(state, model):
-                held[...] = given[...]
+        unpack(arrived, slots, state)
 
     train_step(x_ref, y_ref, *state, *work, block)
 
@@ -178,39 +187,97 @@
         pack(state, slots, sent)
 
 
+def first_visit_kernel(slots, block, picks_ref, x_ref, y_ref, *refs):
+    model, sent, scratch = refs[:4], refs[4], refs[5:]
+    state, work, batch = scratch[:4], scratch[4:7], scratch[7:9]
+    held, table, picked, sems, model_sems = scratch[9:]
+    step = pl.program_id(0)
+
+    @pl.when(step == 0)
+    def _():
+        copies = table_copies(x_ref, y_ref, held, sems)
+        loads = [
+            pltpu.make_async_copy(ref, kept, model_sems.at[index])
+            for index, (ref, kept) in enumerate(zip(model, state))
+        ]
+        for copy in copies + loads:
+            copy.start()
+        build_table(copies, held, table)
+        for copy in loads:
+            copy.wait()
+
+    pick_rows(picks_ref, step, 0, table, picked, batch, 0)
+    train_step(*batch, *state, *work, block)
+
+    @pl.when(step == pl.num_programs(0) - 1)
+    def _():
+        pack(state, slots, sent)
+
+
 def whole(shape):
     return pl.BlockSpec(shape, lambda step: (0,) * len(shape))
 
 
-def visit(batch_x, batch_y, model, shapes, steps, slots, packed_shape):
-    rows, width = batch_x.shape[0] // steps, batch_x.shape[1]
-    hidden = shapes[0][1]
-    packed_input = len(model) == 1
-    batch_spec = pl.BlockSpec((rows, width), lambda step: (step, 0))
-    flops = steps * 10 * rows * width * hidden
+SCALARS = pl.BlockSpec(memory_space=pltpu.SMEM)
+ANYWHERE = pl.BlockSpec(memory_space=pl.ANY)
+
+
+def visit(kernel, args, in_specs, more_scratch, limit, sizes, slots, packed_shape):
+    steps, rows, width, hidden = sizes
     return pl.pallas_call(
-        functools.partial(visit_kernel, slots, packed_input, rows // 4),
+        functools.partial(kernel, slots, rows // 4),
         grid=(steps,),
-        in_specs=[batch_spec, batch_spec] + [whole(member.shape) for member in model],
+        in_specs=in_specs,
         out_specs=whole(packed_shape),
         out_shape=jax.ShapeDtypeStruct(packed_shape, BF16),
         scratch_shapes=[
-            pltpu.VMEM(shapes[0], F32),
-            pltpu.VMEM(shapes[1], F32),
-            pltpu.VMEM(shapes[2], BF16),
-            pltpu.VMEM(shapes[3], BF16),
+            pltpu.VMEM((width, hidden), F32),
+            pltpu.VMEM((hidden, width), F32),
+            pltpu.VMEM((width, hidden), BF16),
+            pltpu.VMEM((hidden, width), BF16),
             pltpu.VMEM((rows, hidden), BF16),
             pltpu.VMEM((rows, width), BF16),
             pltpu.VMEM((rows, hidden), BF16),
+            *more_scratch,
         ],
         cost_estimate=pl.CostEstimate(
-            flops=flops,
-            bytes_accessed=4 * batch_x.size + 8 * width * hidden * 4,
+            flops=steps * 10 * rows * width * hidden,
+            bytes_accessed=4 * steps * rows * width + 32 * width * hidden,
             transcendentals=2 * steps * rows * hidden,
         ),
-        compiler_params=pltpu.CompilerParams(vmem_limit_bytes=28 * MIB),
+        compiler_params=pltpu.CompilerParams(vmem_limit_bytes=limit * MIB),
         name="visit",
-    )(batch_x, batch_y, *model)
+    )(*args)
+
+
+def first_visit(features, targets, picks, model, sizes, slots, packed_shape):
+    _, rows, width, _ = sizes
+    scratch = [pltpu.VMEM((rows, width), BF16)] * 2 + table_scratch(features, rows)
+    return visit(
+        first_visit_kernel,
+        (picks, features, targets, *model),
+        [SCALARS] + [ANYWHERE] * 6,
+        scratch + [pltpu.SemaphoreType.DMA((4,))],
+        FIRST_MIB,
+        sizes,
+        slots,
+        packed_shape,
+    )
+
+
+def later_visit(batch, packed, sizes, slots):
+    _, rows, width, _ = sizes
+    batch_spec = pl.BlockSpec((rows, width), lambda step: (step, 0))
+    return visit(
+        later_visit_kernel,
+        (*batch, packed),
+        [batch_spec, batch_spec, whole(packed.shape)],
+        [],
+        LATER_MIB,
+        sizes,
+        slots,
+        packed.shape,
+    )
 
 
 def reorder_kernel(source_ref, packed_ref, out_ref, sems):
@@ -271,8 +338,11 @@
     return lax.all_to_all(packed, "hop", split_axis=0, concat_axis=0, tiled=True)
 
 
-def move(packed, source):
-    return exchange(reorder(exchange(packed), source))
+def move(packed, source, beside=()):
+    spread = exchange(packed)
+    if beside:
+        spread, *beside = lax.optimization_barrier((spread, *beside))
+    return exchange(reorder(spread, source)), beside
 
 
 def on_device(
@@ -283,14 +353,17 @@
     shapes = [member.shape for member in model]
     slots, depth = tile_slots(shapes, devices)
     packed_shape = (devices, depth, SUB, LANE)
-    _, visits, steps, _ = row_index.shape
+    _, visits, steps, rows = row_index.shape
+    sizes = (steps, rows, *shapes[0])
+    picks = jnp.transpose(row_index, (0, 2, 1, 3))
     sources = [invert(hop_order[visit_index]) for visit_index in range(visits)]
-    held = model
-    for visit_index in range(visits):
-        batch_x, batch_y = fetch(features, targets, row_index, visit_index)
-        packed = visit(batch_x, batch_y, held, shapes, steps, slots, packed_shape)
-        held = (move(packed, sources[visit_index]),)
-    outs = unpack_blocks(held[0], [(m.shape, m.dtype) for m in model], devices)
+    packed = first_visit(features, targets, picks, model, sizes, slots, packed_shape)
+    for visit_index in range(1, visits):
+        batch = fetch(features, targets, picks, visit_index)
+        packed, batch = move(packed, sources[visit_index - 1], batch)
+        packed = later_visit(batch, packed, sizes, slots)
+    packed, _ = move(packed, sources[-1])
+    outs = unpack_blocks(packed, [(m.shape, m.dtype) for m in model], devices)
     return tuple(member[None] for member in outs)
 
 

time: 211 us -> 202 us (0.957)
  blocking collectives: 44.8 us -> 89.8 us
  waiting for transfers between devices: 84.6 us -> 54.4 us
  starting transfers between devices: 24.6 us -> 11.9 us
  local copies, waits for them, and re-layouts: 6.41 us -> 0.02 us
  Pallas kernels: 49.1 us -> 44.3 us
    all_to_all x1 -> x2, blocking collectives: 44.8 us -> 89.8 us  [exchange(): lax.all_to_all(packed, 'hop', split_axis=0, concat_axis=0, tiled=True)]
    all_to_all x3 -> x2, waiting for transfers between devices: 84.6 us -> 54.4 us  [exchange(): lax.all_to_all(packed, 'hop', split_axis=0, concat_axis=0, tiled=True)]
    all_to_all x3 -> x2, starting transfers between devices: 24.6 us -> 11.9 us  [exchange(): lax.all_to_all(packed, 'hop', split_axis=0, concat_axis=0, tiled=True)]
    unnamed x19 -> x6, local copies, waits for them, and re-layouts: 6.41 us -> 0.01 us
    pallas_call x4 -> x3, Pallas kernels: 42.6 us -> 36.9 us  [the longest x2 26.8 us: visit(): pl.pallas_call(functools.partial(kernel, slots, rows // 4), grid=(steps,)...]
  transfers between devices with their start and end apart: 3 -> 2, of which waited for: 3 -> 2; matrix products, arithmetic and copies ran while one was open for 0% -> 0% of each run, Pallas kernels for 6% -> 5%
where the time goes in v4:
time: 202 us; the launch traced here: 201 us
  blocking collectives  89.8 us (44%)
  waiting for transfers between devices  54.4 us (27%)
  Pallas kernels  44.3 us (22%)
  starting transfers between devices  11.9 us (6%)
    all_to_all x2, blocking collectives, exchange(): lax.all_to_all(packed, 'hop', split_axis=0, concat_axis=0, tiled=True)  89.8 us
    all_to_all x2, waiting for transfers between devices, exchange(): lax.all_to_all(packed, 'hop', split_axis=0, concat_axis=0, tiled=True)  54.4 us
    pallas_call x2, Pallas kernels, visit(): pl.pallas_call(functools.partial(kernel, slots, rows // 4), grid=(steps,)...  26.8 us
    all_to_all x2, starting transfers between devices, exchange(): lax.all_to_all(packed, 'hop', split_axis=0, concat_axis=0, tiled=True)  11.9 us
    pallas_call x1, Pallas kernels, fetch(): pl.pallas_call(functools.partial(fetch_kernel, visit_index), in_specs=[SC...  10.2 us
    pallas_call x2, Pallas kernels, reorder(): pl.pallas_call(reorder_kernel, in_specs=[pl.BlockSpec(memory_space=pltpu....  5.52 us
  transfers between devices with their start and end apart: 2, of which 2 were waited for; matrix products, arithmetic and copies ran while one was open for 0% of the time, Pallas kernels for 5%

profile of v4, /device:TPU:1, one launch (start us, length us, event | category | flops | bytes accessed | tf_op | source)
XLA Modules:
  0.0 201.3 jit_solution(13259354992170576975)
XLA Ops:
  0.6 17.6 %visit.2 = bf16[16,48,8,128]{3,2,1,0:T(8,128)(2,1)} custom-call(s32[1,3,2,512]{3,2,1,0:T(2,128)} %bitcast.13, bf16[4096,384]{1,0:T(8,128)(2,1)} %x_ref.3, bf16[4096,384]{1,0:T(8,128)(2,1)} %y_ref.3, f32[384,512]{1,0:T(8,128)} %bitcast.15, f32[512,384]{1,0:T(8,128)} %bitcast.16, bf16[384,512]{1,0:T(8,128)(2,1)} %bitcast.19, bf16[512,384]{1,0:T(8,128)(2,1)} %bitcast.20), custom_call_target="tpu_custom_call" | custom-call | flops 3019898880 | bytes 8650752 | tf_op jit(solution)/shard_map/visit/pallas_call | solution.py:227
  18.2 7.3 %all-to-all-start = ((bf16[16,48,8,128]{3,2,1,0:T(8,128)(2,1)}), bf16[16,48,8,128]{3,2,1,0:T(8,128)(2,1)S(1)}, u32[]{:S(2)}, u32[]{:S(2)}) async-start(bf16[16,48,8,128]{3,2,1,0:T(8,128)(2,1)} %visit.2), calls=%async_computation | async-start | bytes 3145728 | tf_op jit(solution)/shard_map/all_to_all | solution.py:338
  25.6 0.0 copy-start.2
  25.6 10.2 %fetch.1 = (bf16[1536,384]{1,0:T(8,128)(2,1)}, bf16[1536,384]{1,0:T(8,128)(2,1)}) custom-call(s32[1,3,2,512]{3,2,1,0:T(2,128)} %bitcast.14, bf16[4096,384]{1,0:T(8,128)(2,1)} %x_ref.3, bf16[4096,384]{1,0:T(8,128)(2,1)} %y_ref.3), custom_call_target="tpu_custom_call" | custom-call | bytes 6291456 | tf_op jit(solution)/shard_map/fetch/pallas_call | solution.py:92
  35.8 0.0 copy-done.2
  35.8 0.1 select_reduce_fusion.source_ref
  35.9 22.1 %all-to-all-done.packed_ref = bf16[16,48,8,128]{3,2,1,0:T(8,128)(2,1)S(1)} async-done(((bf16[16,48,8,128]{3,2,1,0:T(8,128)(2,1)}), bf16[16,48,8,128]{3,2,1,0:T(8,128)(2,1)S(1)}, u32[]{:S(2)}, u32[]{:S(2)}) %all-to-all-start) | async-done | bytes 1572896 | tf_op jit(solution)/shard_map/all_to_all | solution.py:338
  58.0 2.8 %reorder.2 = bf16[16,48,8,128]{3,2,1,0:T(8,128)(2,1)S(1)} custom-call(s32[16]{0:T(128)S(1)} %select_reduce_fusion.source_ref, bf16[16,48,8,128]{3,2,1,0:T(8,128)(2,1)S(1)} %all-to-all-done.packed_ref), custom_call_target="tpu_custom_call" | custom-call | tf_op jit(solution)/shard_map/reorder/pallas_call | solution.py:295
  60.8 0.0 copy-start
  60.8 0.0 copy-start.1
  60.8 45.0 %all_to_all.20.arrived = bf16[16,48,8,128]{3,2,1,0:T(8,128)(2,1)S(1)} all-to-all(bf16[16,48,8,128]{3,2,1,0:T(8,128)(2,1)S(1)} %reorder.2), channel_id=1, replica_groups=mesh['groups'=2,'hop'=16] {'hop'}, dimensions={0} | all-to-all | bytes 3145728 | tf_op jit(solution)/shard_map/all_to_all | solution.py:338
  105.7 0.0 copy-done
  105.7 0.0 copy-done.1
  105.7 9.2 %visit.3 = bf16[16,48,8,128]{3,2,1,0:T(8,128)(2,1)} custom-call(bf16[1536,384]{1,0:T(8,128)(2,1)S(1)} %copy-done, bf16[1536,384]{1,0:T(8,128)(2,1)S(1)} %copy-done.1, bf16[16,48,8,128]{3,2,1,0:T(8,128)(2,1)S(1)} %all_to_all.20.arrived), custom_call_target="tpu_custom_call" | custom-call | flops 3019898880 | bytes 8650752 | tf_op jit(solution)/shard_map/visit/pallas_call | solution.py:227
  114.9 4.5 %all-to-all-start.2 = ((bf16[16,48,8,128]{3,2,1,0:T(8,128)(2,1)}), bf16[16,48,8,128]{3,2,1,0:T(8,128)(2,1)S(1)}, u32[]{:S(2)}, u32[]{:S(2)}) async-start(bf16[16,48,8,128]{3,2,1,0:T(8,128)(2,1)} %visit.3), calls=%async_computation.2 | async-start | bytes 3145728 | tf_op jit(solution)/shard_map/all_to_all | solution.py:338
  119.4 0.1 select_reduce_fusion.1.source_ref
  119.5 32.3 %all-to-all-done.2.packed_ref = bf16[16,48,8,128]{3,2,1,0:T(8,128)(2,1)S(1)} async-done(((bf16[16,48,8,128]{3,2,1,0:T(8,128)(2,1)}), bf16[16,48,8,128]{3,2,1,0:T(8,128)(2,1)S(1)}, u32[]{:S(2)}, u32[]{:S(2)}) %all-to-all-start.2) | async-done | bytes 1572896 | tf_op jit(solution)/shard_map/all_to_all | solution.py:338
  151.8 2.8 %reorder.3 = bf16[16,48,8,128]{3,2,1,0:T(8,128)(2,1)S(1)} custom-call(s32[16]{0:T(128)S(1)} %select_reduce_fusion.1.source_ref, bf16[16,48,8,128]{3,2,1,0:T(8,128)(2,1)S(1)} %all-to-all-done.2.packed_ref), custom_call_target="tpu_custom_call" | custom-call | tf_op jit(solution)/shard_map/reorder/pallas_call | solution.py:295
  154.6 44.8 %all_to_all.21.packed_ref = bf16[16,48,8,128]{3,2,1,0:T(8,128)(2,1)S(1)} all-to-all(bf16[16,48,8,128]{3,2,1,0:T(8,128)(2,1)S(1)} %reorder.3), channel_id=1, replica_groups=mesh['groups'=2,'hop'=16] {'hop'}, dimensions={0} | all-to-all | bytes 3145728 | tf_op jit(solution)/shard_map/all_to_all | solution.py:338
  199.4 1.9 unpack.1
  (1 shorter events, 0.0 us)
Async XLA Ops:
  18.2 39.7 %all-to-all-start = ((bf16[16,48,8,128]{3,2,1,0:T(8,128)(2,1)}), bf16[16,48,8,128]{3,2,1,0:T(8,128)(2,1)S(1)}, u32[]{:S(2)}, u32[]{:S(2)}) async-start(bf16[16,48,8,128]{3,2,1,0:T(8,128)(2,1)} %visit.2), calls=%async_computation | async-start | bytes 3145728 | tf_op jit(solution)/shard_map/all_to_all | solution.py:338
  25.6 10.2 %copy-start.2 = (s32[2,16]{1,0:T(2,128)S(1)}, s32[2,16]{1,0:T(2,128)}, u32[]{:S(2)}) copy-start(s32[2,16]{1,0:T(2,128)} %param.11) | copy-start | bytes 388
  60.8 45.0 %copy-start = (bf16[1536,384]{1,0:T(8,128)(2,1)S(1)}, bf16[1536,384]{1,0:T(8,128)(2,1)}, u32[]{:S(2)}) copy-start(bf16[1536,384]{1,0:T(8,128)(2,1)} %get-tuple-element.15.x_ref) | copy-start | bytes 3538948
  60.8 45.0 %copy-start.1 = (bf16[1536,384]{1,0:T(8,128)(2,1)S(1)}, bf16[1536,384]{1,0:T(8,128)(2,1)}, u32[]{:S(2)}) copy-start(bf16[1536,384]{1,0:T(8,128)(2,1)} %get-tuple-element.16.y_ref) | copy-start | bytes 3538948
  114.9 36.9 %all-to-all-start.2 = ((bf16[16,48,8,128]{3,2,1,0:T(8,128)(2,1)}), bf16[16,48,8,128]{3,2,1,0:T(8,128)(2,1)S(1)}, u32[]{:S(2)}, u32[]{:S(2)}) async-start(bf16[16,48,8,128]{3,2,1,0:T(8,128)(2,1)} %visit.3), calls=%async_computation.2 | async-start | bytes 3145728 | tf_op jit(solution)/shard_map/all_to_all | solution.py:338

commit v5 on v4

--- a/solution.py
+++ b/solution.py
@@ -6,6 +6,7 @@
 from jax.experimental import pallas as pl
 from jax.experimental.pallas import tpu as pltpu
 from jax.sharding import PartitionSpec as P
+
 
 MOMENTUM = 0.9
 LEARN_RATE = 0.1
@@ -136,6 +137,22 @@
     for ref, places in zip(refs, slots):
         for chunk, slot, row, col in places:
             ref[row : row + SUB, col : col + LANE] = packed_ref[chunk, slot].astype(ref.dtype)
+
+
+def collect(me_ref, piece_refs, packed_ref, sems):
+    chip = me_ref[0] // 2
+    return [
+        pltpu.make_async_copy(ref, packed_ref.at[chip ^ k], sems.at[k])
+        for k, ref in enumerate(piece_refs)
+    ]
+
+
+def scatter(me_ref, packed_ref, piece_refs, sems):
+    chip = me_ref[0] // 2
+    return [
+        pltpu.make_async_copy(packed_ref.at[chip ^ k], ref, sems.at[k])
+        for k, ref in enumerate(piece_refs)
+    ]
 
 
 def train_step(x_ref, y_ref, win, wout, min_, mout, hid, dout, dpre, block):
@@ -172,25 +189,44 @@
     win[...] = win[...] - LEARN_RATE * moment.astype(F32)
 
 
-def later_visit_kernel(slots, block, x_ref, y_ref, arrived, sent, *scratch):
-    state, work = scratch[:4], scratch[4:]
+def send_out(slots, pieces, me_ref, state, refs, packed, sems):
+    weights_ref, moment_refs = refs[0], refs[1:]
+    pack(state[2:], slots[pieces], packed)
+    copies = scatter(me_ref, packed, moment_refs, sems)
+    for copy in copies:
+        copy.start()
+    pack(state[:2], slots[2 * pieces], weights_ref)
+    for copy in copies:
+        copy.wait()
+
+
+def later_visit_kernel(slots, pieces, block, me_ref, x_ref, y_ref, weights_ref, *refs):
+    moment_refs, sent, scratch = refs[:pieces], refs[pieces:][: pieces + 1], refs[2 * pieces + 1 :]
+    state, work, (packed, sems) = scratch[:4], scratch[4:7], scratch[7:9]
     step = pl.program_id(0)
 
     @pl.when(step == 0)
     def _():
-        unpack(arrived, slots, state)
+        copies = collect(me_ref, moment_refs, packed, sems)
+        for copy in copies:
+            copy.start()
+        unpack(weights_ref, slots[2 * pieces], state[:2])
+        for copy in copies:
+            copy.wait()
+        unpack(packed, slots[pieces], state[2:])
 
     train_step(x_ref, y_ref, *state, *work, block)
 
     @pl.when(step == pl.num_programs(0) - 1)
     def _():
-        pack(state, slots, sent)
-
-
-def first_visit_kernel(slots, block, picks_ref, x_ref, y_ref, *refs):
-    model, sent, scratch = refs[:4], refs[4], refs[5:]
-    state, work, batch = scratch[:4], scratch[4:7], scratch[7:9]
-    held, table, picked, sems, model_sems = scratch[9:]
+        send_out(slots, pieces, me_ref, state, sent, packed, sems)
+
+
+def first_visit_kernel(slots, pieces, block, me_ref, picks_ref, x_ref, y_ref, *refs):
+    model, sent, scratch = refs[:4], refs[4:][: pieces + 1], refs[pieces + 5 :]
+    state, work, (packed, packed_sems) = scratch[:4], scratch[4:7], scratch[7:9]
+    batch = scratch[9:11]
+    held, table, picked, sems, model_sems = scratch[11:]
     step = pl.program_id(0)
 
     @pl.when(step == 0)
@@ -211,7 +247,7 @@
 
     @pl.when(step == pl.num_programs(0) - 1)
     def _():
-        pack(state, slots, sent)
+        send_out(slots, pieces, me_ref, state, sent, packed, packed_sems)
 
 
 def whole(shape):
@@ -222,14 +258,19 @@
 ANYWHERE = pl.BlockSpec(memory_space=pl.ANY)
 
 
-def visit(kernel, args, in_specs, more_scratch, limit, sizes, slots, packed_shape):
+def visit(kernel, args, in_specs, more_scratch, limit, sizes, slots):
     steps, rows, width, hidden = sizes
-    return pl.pallas_call(
-        functools.partial(kernel, slots, rows // 4),
+    pieces = min(slots)
+    depth = 2 * width * hidden // (SUB * LANE)
+    piece_shape = (depth // pieces, SUB, LANE)
+    packed_shape = (2 * pieces, depth // (2 * pieces), SUB, LANE)
+    outs = pl.pallas_call(
+        functools.partial(kernel, slots, pieces, rows // 4),
         grid=(steps,),
         in_specs=in_specs,
-        out_specs=whole(packed_shape),
-        out_shape=jax.ShapeDtypeStruct(packed_shape, BF16),
+        out_specs=[whole(packed_shape)] + [ANYWHERE] * pieces,
+        out_shape=[jax.ShapeDtypeStruct(packed_shape, BF16)]
+        + [jax.ShapeDtypeStruct(piece_shape, BF16)] * pieces,
         scratch_shapes=[
             pltpu.VMEM((width, hidden), F32),
             pltpu.VMEM((hidden, width), F32),
@@ -238,6 +279,8 @@
             pltpu.VMEM((rows, hidden), BF16),
             pltpu.VMEM((rows, width), BF16),
             pltpu.VMEM((rows, hidden), BF16),
+            pltpu.VMEM((pieces, *piece_shape), BF16),
+            pltpu.SemaphoreType.DMA((pieces,)),
             *more_scratch,
         ],
         cost_estimate=pl.CostEstimate(
@@ -248,35 +291,34 @@
         compiler_params=pltpu.CompilerParams(vmem_limit_bytes=limit * MIB),
         name="visit",
     )(*args)
-
-
-def first_visit(features, targets, picks, model, sizes, slots, packed_shape):
+    return outs[0], outs[1:]
+
+
+def first_visit(me, features, targets, picks, model, sizes, slots):
     _, rows, width, _ = sizes
     scratch = [pltpu.VMEM((rows, width), BF16)] * 2 + table_scratch(features, rows)
     return visit(
         first_visit_kernel,
-        (picks, features, targets, *model),
-        [SCALARS] + [ANYWHERE] * 6,
+        (me, picks, features, targets, *model),
+        [SCALARS] * 2 + [ANYWHERE] * 6,
         scratch + [pltpu.SemaphoreType.DMA((4,))],
         FIRST_MIB,
         sizes,
         slots,
-        packed_shape,
     )
 
 
-def later_visit(batch, packed, sizes, slots):
+def later_visit(me, batch, weights, moments, sizes, slots):
     _, rows, width, _ = sizes
     batch_spec = pl.BlockSpec((rows, width), lambda step: (step, 0))
     return visit(
         later_visit_kernel,
-        (*batch, packed),
-        [batch_spec, batch_spec, whole(packed.shape)],
+        (me, *batch, weights, *moments),
+        [SCALARS, batch_spec, batch_spec, whole(weights.shape)] + [ANYWHERE] * len(moments),
         [],
         LATER_MIB,
         sizes,
         slots,
-        packed.shape,
     )
 
 
@@ -323,6 +365,92 @@
     )(packed)
 
 
+def stack_kernel(*refs):
+    parts, out_ref, sems = refs[:-2], refs[-2], refs[-1]
+    copies = [
+        pltpu.make_async_copy(ref, out_ref.at[k], sems.at[k]) for k, ref in enumerate(parts)
+    ]
+    for copy in copies:
+        copy.start()
+    for copy in copies:
+        copy.wait()
+
+
+def stacked(parts):
+    shape = (len(parts), *parts[0].shape)
+    return pl.pallas_call(
+        stack_kernel,
+        in_specs=[ANYWHERE] * len(parts),
+        out_specs=pl.BlockSpec(memory_space=pltpu.VMEM),
+        out_shape=jax.ShapeDtypeStruct(shape, parts[0].dtype),
+        scratch_shapes=[pltpu.SemaphoreType.DMA((len(parts),))],
+        compiler_params=pltpu.CompilerParams(vmem_limit_bytes=8 * MIB),
+        name="stack",
+    )(*parts)
+
+
+def route_kernel(pieces, me_ref, source_ref, own_ref, partner_ref, *refs):
+    out_refs, sems = refs[:pieces], refs[pieces]
+    chip, core = me_ref[0] // 2, me_ref[0] % 2
+    for k, out_ref in enumerate(out_refs):
+        source = source_ref[2 * (chip ^ k) + core]
+        place = chip ^ (source // 2)
+
+        @pl.when(source % 2 == core)
+        def _():
+            pltpu.make_async_copy(own_ref.at[place], out_ref, sems.at[k]).start()
+
+        @pl.when(source % 2 != core)
+        def _():
+            pltpu.make_async_copy(partner_ref.at[place], out_ref, sems.at[k]).start()
+
+    for k, out_ref in enumerate(out_refs):
+        pltpu.make_async_copy(own_ref.at[0], out_ref, sems.at[k]).wait()
+
+
+def route(me, source, own, partner):
+    pieces = own.shape[0]
+    in_vmem = pl.BlockSpec(memory_space=pltpu.VMEM)
+    return pl.pallas_call(
+        functools.partial(route_kernel, pieces),
+        in_specs=[SCALARS, SCALARS, in_vmem, in_vmem],
+        out_specs=[ANYWHERE] * pieces,
+        out_shape=[jax.ShapeDtypeStruct(own.shape[1:], own.dtype)] * pieces,
+        scratch_shapes=[pltpu.SemaphoreType.DMA((pieces,))],
+        cost_estimate=pl.CostEstimate(
+            flops=0, bytes_accessed=4 * own.size, transcendentals=0
+        ),
+        compiler_params=pltpu.CompilerParams(vmem_limit_bytes=8 * MIB),
+        name="route",
+    )(me, source, own, partner)
+
+
+def unpack_pieces_kernel(slots, pieces, me_ref, *refs):
+    given, outs, (packed, sems) = refs[:pieces], refs[pieces:-2], refs[-2:]
+    copies = collect(me_ref, given, packed, sems)
+    for copy in copies:
+        copy.start()
+    for copy in copies:
+        copy.wait()
+    unpack(packed, slots, outs)
+
+
+def unpack_pieces(me, given, slots, outs):
+    pieces = len(given)
+    return pl.pallas_call(
+        functools.partial(unpack_pieces_kernel, slots, pieces),
+        in_specs=[SCALARS] + [ANYWHERE] * pieces,
+        out_specs=[pl.BlockSpec(memory_space=pltpu.VMEM)] * len(outs),
+        out_shape=[jax.ShapeDtypeStruct(shape, dtype) for shape, dtype in outs],
+        scratch_shapes=[
+            pltpu.VMEM((pieces, *given[0].shape), BF16),
+            pltpu.SemaphoreType.DMA((pieces,)),
+        ],
+        compiler_params=pltpu.CompilerParams(vmem_limit_bytes=16 * MIB),
+        name="unpack",
+    )(me, *given)
+
+
 def unpack_kernel(slots, packed_ref, *out_refs):
     unpack(packed_ref, slots, out_refs)
 
@@ -338,33 +466,53 @@
     return lax.all_to_all(packed, "hop", split_axis=0, concat_axis=0, tiled=True)
 
 
-def move(packed, source, beside=()):
-    spread = exchange(packed)
+def spread(parts, devices):
+    moved = [None] * len(parts)
+    moved[0] = parts[0]
+    for k in sorted(range(1, len(parts)), reverse=True):
+        moved[k] = lax.ppermute(parts[k], "hop", [(i, i ^ (2 * k)) for i in range(devices)])
+    return moved
+
+
+def move(weights, moments, me, source, devices, beside=()):
+    weights = exchange(weights)
+    moments = spread(moments, devices)
     if beside:
-        spread, *beside = lax.optimization_barrier((spread, *beside))
-    return exchange(reorder(spread, source)), beside
+        weights, *beside = lax.optimization_barrier((weights, *beside))
+    weights = reorder(weights, source)
+    weights = exchange(weights)
+    own = stacked(moments)
+    partner = lax.ppermute(own, "hop", [(i, i ^ 1) for i in range(devices)])
+    moments = route(me, source, own, partner)
+    moments = spread(moments, devices)
+    return weights, moments, beside
 
 
 def on_device(
     features, targets, row_index, hop_order, weight_in, weight_out, moment_in, moment_out
 ):
     devices = lax.axis_size("hop")
+    me = lax.axis_index("hop").astype(jnp.int32).reshape(1)
     model = (weight_in[0], weight_out[0], moment_in[0], moment_out[0])
-    shapes = [member.shape for member in model]
-    slots, depth = tile_slots(shapes, devices)
-    packed_shape = (devices, depth, SUB, LANE)
+    outs = [(member.shape, member.dtype) for member in model]
+    shapes = [member.shape for member in model[:2]]
+    pieces = devices // 2
+    slots = {count: tile_slots(shapes, count)[0] for count in (pieces, devices)}
     _, visits, steps, rows = row_index.shape
     sizes = (steps, rows, *shapes[0])
     picks = jnp.transpose(row_index, (0, 2, 1, 3))
     sources = [invert(hop_order[visit_index]) for visit_index in range(visits)]
-    packed = first_visit(features, targets, picks, model, sizes, slots, packed_shape)
+    weights, moments = first_visit(me, features, targets, picks, model, sizes, slots)
     for visit_index in range(1, visits):
         batch = fetch(features, targets, picks, visit_index)
-        packed, batch = move(packed, sources[visit_index - 1], batch)
-        packed = later_visit(batch, packed, sizes, slots)
-    packed, _ = move(packed, sources[-1])
-    outs = unpack_blocks(packed, [(m.shape, m.dtype) for m in model], devices)
-    return tuple(member[None] for member in outs)
+        weights, moments, batch = move(
+            weights, moments, me, sources[visit_index - 1], devices, batch
+        )
+        weights, moments = later_visit(me, batch, weights, moments, sizes, slots)
+    weights, moments, _ = move(weights, moments, me, sources[-1], devices)
+    weights = unpack_blocks(weights, outs[:2], devices)
+    moments = unpack_pieces(me, moments, slots[pieces], outs[2:])
+    return tuple(member[None] for member in (*weights, *moments))
 
 
 def solution(mesh):

time: 202 us -> 237 us (1.17); the launches traced: 201 us -> 233 us
  blocking collectives: 89.8 us -> 0 us
  starting transfers between devices: 11.9 us -> 79.4 us
  waiting for transfers between devices: 54.4 us -> 86.3 us
  local copies, waits for them, and re-layouts: 0.02 us -> 14.8 us
  Pallas kernels: 44.3 us -> 52 us
    all_to_all x2 -> x0, blocking collectives: 89.8 us -> none  [exchange(): lax.all_to_all(packed, 'hop', split_axis=0, concat_axis=0, tiled=True)]
    ppermute x0 -> x30, waiting for transfers between devices: none -> 59.5 us  [the longest x28 55.7 us: spread(): lax.ppermute(parts[k], 'hop', [(i, i ^ 2 * k) for i in range(devices)])]
    ppermute x0 -> x30, starting transfers between devices: none -> 54.1 us  [the longest x28 50.9 us: spread(): lax.ppermute(parts[k], 'hop', [(i, i ^ 2 * k) for i in range(devices)])]
    all_to_all x2 -> x4, waiting for transfers between devices: 54.4 us -> 26.8 us  [exchange(): lax.all_to_all(packed, 'hop', split_axis=0, concat_axis=0, tiled=True)]
    unnamed x6 -> x62, local copies, waits for them, and re-layouts: 0.01 us -> 14.8 us
    all_to_all x2 -> x4, starting transfers between devices: 11.9 us -> 25.3 us  [exchange(): lax.all_to_all(packed, 'hop', split_axis=0, concat_axis=0, tiled=True)]
    pallas_call x2 -> x7, Pallas kernels: 26.8 us -> 37 us  [the longest x2 29.2 us: visit(): pl.pallas_call(functools.partial(kernel, slots, pieces, rows // 4), grid=...]
    pallas_call x2, Pallas kernels: 5.52 us -> 3.09 us  [reorder(): pl.pallas_call(reorder_kernel, in_specs=[pl.BlockSpec(memory_space=pltpu....]
  transfers between devices with their start and end apart: 2 -> 34, of which waited for: 2 -> 17; matrix products, arithmetic and copies ran while one was open for 0% -> 0% of each run, Pallas kernels for 5% -> 8%
where the time goes in v5:
time: 237 us; the launch traced here: 233 us
  waiting for transfers between devices  86.3 us (36%)
  starting transfers between devices  79.4 us (34%)
  Pallas kernels  52 us (22%)
  local copies, waits for them, and re-layouts  14.8 us (6%)
    ppermute x28, waiting for transfers between devices, spread(): lax.ppermute(parts[k], 'hop', [(i, i ^ 2 * k) for i in range(devices)])  55.7 us
    ppermute x28, starting transfers between devices, spread(): lax.ppermute(parts[k], 'hop', [(i, i ^ 2 * k) for i in range(devices)])  50.9 us
    pallas_call x2, Pallas kernels, visit(): pl.pallas_call(functools.partial(kernel, slots, pieces, rows // 4), grid=...  29.2 us
    all_to_all x4, waiting for transfers between devices, exchange(): lax.all_to_all(packed, 'hop', split_axis=0, concat_axis=0, tiled=True)  26.8 us
    all_to_all x4, starting transfers between devices, exchange(): lax.all_to_all(packed, 'hop', split_axis=0, concat_axis=0, tiled=True)  25.3 us
    unnamed x62, local copies, waits for them, and re-layouts  14.8 us
    pallas_call x1, Pallas kernels, fetch(): pl.pallas_call(functools.partial(fetch_kernel, visit_index), in_specs=[SC...  10.2 us
  transfers between devices with their start and end apart: 34, of which 17 were waited for; matrix products, arithmetic and copies ran while one was open for 0% of the time, Pallas kernels for 8%

profile of v5, /device:TPU:1, one launch (start us, length us, event | category | flops | bytes accessed | tf_op | source)
XLA Modules:
  0.0 233.5 jit_solution(4495243954040245135)
XLA Ops:
  0.6 18.1 %visit.2 = (bf16[16,24,8,128]{3,2,1,0:T(8,128)(2,1)}, bf16[48,8,128]{2,1,0:T(8,128)(2,1)}, bf16[48,8,128]{2,1,0:T(8,128)(2,1)}, bf16[48,8,128]{2,1,0:T(8,128)(2,...) custom-call(s32[1]{0:T(128)} %bitcast.1.me_ref, ...), custom_call_target="tpu_custom_call" | custom-call | flops 3019898880 | bytes 8650752 | tf_op jit(solution)/shard_map/visit/pallas_call | solution.py:267
  18.8 7.4 %all-to-all-start = ((bf16[16,24,8,128]{3,2,1,0:T(8,128)(2,1)}), bf16[16,24,8,128]{3,2,1,0:T(8,128)(2,1)S(1)}, u32[]{:S(2)}, u32[]{:S(2)}) async-start(bf16[16,24,8,128]{3,2,1,0:T(8,128)(2,1)} %get-tuple-element.47), calls=%async_computation | async-start | bytes 1572864 | tf_op jit(solution)/shard_map/all_to_all | solution.py:466
  26.1 10.2 %fetch.1 = (bf16[1536,384]{1,0:T(8,128)(2,1)}, bf16[1536,384]{1,0:T(8,128)(2,1)}) custom-call(s32[1,3,2,512]{3,2,1,0:T(2,128)} %bitcast.15, bf16[4096,384]{1,0:T(8,128)(2,1)} %x_ref.3, bf16[4096,384]{1,0:T(8,128)(2,1)} %y_ref.3), custom_call_target="tpu_custom_call" | custom-call | bytes 6291456 | tf_op jit(solution)/shard_map/fetch/pallas_call | solution.py:93
  36.5 8.2 %all-to-all-done.packed_ref = bf16[16,24,8,128]{3,2,1,0:T(8,128)(2,1)S(1)} async-done(((bf16[16,24,8,128]{3,2,1,0:T(8,128)(2,1)}), bf16[16,24,8,128]{3,2,1,0:T(8,128)(2,1)S(1)}, u32[]{:S(2)}, u32[]{:S(2)}) %all-to-all-start) | async-done | bytes 786464 | tf_op jit(solution)/shard_map/all_to_all | solution.py:466
  44.8 1.5 reorder.2
  46.3 5.5 %all-to-all-start.1 = ((bf16[16,24,8,128]{3,2,1,0:T(8,128)(2,1)}), bf16[16,24,8,128]{3,2,1,0:T(8,128)(2,1)S(1)}, u32[]{:S(2)}, u32[]{:S(2)}) async-start(bf16[16,24,8,128]{3,2,1,0:T(8,128)(2,1)} %reorder.2), calls=%async_computation.1 | async-start | bytes 1572864 | tf_op jit(solution)/shard_map/all_to_all | solution.py:466
  51.8 1.4 collective-permute-start
  53.1 1.2 collective-permute-start.1
  54.4 2.3 collective-permute-start.3
  57.8 3.0 %collective-permute-done.refs_1_ = bf16[48,8,128]{2,1,0:T(8,128)(2,1)S(1)} collective-permute-done((bf16[48,8,128]{2,1,0:T(8,128)(2,1)}, bf16[48,8,128]{2,1,0:T(8,128)(2,1)S(1)}, u32[]{:S(2)}, u32[]{:S(2)}) %collective-permute-start) | collective-permute-done | bytes 98336 | tf_op jit(solution)/shard_map/ppermute | solution.py:473
  60.8 4.0 %collective-permute-start.5 = (bf16[48,8,128]{2,1,0:T(8,128)(2,1)S(1)}, bf16[48,8,128]{2,1,0:T(8,128)(2,1)S(1)}, u32[]{:S(2)}, u32[]{:S(2)}) collective-permute-start(bf16[48,8,128]{2,1,0:T(8,128)(2,1)S(1)} %copy-done.29), channel_id=1, source_target_pairs={{0,12},{1,13},{2,14},{3,15},{4,8},{5,9},{6,10},{7,11},{8,4},{9,5},... | collective-permute-start | bytes 294920 | tf_op jit(solution)/shard_map/ppermute | solution.py:473
  64.8 2.4 %collective-permute-done.1.refs_2_ = bf16[48,8,128]{2,1,0:T(8,128)(2,1)S(1)} collective-permute-done((bf16[48,8,128]{2,1,0:T(8,128)(2,1)}, bf16[48,8,128]{2,1,0:T(8,128)(2,1)S(1)}, u32[]{:S(2)}, u32[]{:S(2)}) %collective-permute-start.1) | collective-permute-done | bytes 98336 | tf_op jit(solution)/shard_map/ppermute | solution.py:473
  67.2 3.7 %collective-permute-start.6 = (bf16[48,8,128]{2,1,0:T(8,128)(2,1)S(1)}, bf16[48,8,128]{2,1,0:T(8,128)(2,1)S(1)}, u32[]{:S(2)}, u32[]{:S(2)}) collective-permute-start(bf16[48,8,128]{2,1,0:T(8,128)(2,1)S(1)} %copy-done.28), channel_id=1, source_target_pairs={{0,14},{1,15},{2,12},{3,13},{4,10},{5,11},{6,8},{7,9},{8,6},{9,7},... | collective-permute-start | bytes 294920 | tf_op jit(solution)/shard_map/ppermute | solution.py:473
  71.7 10.6 %collective-permute-done.3.refs_4_ = bf16[48,8,128]{2,1,0:T(8,128)(2,1)S(1)} collective-permute-done((bf16[48,8,128]{2,1,0:T(8,128)(2,1)}, bf16[48,8,128]{2,1,0:T(8,128)(2,1)S(1)}, u32[]{:S(2)}, u32[]{:S(2)}) %collective-permute-start.3) | collective-permute-done | bytes 98336 | tf_op jit(solution)/shard_map/ppermute | solution.py:473
  82.4 3.0 %collective-permute-done.4.refs_5_ = bf16[48,8,128]{2,1,0:T(8,128)(2,1)S(1)} collective-permute-done((bf16[48,8,128]{2,1,0:T(8,128)(2,1)S(1)}, bf16[48,8,128]{2,1,0:T(8,128)(2,1)S(1)}, u32[]{:S(2)}, u32[]{:S(2)}) %collective-permute-start.4) | collective-permute-done | bytes 98336 | tf_op jit(solution)/shard_map/ppermute | solution.py:473
  86.4 1.6 collective-permute-start.7
  88.1 1.9 collective-permute-done.7.partner_ref
  90.0 1.8 route.2
  92.7 3.9 %collective-permute-start.9 = (bf16[48,8,128]{2,1,0:T(8,128)(2,1)S(1)}, bf16[48,8,128]{2,1,0:T(8,128)(2,1)S(1)}, u32[]{:S(2)}, u32[]{:S(2)}) collective-permute-start(bf16[48,8,128]{2,1,0:T(8,128)(2,1)S(1)} %get-tuple-element.63), channel_id=1, source_target_pairs={{0,4},{1,5},{2,6},{3,7},{4,0},{5,1},{6,2},{7,3},{8,12},{9,13},{10,... | collective-permute-start | bytes 294920 | tf_op jit(solution)/shard_map/ppermute | solution.py:473
  97.5 1.5 collective-permute-start.11
  100.5 1.2 collective-permute-start.13
  102.4 2.9 %collective-permute-start.14 = (bf16[48,8,128]{2,1,0:T(8,128)(2,1)S(1)}, bf16[48,8,128]{2,1,0:T(8,128)(2,1)S(1)}, u32[]{:S(2)}, u32[]{:S(2)}) collective-permute-start(bf16[48,8,128]{2,1,0:T(8,128)(2,1)S(1)} %get-tuple-element.68), channel_id=1, source_target_pairs={{0,14},{1,15},{2,12},{3,13},{4,10},{5,11},{6,8},{7,9},{8,6},{9,7},... | collective-permute-start | bytes 294920 | tf_op jit(solution)/shard_map/ppermute | solution.py:473
  106.6 6.8 %collective-permute-done.12.refs_5_ = bf16[48,8,128]{2,1,0:T(8,128)(2,1)S(1)} collective-permute-done((bf16[48,8,128]{2,1,0:T(8,128)(2,1)S(1)}, bf16[48,8,128]{2,1,0:T(8,128)(2,1)S(1)}, u32[]{:S(2)}, u32[]{:S(2)}) %collective-permute-start.12) | collective-permute-done | bytes 98336 | tf_op jit(solution)/shard_map/ppermute | solution.py:473
  122.5 11.1 %visit.3 = (bf16[16,24,8,128]{3,2,1,0:T(8,128)(2,1)}, bf16[48,8,128]{2,1,0:T(8,128)(2,1)S(1)}, bf16[48,8,128]{2,1,0:T(8,128)(2,1)S(1)}, bf16[48,8,128]{2,1,0:T(8...) custom-call(s32[1]{0:T(128)} %bitcast.1.me_ref, ...), custom_call_target="tpu_custom_call" | custom-call | flops 3019898880 | bytes 8650752 | tf_op jit(solution)/shard_map/visit/pallas_call | solution.py:267
  136.1 7.0 %all-to-all-start.2 = ((bf16[16,24,8,128]{3,2,1,0:T(8,128)(2,1)}), bf16[16,24,8,128]{3,2,1,0:T(8,128)(2,1)S(1)}, u32[]{:S(2)}, u32[]{:S(2)}) async-start(bf16[16,24,8,128]{3,2,1,0:T(8,128)(2,1)} %get-tuple-element.69), calls=%async_computation.2 | async-start | bytes 1572864 | tf_op jit(solution)/shard_map/all_to_all | solution.py:466
  143.2 18.5 %all-to-all-done.2.packed_ref = bf16[16,24,8,128]{3,2,1,0:T(8,128)(2,1)S(1)} async-done(((bf16[16,24,8,128]{3,2,1,0:T(8,128)(2,1)}), bf16[16,24,8,128]{3,2,1,0:T(8,128)(2,1)S(1)}, u32[]{:S(2)}, u32[]{:S(2)}) %all-to-all-start.2) | async-done | bytes 786464 | tf_op jit(solution)/shard_map/all_to_all | solution.py:466
  161.7 1.5 reorder.3
  163.3 5.5 %all-to-all-start.3 = ((bf16[16,24,8,128]{3,2,1,0:T(8,128)(2,1)}), bf16[16,24,8,128]{3,2,1,0:T(8,128)(2,1)S(1)}, u32[]{:S(2)}, u32[]{:S(2)}) async-start(bf16[16,24,8,128]{3,2,1,0:T(8,128)(2,1)} %reorder.3), calls=%async_computation.3 | async-start | bytes 1572864 | tf_op jit(solution)/shard_map/all_to_all | solution.py:466
  168.7 1.4 collective-permute-start.15
  170.1 1.2 collective-permute-start.16
  171.4 2.3 collective-permute-start.18
  173.7 1.2 collective-permute-start.19
  174.9 2.9 %collective-permute-done.15.refs_1_ = bf16[48,8,128]{2,1,0:T(8,128)(2,1)S(1)} collective-permute-done((bf16[48,8,128]{2,1,0:T(8,128)(2,1)S(1)}, bf16[48,8,128]{2,1,0:T(8,128)(2,1)S(1)}, u32[]{:S(2)}, u32[]{:S(2)}) %collective-permute-start.15) | collective-permute-done | bytes 98336 | tf_op jit(solution)/shard_map/ppermute | solution.py:473
  177.8 4.0 %collective-permute-start.20 = (bf16[48,8,128]{2,1,0:T(8,128)(2,1)S(1)}, bf16[48,8,128]{2,1,0:T(8,128)(2,1)S(1)}, u32[]{:S(2)}, u32[]{:S(2)}) collective-permute-start(bf16[48,8,128]{2,1,0:T(8,128)(2,1)S(1)} %get-tuple-element.78), channel_id=1, source_target_pairs={{0,12},{1,13},{2,14},{3,15},{4,8},{5,9},{6,10},{7,11},{8,4},{9,5},... | collective-permute-start | bytes 294920 | tf_op jit(solution)/shard_map/ppermute | solution.py:473
  181.8 2.3 collective-permute-done.16.refs_2_
  184.1 3.7 %collective-permute-start.21 = (bf16[48,8,128]{2,1,0:T(8,128)(2,1)S(1)}, bf16[48,8,128]{2,1,0:T(8,128)(2,1)S(1)}, u32[]{:S(2)}, u32[]{:S(2)}) collective-permute-start(bf16[48,8,128]{2,1,0:T(8,128)(2,1)S(1)} %get-tuple-element.79), channel_id=1, source_target_pairs={{0,14},{1,15},{2,12},{3,13},{4,10},{5,11},{6,8},{7,9},{8,6},{9,7},... | collective-permute-start | bytes 294920 | tf_op jit(solution)/shard_map/ppermute | solution.py:473
  188.7 10.6 %collective-permute-done.18.refs_4_ = bf16[48,8,128]{2,1,0:T(8,128)(2,1)S(1)} collective-permute-done((bf16[48,8,128]{2,1,0:T(8,128)(2,1)S(1)}, bf16[48,8,128]{2,1,0:T(8,128)(2,1)S(1)}, u32[]{:S(2)}, u32[]{:S(2)}) %collective-permute-start.18) | collective-permute-done | bytes 98336 | tf_op jit(solution)/shard_map/ppermute | solution.py:473
  199.3 3.0 %collective-permute-done.19.refs_5_ = bf16[48,8,128]{2,1,0:T(8,128)(2,1)S(1)} collective-permute-done((bf16[48,8,128]{2,1,0:T(8,128)(2,1)S(1)}, bf16[48,8,128]{2,1,0:T(8,128)(2,1)S(1)}, u32[]{:S(2)}, u32[]{:S(2)}) %collective-permute-start.19) | collective-permute-done | bytes 98336 | tf_op jit(solution)/shard_map/ppermute | solution.py:473
  203.4 1.6 collective-permute-start.22
  205.0 1.9 collective-permute-done.22.partner_ref
  206.9 1.8 route.3
  209.1 3.9 %collective-permute-start.24 = (bf16[48,8,128]{2,1,0:T(8,128)(2,1)S(1)}, bf16[48,8,128]{2,1,0:T(8,128)(2,1)S(1)}, u32[]{:S(2)}, u32[]{:S(2)}) collective-permute-start(bf16[48,8,128]{2,1,0:T(8,128)(2,1)S(1)} %get-tuple-element.82), channel_id=1, source_target_pairs={{0,4},{1,5},{2,6},{3,7},{4,0},{5,1},{6,2},{7,3},{8,12},{9,13},{10,... | collective-permute-start | bytes 294920 | tf_op jit(solution)/shard_map/ppermute | solution.py:473
  213.8 1.5 collective-permute-start.26
  216.3 1.2 collective-permute-start.28
  217.5 2.9 %collective-permute-start.29 = (bf16[48,8,128]{2,1,0:T(8,128)(2,1)S(1)}, bf16[48,8,128]{2,1,0:T(8,128)(2,1)S(1)}, u32[]{:S(2)}, u32[]{:S(2)}) collective-permute-start(bf16[48,8,128]{2,1,0:T(8,128)(2,1)S(1)} %get-tuple-element.87), channel_id=1, source_target_pairs={{0,14},{1,15},{2,12},{3,13},{4,10},{5,11},{6,8},{7,9},{8,6},{9,7},... | collective-permute-start | bytes 294920 | tf_op jit(solution)/shard_map/ppermute | solution.py:473
  221.2 8.6 %collective-permute-done.27.refs_5_ = bf16[48,8,128]{2,1,0:T(8,128)(2,1)S(1)} collective-permute-done((bf16[48,8,128]{2,1,0:T(8,128)(2,1)S(1)}, bf16[48,8,128]{2,1,0:T(8,128)(2,1)S(1)}, u32[]{:S(2)}, u32[]{:S(2)}) %collective-permute-start.27) | collective-permute-done | bytes 98336 | tf_op jit(solution)/shard_map/ppermute | solution.py:473
  229.8 2.0 unpack.3
  231.8 1.7 unpack.2
  (96 shorter events, 25.2 us)
Async XLA Ops:
  18.8 26.0 %all-to-all-start = ((bf16[16,24,8,128]{3,2,1,0:T(8,128)(2,1)}), bf16[16,24,8,128]{3,2,1,0:T(8,128)(2,1)S(1)}, u32[]{:S(2)}, u32[]{:S(2)}) async-start(bf16[16,24,8,128]{3,2,1,0:T(8,128)(2,1)} %get-tuple-element.47), calls=%async_computation | async-start | bytes 1572864 | tf_op jit(solution)/shard_map/all_to_all | solution.py:466
  26.1 10.2 %copy-start.27 = (s32[2,16]{1,0:T(2,128)S(1)}, s32[2,16]{1,0:T(2,128)}, u32[]{:S(2)}) copy-start(s32[2,16]{1,0:T(2,128)} %param.11) | copy-start | bytes 388
  36.4 20.3 %copy-start.30 = (bf16[48,8,128]{2,1,0:T(8,128)(2,1)S(1)}, bf16[48,8,128]{2,1,0:T(8,128)(2,1)}, u32[]{:S(2)}) copy-start(bf16[48,8,128]{2,1,0:T(8,128)(2,1)} %get-tuple-element.58) | copy-start | bytes 294916
  36.4 24.4 %copy-start.29 = (bf16[48,8,128]{2,1,0:T(8,128)(2,1)S(1)}, bf16[48,8,128]{2,1,0:T(8,128)(2,1)}, u32[]{:S(2)}) copy-start(bf16[48,8,128]{2,1,0:T(8,128)(2,1)} %get-tuple-element.59) | copy-start | bytes 294916
  36.4 30.8 %copy-start.28 = (bf16[48,8,128]{2,1,0:T(8,128)(2,1)S(1)}, bf16[48,8,128]{2,1,0:T(8,128)(2,1)}, u32[]{:S(2)}) copy-start(bf16[48,8,128]{2,1,0:T(8,128)(2,1)} %get-tuple-element.60) | copy-start | bytes 294916
  36.4 48.9 %copy-start = (bf16[48,8,128]{2,1,0:T(8,128)(2,1)S(1)}, bf16[48,8,128]{2,1,0:T(8,128)(2,1)}, u32[]{:S(2)}) copy-start(bf16[48,8,128]{2,1,0:T(8,128)(2,1)} %get-tuple-element.53.refs_0_) | copy-start | bytes 294916
  44.8 70.5 %copy-start.1 = (bf16[1536,384]{1,0:T(8,128)(2,1)S(1)}, bf16[1536,384]{1,0:T(8,128)(2,1)}, u32[]{:S(2)}) copy-start(bf16[1536,384]{1,0:T(8,128)(2,1)} %get-tuple-element.50.x_ref) | copy-start | bytes 3538948
  44.8 70.5 %copy-start.2 = (bf16[1536,384]{1,0:T(8,128)(2,1)S(1)}, bf16[1536,384]{1,0:T(8,128)(2,1)}, u32[]{:S(2)}) copy-start(bf16[1536,384]{1,0:T(8,128)(2,1)} %get-tuple-element.51.y_ref) | copy-start | bytes 3538948
  46.3 69.0 %all-to-all-start.1 = ((bf16[16,24,8,128]{3,2,1,0:T(8,128)(2,1)}), bf16[16,24,8,128]{3,2,1,0:T(8,128)(2,1)S(1)}, u32[]{:S(2)}, u32[]{:S(2)}) async-start(bf16[16,24,8,128]{3,2,1,0:T(8,128)(2,1)} %reorder.2), calls=%async_computation.1 | async-start | bytes 1572864 | tf_op jit(solution)/shard_map/all_to_all | solution.py:466
  51.8 9.1 %collective-permute-start = (bf16[48,8,128]{2,1,0:T(8,128)(2,1)}, bf16[48,8,128]{2,1,0:T(8,128)(2,1)S(1)}, u32[]{:S(2)}, u32[]{:S(2)}) collective-permute-start(bf16[48,8,128]{2,1,0:T(8,128)(2,1)} %get-tuple-element.54), channel_id=1, source_target_pairs={{0,2},{1,3},{2,0},{3,1},{4,6},{5,7},{6,4},{7,5},{8,10},{9,11},{10,... | collective-permute-start | bytes 294920 | tf_op jit(solution)/shard_map/ppermute | solution.py:473
  53.1 14.1 %collective-permute-start.1 = (bf16[48,8,128]{2,1,0:T(8,128)(2,1)}, bf16[48,8,128]{2,1,0:T(8,128)(2,1)S(1)}, u32[]{:S(2)}, u32[]{:S(2)}) collective-permute-start(bf16[48,8,128]{2,1,0:T(8,128)(2,1)} %get-tuple-element.55), channel_id=1, source_target_pairs={{0,4},{1,5},{2,6},{3,7},{4,0},{5,1},{6,2},{7,3},{8,12},{9,13},{10,... | collective-permute-start | bytes 294920 | tf_op jit(solution)/shard_map/ppermute | solution.py:473
  54.3 17.4 %collective-permute-start.2 = (bf16[48,8,128]{2,1,0:T(8,128)(2,1)}, bf16[48,8,128]{2,1,0:T(8,128)(2,1)S(1)}, u32[]{:S(2)}, u32[]{:S(2)}) collective-permute-start(bf16[48,8,128]{2,1,0:T(8,128)(2,1)} %get-tuple-element.56), channel_id=1, source_target_pairs={{0,6},{1,7},{2,4},{3,5},{4,2},{5,3},{6,0},{7,1},{8,14},{9,15},{10,... | collective-permute-start | bytes 294920 | tf_op jit(solution)/shard_map/ppermute | solution.py:473
  54.4 27.9 %collective-permute-start.3 = (bf16[48,8,128]{2,1,0:T(8,128)(2,1)}, bf16[48,8,128]{2,1,0:T(8,128)(2,1)S(1)}, u32[]{:S(2)}, u32[]{:S(2)}) collective-permute-start(bf16[48,8,128]{2,1,0:T(8,128)(2,1)} %get-tuple-element.57), channel_id=1, source_target_pairs={{0,8},{1,9},{2,10},{3,11},{4,12},{5,13},{6,14},{7,15},{8,0},{9,1},... | collective-permute-start | bytes 294920 | tf_op jit(solution)/shard_map/ppermute | solution.py:473
  56.7 28.7 %collective-permute-start.4 = (bf16[48,8,128]{2,1,0:T(8,128)(2,1)S(1)}, bf16[48,8,128]{2,1,0:T(8,128)(2,1)S(1)}, u32[]{:S(2)}, u32[]{:S(2)}) collective-permute-start(bf16[48,8,128]{2,1,0:T(8,128)(2,1)S(1)} %copy-done.30), channel_id=1, source_target_pairs={{0,10},{1,11},{2,8},{3,9},{4,14},{5,15},{6,12},{7,13},{8,2},{9,3},... | collective-permute-start | bytes 294920 | tf_op jit(solution)/shard_map/ppermute | solution.py:473
  60.8 24.5 %collective-permute-start.5 = (bf16[48,8,128]{2,1,0:T(8,128)(2,1)S(1)}, bf16[48,8,128]{2,1,0:T(8,128)(2,1)S(1)}, u32[]{:S(2)}, u32[]{:S(2)}) collective-permute-start(bf16[48,8,128]{2,1,0:T(8,128)(2,1)S(1)} %copy-done.29), channel_id=1, source_target_pairs={{0,12},{1,13},{2,14},{3,15},{4,8},{5,9},{6,10},{7,11},{8,4},{9,5},... | collective-permute-start | bytes 294920 | tf_op jit(solution)/shard_map/ppermute | solution.py:473
  67.2 18.1 %collective-permute-start.6 = (bf16[48,8,128]{2,1,0:T(8,128)(2,1)S(1)}, bf16[48,8,128]{2,1,0:T(8,128)(2,1)S(1)}, u32[]{:S(2)}, u32[]{:S(2)}) collective-permute-start(bf16[48,8,128]{2,1,0:T(8,128)(2,1)S(1)} %copy-done.28), channel_id=1, source_target_pairs={{0,14},{1,15},{2,12},{3,13},{4,10},{5,11},{6,8},{7,9},{8,6},{9,7},... | collective-permute-start | bytes 294920 | tf_op jit(solution)/shard_map/ppermute | solution.py:473
  86.4 3.5 %collective-permute-start.7 = (bf16[8,48,8,128]{3,2,1,0:T(8,128)(2,1)S(1)}, bf16[8,48,8,128]{3,2,1,0:T(8,128)(2,1)S(1)}, u32[]{:S(2)}, u32[]{:S(2)}) collective-permute-start(bf16[8,48,8,128]{3,2,1,0:T(8,128)(2,1)S(1)} %stack.2.own_ref), channel_id=1, source_target_pairs={{0,1},{1,0},{2,3},{3,2},{4,5},{5,4},{6,7},{7,6},{8,9},{9,8},{10,11... | collective-permute-start | bytes 2359304 | tf_op jit(solution)/shard_map/ppermute | solution.py:485
  92.4 7.5 %collective-permute-start.8 = (bf16[48,8,128]{2,1,0:T(8,128)(2,1)S(1)}, bf16[48,8,128]{2,1,0:T(8,128)(2,1)S(1)}, u32[]{:S(2)}, u32[]{:S(2)}) collective-permute-start(bf16[48,8,128]{2,1,0:T(8,128)(2,1)S(1)} %get-tuple-element.62), channel_id=1, source_target_pairs={{0,2},{1,3},{2,0},{3,1},{4,6},{5,7},{6,4},{7,5},{8,10},{9,11},{10,... | collective-permute-start | bytes 294920 | tf_op jit(solution)/shard_map/ppermute | solution.py:473
  92.7 9.0 %collective-permute-start.9 = (bf16[48,8,128]{2,1,0:T(8,128)(2,1)S(1)}, bf16[48,8,128]{2,1,0:T(8,128)(2,1)S(1)}, u32[]{:S(2)}, u32[]{:S(2)}) collective-permute-start(bf16[48,8,128]{2,1,0:T(8,128)(2,1)S(1)} %get-tuple-element.63), channel_id=1, source_target_pairs={{0,4},{1,5},{2,6},{3,7},{4,0},{5,1},{6,2},{7,3},{8,12},{9,13},{10,... | collective-permute-start | bytes 294920 | tf_op jit(solution)/shard_map/ppermute | solution.py:473
  96.6 8.7 %collective-permute-start.10 = (bf16[48,8,128]{2,1,0:T(8,128)(2,1)S(1)}, bf16[48,8,128]{2,1,0:T(8,128)(2,1)S(1)}, u32[]{:S(2)}, u32[]{:S(2)}) collective-permute-start(bf16[48,8,128]{2,1,0:T(8,128)(2,1)S(1)} %get-tuple-element.64), channel_id=1, source_target_pairs={{0,6},{1,7},{2,4},{3,5},{4,2},{5,3},{6,0},{7,1},{8,14},{9,15},{10,... | collective-permute-start | bytes 294920 | tf_op jit(solution)/shard_map/ppermute | solution.py:473
  97.5 8.5 %collective-permute-start.11 = (bf16[48,8,128]{2,1,0:T(8,128)(2,1)S(1)}, bf16[48,8,128]{2,1,0:T(8,128)(2,1)S(1)}, u32[]{:S(2)}, u32[]{:S(2)}) collective-permute-start(bf16[48,8,128]{2,1,0:T(8,128)(2,1)S(1)} %get-tuple-element.65), channel_id=1, source_target_pairs={{0,8},{1,9},{2,10},{3,11},{4,12},{5,13},{6,14},{7,15},{8,0},{9,1},... | collective-permute-start | bytes 294920 | tf_op jit(solution)/shard_map/ppermute | solution.py:473
  99.0 14.4 %collective-permute-start.12 = (bf16[48,8,128]{2,1,0:T(8,128)(2,1)S(1)}, bf16[48,8,128]{2,1,0:T(8,128)(2,1)S(1)}, u32[]{:S(2)}, u32[]{:S(2)}) collective-permute-start(bf16[48,8,128]{2,1,0:T(8,128)(2,1)S(1)} %get-tuple-element.66), channel_id=1, source_target_pairs={{0,10},{1,11},{2,8},{3,9},{4,14},{5,15},{6,12},{7,13},{8,2},{9,3},... | collective-permute-start | bytes 294920 | tf_op jit(solution)/shard_map/ppermute | solution.py:473
  100.5 13.5 %collective-permute-start.13 = (bf16[48,8,128]{2,1,0:T(8,128)(2,1)S(1)}, bf16[48,8,128]{2,1,0:T(8,128)(2,1)S(1)}, u32[]{:S(2)}, u32[]{:S(2)}) collective-permute-start(bf16[48,8,128]{2,1,0:T(8,128)(2,1)S(1)} %get-tuple-element.67), channel_id=1, source_target_pairs={{0,12},{1,13},{2,14},{3,15},{4,8},{5,9},{6,10},{7,11},{8,4},{9,5},... | collective-permute-start | bytes 294920 | tf_op jit(solution)/shard_map/ppermute | solution.py:473
  102.4 12.3 %collective-permute-start.14 = (bf16[48,8,128]{2,1,0:T(8,128)(2,1)S(1)}, bf16[48,8,128]{2,1,0:T(8,128)(2,1)S(1)}, u32[]{:S(2)}, u32[]{:S(2)}) collective-permute-start(bf16[48,8,128]{2,1,0:T(8,128)(2,1)S(1)} %get-tuple-element.68), channel_id=1, source_target_pairs={{0,14},{1,15},{2,12},{3,13},{4,10},{5,11},{6,8},{7,9},{8,6},{9,7},... | collective-permute-start | bytes 294920 | tf_op jit(solution)/shard_map/ppermute | solution.py:473
  115.3 0.9 copy-start.4
  118.0 0.9 copy-start.14
  118.9 0.9 copy-start.18
  136.1 32.6 %copy-start.22 = (bf16[48,8,128]{2,1,0:T(8,128)(2,1)S(1)}, bf16[48,8,128]{2,1,0:T(8,128)(2,1)}, u32[]{:S(2)}) copy-start(bf16[48,8,128]{2,1,0:T(8,128)(2,1)} %copy-done.21) | copy-start | bytes 294916
  136.1 34.0 %copy-start.16 = (bf16[48,8,128]{2,1,0:T(8,128)(2,1)S(1)}, bf16[48,8,128]{2,1,0:T(8,128)(2,1)}, u32[]{:S(2)}) copy-start(bf16[48,8,128]{2,1,0:T(8,128)(2,1)} %copy-done.15) | copy-start | bytes 294916
  136.1 35.2 %copy-start.8 = (bf16[48,8,128]{2,1,0:T(8,128)(2,1)S(1)}, bf16[48,8,128]{2,1,0:T(8,128)(2,1)}, u32[]{:S(2)}) copy-start(bf16[48,8,128]{2,1,0:T(8,128)(2,1)} %copy-done.7) | copy-start | bytes 294916
  136.1 35.3 %copy-start.6 = (bf16[48,8,128]{2,1,0:T(8,128)(2,1)S(1)}, bf16[48,8,128]{2,1,0:T(8,128)(2,1)}, u32[]{:S(2)}) copy-start(bf16[48,8,128]{2,1,0:T(8,128)(2,1)} %copy-done.5) | copy-start | bytes 294916
  136.1 25.6 %all-to-all-start.2 = ((bf16[16,24,8,128]{3,2,1,0:T(8,128)(2,1)}), bf16[16,24,8,128]{3,2,1,0:T(8,128)(2,1)S(1)}, u32[]{:S(2)}, u32[]{:S(2)}) async-start(bf16[16,24,8,128]{3,2,1,0:T(8,128)(2,1)} %get-tuple-element.69), calls=%async_computation.2 | async-start | bytes 1572864 | tf_op jit(solution)/shard_map/all_to_all | solution.py:466
  163.3 68.5 %all-to-all-start.3 = ((bf16[16,24,8,128]{3,2,1,0:T(8,128)(2,1)}), bf16[16,24,8,128]{3,2,1,0:T(8,128)(2,1)S(1)}, u32[]{:S(2)}, u32[]{:S(2)}) async-start(bf16[16,24,8,128]{3,2,1,0:T(8,128)(2,1)} %reorder.3), calls=%async_computation.3 | async-start | bytes 1572864 | tf_op jit(solution)/shard_map/all_to_all | solution.py:466
  168.7 9.1 %collective-permute-start.15 = (bf16[48,8,128]{2,1,0:T(8,128)(2,1)S(1)}, bf16[48,8,128]{2,1,0:T(8,128)(2,1)S(1)}, u32[]{:S(2)}, u32[]{:S(2)}) collective-permute-start(bf16[48,8,128]{2,1,0:T(8,128)(2,1)S(1)} %copy-done.22), channel_id=1, source_target_pairs={{0,2},{1,3},{2,0},{3,1},{4,6},{5,7},{6,4},{7,5},{8,10},{9,11},{10,... | collective-permute-start | bytes 294920 | tf_op jit(solution)/shard_map/ppermute | solution.py:473
  170.1 13.9 %collective-permute-start.16 = (bf16[48,8,128]{2,1,0:T(8,128)(2,1)S(1)}, bf16[48,8,128]{2,1,0:T(8,128)(2,1)S(1)}, u32[]{:S(2)}, u32[]{:S(2)}) collective-permute-start(bf16[48,8,128]{2,1,0:T(8,128)(2,1)S(1)} %copy-done.16), channel_id=1, source_target_pairs={{0,4},{1,5},{2,6},{3,7},{4,0},{5,1},{6,2},{7,3},{8,12},{9,13},{10,... | collective-permute-start | bytes 294920 | tf_op jit(solution)/shard_map/ppermute | solution.py:473
  171.3 17.4 %collective-permute-start.17 = (bf16[48,8,128]{2,1,0:T(8,128)(2,1)S(1)}, bf16[48,8,128]{2,1,0:T(8,128)(2,1)S(1)}, u32[]{:S(2)}, u32[]{:S(2)}) collective-permute-start(bf16[48,8,128]{2,1,0:T(8,128)(2,1)S(1)} %copy-done.8), channel_id=1, source_target_pairs={{0,6},{1,7},{2,4},{3,5},{4,2},{5,3},{6,0},{7,1},{8,14},{9,15},{10,... | collective-permute-start | bytes 294920 | tf_op jit(solution)/shard_map/ppermute | solution.py:473
  171.4 27.9 %collective-permute-start.18 = (bf16[48,8,128]{2,1,0:T(8,128)(2,1)S(1)}, bf16[48,8,128]{2,1,0:T(8,128)(2,1)S(1)}, u32[]{:S(2)}, u32[]{:S(2)}) collective-permute-start(bf16[48,8,128]{2,1,0:T(8,128)(2,1)S(1)} %copy-done.6), channel_id=1, source_target_pairs={{0,8},{1,9},{2,10},{3,11},{4,12},{5,13},{6,14},{7,15},{8,0},{9,1},... | collective-permute-start | bytes 294920 | tf_op jit(solution)/shard_map/ppermute | solution.py:473
  173.7 28.6 %collective-permute-start.19 = (bf16[48,8,128]{2,1,0:T(8,128)(2,1)S(1)}, bf16[48,8,128]{2,1,0:T(8,128)(2,1)S(1)}, u32[]{:S(2)}, u32[]{:S(2)}) collective-permute-start(bf16[48,8,128]{2,1,0:T(8,128)(2,1)S(1)} %get-tuple-element.77), channel_id=1, source_target_pairs={{0,10},{1,11},{2,8},{3,9},{4,14},{5,15},{6,12},{7,13},{8,2},{9,3},... | collective-permute-start | bytes 294920 | tf_op jit(solution)/shard_map/ppermute | solution.py:473
  177.8 24.5 %collective-permute-start.20 = (bf16[48,8,128]{2,1,0:T(8,128)(2,1)S(1)}, bf16[48,8,128]{2,1,0:T(8,128)(2,1)S(1)}, u32[]{:S(2)}, u32[]{:S(2)}) collective-permute-start(bf16[48,8,128]{2,1,0:T(8,128)(2,1)S(1)} %get-tuple-element.78), channel_id=1, source_target_pairs={{0,12},{1,13},{2,14},{3,15},{4,8},{5,9},{6,10},{7,11},{8,4},{9,5},... | collective-permute-start | bytes 294920 | tf_op jit(solution)/shard_map/ppermute | solution.py:473
  184.1 18.2 %collective-permute-start.21 = (bf16[48,8,128]{2,1,0:T(8,128)(2,1)S(1)}, bf16[48,8,128]{2,1,0:T(8,128)(2,1)S(1)}, u32[]{:S(2)}, u32[]{:S(2)}) collective-permute-start(bf16[48,8,128]{2,1,0:T(8,128)(2,1)S(1)} %get-tuple-element.79), channel_id=1, source_target_pairs={{0,14},{1,15},{2,12},{3,13},{4,10},{5,11},{6,8},{7,9},{8,6},{9,7},... | collective-permute-start | bytes 294920 | tf_op jit(solution)/shard_map/ppermute | solution.py:473
  203.4 3.5 %collective-permute-start.22 = (bf16[8,48,8,128]{3,2,1,0:T(8,128)(2,1)S(1)}, bf16[8,48,8,128]{3,2,1,0:T(8,128)(2,1)S(1)}, u32[]{:S(2)}, u32[]{:S(2)}) collective-permute-start(bf16[8,48,8,128]{3,2,1,0:T(8,128)(2,1)S(1)} %stack.3.own_ref), channel_id=1, source_target_pairs={{0,1},{1,0},{2,3},{3,2},{4,5},{5,4},{6,7},{7,6},{8,9},{9,8},{10,11... | collective-permute-start | bytes 2359304 | tf_op jit(solution)/shard_map/ppermute | solution.py:485
  208.7 7.6 %collective-permute-start.23 = (bf16[48,8,128]{2,1,0:T(8,128)(2,1)S(1)}, bf16[48,8,128]{2,1,0:T(8,128)(2,1)S(1)}, u32[]{:S(2)}, u32[]{:S(2)}) collective-permute-start(bf16[48,8,128]{2,1,0:T(8,128)(2,1)S(1)} %get-tuple-element.81), channel_id=1, source_target_pairs={{0,2},{1,3},{2,0},{3,1},{4,6},{5,7},{6,4},{7,5},{8,10},{9,11},{10,... | collective-permute-start | bytes 294920 | tf_op jit(solution)/shard_map/ppermute | solution.py:473
  209.1 8.4 %collective-permute-start.24 = (bf16[48,8,128]{2,1,0:T(8,128)(2,1)S(1)}, bf16[48,8,128]{2,1,0:T(8,128)(2,1)S(1)}, u32[]{:S(2)}, u32[]{:S(2)}) collective-permute-start(bf16[48,8,128]{2,1,0:T(8,128)(2,1)S(1)} %get-tuple-element.82), channel_id=1, source_target_pairs={{0,4},{1,5},{2,6},{3,7},{4,0},{5,1},{6,2},{7,3},{8,12},{9,13},{10,... | collective-permute-start | bytes 294920 | tf_op jit(solution)/shard_map/ppermute | solution.py:473
  213.0 8.2 %collective-permute-start.25 = (bf16[48,8,128]{2,1,0:T(8,128)(2,1)S(1)}, bf16[48,8,128]{2,1,0:T(8,128)(2,1)S(1)}, u32[]{:S(2)}, u32[]{:S(2)}) collective-permute-start(bf16[48,8,128]{2,1,0:T(8,128)(2,1)S(1)} %get-tuple-element.83), channel_id=1, source_target_pairs={{0,6},{1,7},{2,4},{3,5},{4,2},{5,3},{6,0},{7,1},{8,14},{9,15},{10,... | collective-permute-start | bytes 294920 | tf_op jit(solution)/shard_map/ppermute | solution.py:473
  213.8 7.3 %collective-permute-start.26 = (bf16[48,8,128]{2,1,0:T(8,128)(2,1)S(1)}, bf16[48,8,128]{2,1,0:T(8,128)(2,1)S(1)}, u32[]{:S(2)}, u32[]{:S(2)}) collective-permute-start(bf16[48,8,128]{2,1,0:T(8,128)(2,1)S(1)} %get-tuple-element.84), channel_id=1, source_target_pairs={{0,8},{1,9},{2,10},{3,11},{4,12},{5,13},{6,14},{7,15},{8,0},{9,1},... | collective-permute-start | bytes 294920 | tf_op jit(solution)/shard_map/ppermute | solution.py:473
  215.4 14.4 %collective-permute-start.27 = (bf16[48,8,128]{2,1,0:T(8,128)(2,1)S(1)}, bf16[48,8,128]{2,1,0:T(8,128)(2,1)S(1)}, u32[]{:S(2)}, u32[]{:S(2)}) collective-permute-start(bf16[48,8,128]{2,1,0:T(8,128)(2,1)S(1)} %get-tuple-element.85), channel_id=1, source_target_pairs={{0,10},{1,11},{2,8},{3,9},{4,14},{5,15},{6,12},{7,13},{8,2},{9,3},... | collective-permute-start | bytes 294920 | tf_op jit(solution)/shard_map/ppermute | solution.py:473
  216.3 13.5 %collective-permute-start.28 = (bf16[48,8,128]{2,1,0:T(8,128)(2,1)S(1)}, bf16[48,8,128]{2,1,0:T(8,128)(2,1)S(1)}, u32[]{:S(2)}, u32[]{:S(2)}) collective-permute-start(bf16[48,8,128]{2,1,0:T(8,128)(2,1)S(1)} %get-tuple-element.86), channel_id=1, source_target_pairs={{0,12},{1,13},{2,14},{3,15},{4,8},{5,9},{6,10},{7,11},{8,4},{9,5},... | collective-permute-start | bytes 294920 | tf_op jit(solution)/shard_map/ppermute | solution.py:473
  217.5 12.3 %collective-permute-start.29 = (bf16[48,8,128]{2,1,0:T(8,128)(2,1)S(1)}, bf16[48,8,128]{2,1,0:T(8,128)(2,1)S(1)}, u32[]{:S(2)}, u32[]{:S(2)}) collective-permute-start(bf16[48,8,128]{2,1,0:T(8,128)(2,1)S(1)} %get-tuple-element.87), channel_id=1, source_target_pairs={{0,14},{1,15},{2,12},{3,13},{4,10},{5,11},{6,8},{7,9},{8,6},{9,7},... | collective-permute-start | bytes 294920 | tf_op jit(solution)/shard_map/ppermute | solution.py:473
  (17 other events, 12.1 us)

commit v6 on v5

--- a/solution.py
+++ b/solution.py
@@ -13,8 +13,8 @@
 SUB, LANE = 8, 128
 MIB = 1 << 20
 STRIDE = SUB + 1
-FETCH_BLOCKS, UNROLL, UNPACK_BLOCKS = 4, 16, 4
-FIRST_MIB, FETCH_MIB, LATER_MIB = 58, 58, 28
+FETCH_BLOCKS, UNROLL = 4, 32
+FIRST_MIB, FETCH_MIB, LATER_MIB, LAST_MIB, SETTLE_MIB = 58, 58, 58, 58, 16
 F32, BF16 = jnp.float32, jnp.bfloat16
 HALF_ROOT = 0.7071067811865476
 PDF_SCALE = 0.3989422804014327
@@ -155,10 +155,8 @@
     ]
 
 
-def train_step(x_ref, y_ref, win, wout, min_, mout, hid, dout, dpre, block):
+def gradients(x_ref, y_ref, cast_in, cast_out, hid, dout, dpre, block):
     rows = x_ref.shape[0]
-    cast_in = win[...].astype(BF16)
-    cast_out = wout[...].astype(BF16)
     for start in range(0, rows, block):
         part = slice(start, start + block)
         batch_x = x_ref[part, :]
@@ -178,30 +176,45 @@
             d_out, cast_out, (((1,), (1,)), ((), ())), preferred_element_type=F32
         )
         dpre[part, :] = (d_hidden * (cdf + preact * pdf)).astype(BF16)
-    over_rows = (((0,), (0,)), ((), ()))
-    grad = lax.dot_general(hid[...], dout[...], over_rows, preferred_element_type=F32)
-    moment = (MOMENTUM * mout[...].astype(F32) + grad).astype(BF16)
+
+
+OVER_ROWS = (((0,), (0,)), ((), ()))
+
+
+def momentum_in(x_ref, dpre, moment):
+    grad = lax.dot_general(x_ref[...], dpre[...], OVER_ROWS, preferred_element_type=F32)
+    return (MOMENTUM * moment[...].astype(F32) + grad).astype(BF16)
+
+
+def momentum_out(hid, dout, moment):
+    grad = lax.dot_general(hid[...], dout[...], OVER_ROWS, preferred_element_type=F32)
+    return (MOMENTUM * moment[...].astype(F32) + grad).astype(BF16)
+
+
+def stepped(weight, moment):
+    return weight - LEARN_RATE * moment.astype(F32)
+
+
+def train_step(x_ref, y_ref, win, wout, min_, mout, hid, dout, dpre, block):
+    cast_in, cast_out = win[...].astype(BF16), wout[...].astype(BF16)
+    gradients(x_ref, y_ref, cast_in, cast_out, hid, dout, dpre, block)
+    moment = momentum_out(hid, dout, mout)
     mout[...] = moment
-    wout[...] = wout[...] - LEARN_RATE * moment.astype(F32)
-    grad = lax.dot_general(x_ref[...], dpre[...], over_rows, preferred_element_type=F32)
-    moment = (MOMENTUM * min_[...].astype(F32) + grad).astype(BF16)
+    wout[...] = stepped(wout[...], moment)
+    moment = momentum_in(x_ref, dpre, min_)
     min_[...] = moment
-    win[...] = win[...] - LEARN_RATE * moment.astype(F32)
-
-
-def send_out(slots, pieces, me_ref, state, refs, packed, sems):
-    weights_ref, moment_refs = refs[0], refs[1:]
-    pack(state[2:], slots[pieces], packed)
-    copies = scatter(me_ref, packed, moment_refs, sems)
-    for copy in copies:
-        copy.start()
-    pack(state[:2], slots[2 * pieces], weights_ref)
-    for copy in copies:
-        copy.wait()
+    win[...] = stepped(win[...], moment)
+
+
+def hand_over(slots, pieces, state, sent):
+    packed, kept = sent[0], sent[1:5]
+    pack(state[:2], slots[2 * pieces], packed)
+    for ref, held in zip(kept, state):
+        ref[...] = held[...].astype(BF16)
 
 
 def later_visit_kernel(slots, pieces, block, me_ref, x_ref, y_ref, weights_ref, *refs):
-    moment_refs, sent, scratch = refs[:pieces], refs[pieces:][: pieces + 1], refs[2 * pieces + 1 :]
+    moment_refs, sent, scratch = refs[:pieces], refs[pieces:][:5], refs[pieces + 5 :]
     state, work, (packed, sems) = scratch[:4], scratch[4:7], scratch[7:9]
     step = pl.program_id(0)
 
@@ -214,19 +227,20 @@
         for copy in copies:
             copy.wait()
         unpack(packed, slots[pieces], state[2:])
+        for weight, moment in zip(state[:2], state[2:]):
+            weight[...] = stepped(weight[...], moment[...])
 
     train_step(x_ref, y_ref, *state, *work, block)
 
     @pl.when(step == pl.num_programs(0) - 1)
     def _():
-        send_out(slots, pieces, me_ref, state, sent, packed, sems)
-
-
-def first_visit_kernel(slots, pieces, block, me_ref, picks_ref, x_ref, y_ref, *refs):
-    model, sent, scratch = refs[:4], refs[4:][: pieces + 1], refs[pieces + 5 :]
-    state, work, (packed, packed_sems) = scratch[:4], scratch[4:7], scratch[7:9]
-    batch = scratch[9:11]
-    held, table, picked, sems, model_sems = scratch[11:]
+        hand_over(slots, pieces, state, sent)
+
+
+def first_visit_kernel(slots, pieces, block, picks_ref, x_ref, y_ref, *refs):
+    model, sent, scratch = refs[:4], refs[4:11], refs[11:]
+    state, work, batch = scratch[:4], scratch[4:7], scratch[7:9]
+    held, table, picked, sems, model_sems = scratch[9:]
     step = pl.program_id(0)
 
     @pl.when(step == 0)
@@ -247,7 +261,22 @@
 
     @pl.when(step == pl.num_programs(0) - 1)
     def _():
-        send_out(slots, pieces, me_ref, state, sent, packed, packed_sems)
+        hand_over(slots, pieces, state, sent)
+        pick_rows(picks_ref, step + 1, 0, table, picked, sent[5:], 0)
+
+
+def last_step_kernel(slots, pieces, block, me_ref, x_ref, y_ref, *refs):
+    cast_in, cast_out, min_, mout = refs[:4]
+    moment_refs, (hid, dout, dpre, new_in, new_out, packed, sems) = refs[4:-7], refs[-7:]
+    gradients(x_ref, y_ref, cast_in[...], cast_out[...], hid, dout, dpre, block)
+    new_out[...] = momentum_out(hid, dout, mout)
+    new_in[...] = momentum_in(x_ref, dpre, min_)
+    pack((new_in, new_out), slots[pieces], packed)
+    copies = scatter(me_ref, packed, moment_refs, sems)
+    for copy in copies:
+        copy.start()
+    for copy in copies:
+        copy.wait()
 
 
 def whole(shape):
@@ -258,68 +287,106 @@
 ANYWHERE = pl.BlockSpec(memory_space=pl.ANY)
 
 
-def visit(kernel, args, in_specs, more_scratch, limit, sizes, slots):
+def work_scratch(rows, width, hidden):
+    return [
+        pltpu.VMEM((rows, hidden), BF16),
+        pltpu.VMEM((rows, width), BF16),
+        pltpu.VMEM((rows, hidden), BF16),
+    ]
+
+
+def step_cost(steps, rows, width, hidden):
+    return pl.CostEstimate(
+        flops=steps * 10 * rows * width * hidden,
+        bytes_accessed=4 * steps * rows * width + 16 * width * hidden,
+        transcendentals=2 * steps * rows * hidden,
+    )
+
+
+def visit(kernel, args, in_specs, more_outs, more_scratch, limit, sizes, slots):
     steps, rows, width, hidden = sizes
     pieces = min(slots)
     depth = 2 * width * hidden // (SUB * LANE)
-    piece_shape = (depth // pieces, SUB, LANE)
     packed_shape = (2 * pieces, depth // (2 * pieces), SUB, LANE)
-    outs = pl.pallas_call(
+    shapes = [packed_shape] + [(width, hidden), (hidden, width)] * 2 + more_outs
+    return pl.pallas_call(
         functools.partial(kernel, slots, pieces, rows // 4),
-        grid=(steps,),
+        grid=(steps - 1,),
         in_specs=in_specs,
-        out_specs=[whole(packed_shape)] + [ANYWHERE] * pieces,
-        out_shape=[jax.ShapeDtypeStruct(packed_shape, BF16)]
-        + [jax.ShapeDtypeStruct(piece_shape, BF16)] * pieces,
+        out_specs=[whole(shape) for shape in shapes],
+        out_shape=[jax.ShapeDtypeStruct(shape, BF16) for shape in shapes],
         scratch_shapes=[
             pltpu.VMEM((width, hidden), F32),
             pltpu.VMEM((hidden, width), F32),
             pltpu.VMEM((width, hidden), BF16),
             pltpu.VMEM((hidden, width), BF16),
-            pltpu.VMEM((rows, hidden), BF16),
-            pltpu.VMEM((rows, width), BF16),
-            pltpu.VMEM((rows, hidden), BF16),
-            pltpu.VMEM((pieces, *piece_shape), BF16),
-            pltpu.SemaphoreType.DMA((pieces,)),
+            *work_scratch(rows, width, hidden),
             *more_scratch,
         ],
-        cost_estimate=pl.CostEstimate(
-            flops=steps * 10 * rows * width * hidden,
-            bytes_accessed=4 * steps * rows * width + 32 * width * hidden,
-            transcendentals=2 * steps * rows * hidden,
-        ),
+        cost_estimate=step_cost(steps - 1, rows, width, hidden),
         compiler_params=pltpu.CompilerParams(vmem_limit_bytes=limit * MIB),
         name="visit",
     )(*args)
-    return outs[0], outs[1:]
-
-
-def first_visit(me, features, targets, picks, model, sizes, slots):
+
+
+def first_visit(features, targets, picks, model, sizes, slots):
     _, rows, width, _ = sizes
     scratch = [pltpu.VMEM((rows, width), BF16)] * 2 + table_scratch(features, rows)
-    return visit(
+    outs = visit(
         first_visit_kernel,
-        (me, picks, features, targets, *model),
-        [SCALARS] * 2 + [ANYWHERE] * 6,
+        (picks, features, targets, *model),
+        [SCALARS] + [ANYWHERE] * 6,
+        [(rows, width)] * 2,
         scratch + [pltpu.SemaphoreType.DMA((4,))],
         FIRST_MIB,
         sizes,
         slots,
     )
+    return outs[0], outs[1:5], outs[5:]
+
+
+def piece_scratch(pieces, piece_shape):
+    return [pltpu.VMEM((pieces, *piece_shape), BF16), pltpu.SemaphoreType.DMA((pieces,))]
 
 
 def later_visit(me, batch, weights, moments, sizes, slots):
     _, rows, width, _ = sizes
     batch_spec = pl.BlockSpec((rows, width), lambda step: (step, 0))
-    return visit(
+    outs = visit(
         later_visit_kernel,
         (me, *batch, weights, *moments),
         [SCALARS, batch_spec, batch_spec, whole(weights.shape)] + [ANYWHERE] * len(moments),
         [],
+        piece_scratch(len(moments), moments[0].shape),
         LATER_MIB,
         sizes,
         slots,
     )
+    return outs[0], outs[1:]
+
+
+def last_step(me, batch, kept, sizes, slots):
+    _, rows, width, hidden = sizes
+    pieces = min(slots)
+    piece_shape = (2 * width * hidden // (SUB * LANE) // pieces, SUB, LANE)
+    last = batch[0].shape[0] // rows - 1
+    batch_spec = pl.BlockSpec((rows, width), lambda step: (last, 0))
+    return pl.pallas_call(
+        functools.partial(last_step_kernel, slots, pieces, rows // 4),
+        grid=(1,),
+        in_specs=[SCALARS, batch_spec, batch_spec] + [whole(part.shape) for part in kept],
+        out_specs=[ANYWHERE] * pieces,
+        out_shape=[jax.ShapeDtypeStruct(piece_shape, BF16)] * pieces,
+        scratch_shapes=[
+            *work_scratch(rows, width, hidden),
+            pltpu.VMEM((width, hidden), BF16),
+            pltpu.VMEM((hidden, width), BF16),
+            *piece_scratch(pieces, piece_shape),
+        ],
+        cost_estimate=step_cost(1, rows, width, hidden),
+        compiler_params=pltpu.CompilerParams(vmem_limit_bytes=LAST_MIB * MIB),
+        name="last",
+    )(me, *batch, *kept)
 
 
 def reorder_kernel(source_ref, packed_ref, out_ref, sems):
@@ -348,23 +415,6 @@
     )(source, packed)
 
 
-def unpack_blocks(packed, outs, devices):
-    blocks = UNPACK_BLOCKS if devices % UNPACK_BLOCKS == 0 else 1
-    parts = [(shape[0] // blocks, shape[1]) for shape, _ in outs]
-    slots, _ = tile_slots(parts, devices // blocks)
-    return pl.pallas_call(
-        functools.partial(unpack_kernel, slots),
-        grid=(blocks,),
-        in_specs=[
-            pl.BlockSpec((devices // blocks, *packed.shape[1:]), lambda block: (block, 0, 0, 0))
-        ],
-        out_specs=[pl.BlockSpec(part, lambda block: (block, 0)) for part in parts],
-        out_shape=[jax.ShapeDtypeStruct(shape, dtype) for shape, dtype in outs],
-        compiler_params=pltpu.CompilerParams(vmem_limit_bytes=16 * MIB),
-        name="unpack",
-    )(packed)
-
-
 def stack_kernel(*refs):
     parts, out_ref, sems = refs[:-2], refs[-2], refs[-1]
     copies = [
@@ -425,34 +475,30 @@
     )(me, source, own, partner)
 
 
-def unpack_pieces_kernel(slots, pieces, me_ref, *refs):
-    given, outs, (packed, sems) = refs[:pieces], refs[pieces:-2], refs[-2:]
-    copies = collect(me_ref, given, packed, sems)
+def settle_kernel(slots, pieces, me_ref, weights_ref, *refs):
+    moment_refs, outs, (packed, sems) = refs[:pieces], refs[pieces:-2], refs[-2:]
+    copies = collect(me_ref, moment_refs, packed, sems)
     for copy in copies:
         copy.start()
+    unpack(weights_ref, slots[2 * pieces], outs[:2])
     for copy in copies:
         copy.wait()
-    unpack(packed, slots, outs)
-
-
-def unpack_pieces(me, given, slots, outs):
-    pieces = len(given)
-    return pl.pallas_call(
-        functools.partial(unpack_pieces_kernel, slots, pieces),
-        in_specs=[SCALARS] + [ANYWHERE] * pieces,
-        out_specs=[pl.BlockSpec(memory_space=pltpu.VMEM)] * len(outs),
+    unpack(packed, slots[pieces], outs[2:])
+    for weight, moment in zip(outs[:2], outs[2:]):
+        weight[...] = stepped(weight[...], moment[...])
+
+
+def settle(me, weights, moments, slots, outs):
+    in_vmem = pl.BlockSpec(memory_space=pltpu.VMEM)
+    return pl.pallas_call(
+        functools.partial(settle_kernel, slots, len(moments)),
+        in_specs=[SCALARS, in_vmem] + [ANYWHERE] * len(moments),
+        out_specs=[in_vmem] * len(outs),
         out_shape=[jax.ShapeDtypeStruct(shape, dtype) for shape, dtype in outs],
-        scratch_shapes=[
-            pltpu.VMEM((pieces, *given[0].shape), BF16),
-            pltpu.SemaphoreType.DMA((pieces,)),
-        ],
-        compiler_params=pltpu.CompilerParams(vmem_limit_bytes=16 * MIB),
-        name="unpack",
-    )(me, *given)
-
-
-def unpack_kernel(slots, packed_ref, *out_refs):
-    unpack(packed_ref, slots, out_refs)
+        scratch_shapes=piece_scratch(len(moments), moments[0].shape),
+        compiler_params=pltpu.CompilerParams(vmem_limit_bytes=SETTLE_MIB * MIB),
+        name="settle",
+    )(me, weights, *moments)
 
 
 def invert(order):
@@ -474,18 +520,17 @@
     return moved
 
 
-def move(weights, moments, me, source, devices, beside=()):
+def move(weights, me, batch, kept, source, devices, sizes, slots):
     weights = exchange(weights)
+    moments = last_step(me, batch, kept, sizes, slots)
     moments = spread(moments, devices)
-    if beside:
-        weights, *beside = lax.optimization_barrier((weights, *beside))
     weights = reorder(weights, source)
     weights = exchange(weights)
     own = stacked(moments)
     partner = lax.ppermute(own, "hop", [(i, i ^ 1) for i in range(devices)])
     moments = route(me, source, own, partner)
     moments = spread(moments, devices)
-    return weights, moments, beside
+    return weights, moments
 
 
 def on_device(
@@ -496,23 +541,22 @@
     model = (weight_in[0], weight_out[0], moment_in[0], moment_out[0])
     outs = [(member.shape, member.dtype) for member in model]
     shapes = [member.shape for member in model[:2]]
-    pieces = devices // 2
-    slots = {count: tile_slots(shapes, count)[0] for count in (pieces, devices)}
+    slots = {count: tile_slots(shapes, count)[0] for count in (devices // 2, devices)}
     _, visits, steps, rows = row_index.shape
     sizes = (steps, rows, *shapes[0])
     picks = jnp.transpose(row_index, (0, 2, 1, 3))
     sources = [invert(hop_order[visit_index]) for visit_index in range(visits)]
-    weights, moments = first_visit(me, features, targets, picks, model, sizes, slots)
-    for visit_index in range(1, visits):
-        batch = fetch(features, targets, picks, visit_index)
-        weights, moments, batch = move(
-            weights, moments, me, sources[visit_index - 1], devices, batch
+    weights, kept, batch = first_visit(features, targets, picks, model, sizes, slots)
+    for visit_index in range(visits):
+        weights, moments = move(
+            weights, me, batch, kept, sources[visit_index], devices, sizes, slots
         )
-        weights, moments = later_visit(me, batch, weights, moments, sizes, slots)
-    weights, moments, _ = move(weights, moments, me, sources[-1], devices)
-    weights = unpack_blocks(weights, outs[:2], devices)
-    moments = unpack_pieces(me, moments, slots[pieces], outs[2:])
-    return tuple(member[None] for member in (*weights, *moments))
+        if visit_index + 1 < visits:
+            batch = fetch(features, targets, picks, visit_index + 1)
+        if visit_index + 1 < visits:
+            weights, kept = later_visit(me, batch, weights, moments, sizes, slots)
+    results = settle(me, weights, moments, slots, outs)
+    return tuple(member[None] for member in results)
 
 
 def solution(mesh):

time: 237 us -> 229 us (0.966)
  local copies, waits for them, and re-layouts: 14.8 us -> 3.37 us
  Pallas kernels: 52 us -> 56.9 us
  starting transfers between devices: 79.4 us -> 76.7 us
    unnamed x62 -> x24, local copies, waits for them, and re-layouts: 14.8 us -> 3.37 us
    all_to_all x4, waiting for transfers between devices: 26.8 us -> 37 us  [exchange(): lax.all_to_all(packed, 'hop', split_axis=0, concat_axis=0, tiled=True)]
    pallas_call x2 -> x3, Pallas kernels: 3.68 us -> 13 us  [the longest x2 10.2 us: last_step(): pl.pallas_call(functools.partial(last_step_kernel, slots, pieces, rows //...]
    ppermute x28, waiting for transfers between devices: 55.7 us -> 46.7 us  [spread(): lax.ppermute(parts[k], 'hop', [(i, i ^ 2 * k) for i in range(devices)])]
    pallas_call x2, Pallas kernels: 29.2 us -> 25.1 us  [visit(): pl.pallas_call(functools.partial(kernel, slots, pieces, rows // 4), grid=...]
  transfers between devices with their start and end apart: 34 -> 34, of which waited for: 17 -> 17; matrix products, arithmetic and copies ran while one was open for 0% -> 0% of each run, Pallas kernels for 8% -> 11%
where the time goes in v6:
time: 229 us; the launch traced here: 226 us
  waiting for transfers between devices  87.6 us (38%)
  starting transfers between devices  76.7 us (33%)
  Pallas kernels  56.9 us (25%)
  local copies, waits for them, and re-layouts  3.37 us (1%)
    ppermute x28, starting transfers between devices, spread(): lax.ppermute(parts[k], 'hop', [(i, i ^ 2 * k) for i in range(devices)])  48.8 us
    ppermute x28, waiting for transfers between devices, spread(): lax.ppermute(parts[k], 'hop', [(i, i ^ 2 * k) for i in range(devices)])  46.7 us
    all_to_all x4, waiting for transfers between devices, exchange(): lax.all_to_all(packed, 'hop', split_axis=0, concat_axis=0, tiled=True)  37 us
    pallas_call x2, Pallas kernels, visit(): pl.pallas_call(functools.partial(kernel, slots, pieces, rows // 4), grid=...  25.1 us
    all_to_all x4, starting transfers between devices, exchange(): lax.all_to_all(packed, 'hop', split_axis=0, concat_axis=0, tiled=True)  24.6 us
    pallas_call x2, Pallas kernels, last_step(): pl.pallas_call(functools.partial(last_step_kernel, slots, pieces, rows //...  10.2 us
    pallas_call x1, Pallas kernels, fetch(): pl.pallas_call(functools.partial(fetch_kernel, visit_index), in_specs=[SC...  9.83 us
  transfers between devices with their start and end apart: 34, of which 17 were waited for; matrix products, arithmetic and copies ran while one was open for 0% of the time, Pallas kernels for 11%

profile of v6, /device:TPU:1, one launch (start us, length us, event | category | flops | bytes accessed | tf_op | source)
XLA Modules:
  0.0 225.7 jit_solution(10113280781706305716)
XLA Ops:
  0.6 15.5 %visit.2 = (bf16[16,24,8,128]{3,2,1,0:T(8,128)(2,1)}, bf16[384,512]{1,0:T(8,128)(2,1)}, bf16[512,384]{1,0:T(8,128)(2,1)}, bf16[384,512]{1,0:T(8,128)(2,1)}, bf16...) custom-call(s32[1,3,2,512]{3,2,1,0:T(2,128)} %bitcast.18, bf16[4096,384]{1,0:T(8,128)(2,1)} %x_ref.3, ...), custom_call_target="tpu_custom_call" | custom-call | flops 2013265920 | bytes 4718592 | tf_op jit(solution)/shard_map/visit/pallas_call | solution.py:312
  16.1 7.4 %all-to-all-start = ((bf16[16,24,8,128]{3,2,1,0:T(8,128)(2,1)}), bf16[16,24,8,128]{3,2,1,0:T(8,128)(2,1)S(1)}, u32[]{:S(2)}, u32[]{:S(2)}) async-start(bf16[16,24,8,128]{3,2,1,0:T(8,128)(2,1)} %get-tuple-element.56), calls=%async_computation | async-start | bytes 1572864 | tf_op jit(solution)/shard_map/all_to_all | solution.py:512
  23.6 18.5 %all-to-all-done.packed_ref = bf16[16,24,8,128]{3,2,1,0:T(8,128)(2,1)S(1)} async-done(((bf16[16,24,8,128]{3,2,1,0:T(8,128)(2,1)}), bf16[16,24,8,128]{3,2,1,0:T(8,128)(2,1)S(1)}, u32[]{:S(2)}, u32[]{:S(2)}) %all-to-all-start) | async-done | bytes 786464 | tf_op jit(solution)/shard_map/all_to_all | solution.py:512
  42.1 1.5 reorder.2
  43.6 5.5 %all-to-all-start.1 = ((bf16[16,24,8,128]{3,2,1,0:T(8,128)(2,1)}), bf16[16,24,8,128]{3,2,1,0:T(8,128)(2,1)S(1)}, u32[]{:S(2)}, u32[]{:S(2)}) async-start(bf16[16,24,8,128]{3,2,1,0:T(8,128)(2,1)} %reorder.2), calls=%async_computation.1 | async-start | bytes 1572864 | tf_op jit(solution)/shard_map/all_to_all | solution.py:512
  49.1 5.1 %last.2 = (bf16[48,8,128]{2,1,0:T(8,128)(2,1)}, bf16[48,8,128]{2,1,0:T(8,128)(2,1)}, bf16[48,8,128]{2,1,0:T(8,128)(2,1)}, bf16[48,8,128]{2,1,0:T(8,128)(2,1)}, b...) custom-call(s32[1]{0:T(128)} %bitcast.me_ref, ...), custom_call_target="tpu_custom_call" | custom-call | flops 1006632960 | bytes 3932160 | tf_op jit(solution)/shard_map/last/pallas_call | solution.py:374
  54.2 1.4 collective-permute-start
  55.6 1.2 collective-permute-start.1
  56.9 2.3 collective-permute-start.3
  59.2 1.2 collective-permute-start.4
  60.5 2.9 %collective-permute-start.5 = (bf16[48,8,128]{2,1,0:T(8,128)(2,1)}, bf16[48,8,128]{2,1,0:T(8,128)(2,1)S(1)}, u32[]{:S(2)}, u32[]{:S(2)}) collective-permute-start(bf16[48,8,128]{2,1,0:T(8,128)(2,1)} %get-tuple-element.69), channel_id=1, source_target_pairs={{0,12},{1,13},{2,14},{3,15},{4,8},{5,9},{6,10},{7,11},{8,4},{9,5},... | collective-permute-start | bytes 294920 | tf_op jit(solution)/shard_map/ppermute | solution.py:519
  63.4 1.2 collective-permute-done.1.refs_2_
  64.5 3.7 %collective-permute-start.6 = (bf16[48,8,128]{2,1,0:T(8,128)(2,1)}, bf16[48,8,128]{2,1,0:T(8,128)(2,1)S(1)}, u32[]{:S(2)}, u32[]{:S(2)}) collective-permute-start(bf16[48,8,128]{2,1,0:T(8,128)(2,1)} %get-tuple-element.70), channel_id=1, source_target_pairs={{0,14},{1,15},{2,12},{3,13},{4,10},{5,11},{6,8},{7,9},{8,6},{9,7},... | collective-permute-start | bytes 294920 | tf_op jit(solution)/shard_map/ppermute | solution.py:519
  69.1 10.6 %collective-permute-done.3.refs_4_ = bf16[48,8,128]{2,1,0:T(8,128)(2,1)S(1)} collective-permute-done((bf16[48,8,128]{2,1,0:T(8,128)(2,1)}, bf16[48,8,128]{2,1,0:T(8,128)(2,1)S(1)}, u32[]{:S(2)}, u32[]{:S(2)}) %collective-permute-start.3) | collective-permute-done | bytes 98336 | tf_op jit(solution)/shard_map/ppermute | solution.py:519
  79.7 3.0 %collective-permute-done.4.refs_5_ = bf16[48,8,128]{2,1,0:T(8,128)(2,1)S(1)} collective-permute-done((bf16[48,8,128]{2,1,0:T(8,128)(2,1)}, bf16[48,8,128]{2,1,0:T(8,128)(2,1)S(1)}, u32[]{:S(2)}, u32[]{:S(2)}) %collective-permute-start.4) | collective-permute-done | bytes 98336 | tf_op jit(solution)/shard_map/ppermute | solution.py:519
  84.6 1.6 collective-permute-start.7
  86.2 1.9 collective-permute-done.7.partner_ref
  88.1 2.0 route.2
  90.8 4.0 %collective-permute-start.10 = (bf16[48,8,128]{2,1,0:T(8,128)(2,1)S(1)}, bf16[48,8,128]{2,1,0:T(8,128)(2,1)S(1)}, u32[]{:S(2)}, u32[]{:S(2)}) collective-permute-start(bf16[48,8,128]{2,1,0:T(8,128)(2,1)S(1)} %get-tuple-element.74), channel_id=1, source_target_pairs={{0,6},{1,7},{2,4},{3,5},{4,2},{5,3},{6,0},{7,1},{8,14},{9,15},{10,... | collective-permute-start | bytes 294920 | tf_op jit(solution)/shard_map/ppermute | solution.py:519
  94.8 3.2 %collective-permute-start.12 = (bf16[48,8,128]{2,1,0:T(8,128)(2,1)S(1)}, bf16[48,8,128]{2,1,0:T(8,128)(2,1)S(1)}, u32[]{:S(2)}, u32[]{:S(2)}) collective-permute-start(bf16[48,8,128]{2,1,0:T(8,128)(2,1)S(1)} %get-tuple-element.76), channel_id=1, source_target_pairs={{0,10},{1,11},{2,8},{3,9},{4,14},{5,15},{6,12},{7,13},{8,2},{9,3},... | collective-permute-start | bytes 294920 | tf_op jit(solution)/shard_map/ppermute | solution.py:519
  97.9 1.3 collective-permute-start.13
  99.2 2.0 collective-permute-start.14
  102.4 5.9 %collective-permute-done.11.refs_4_ = bf16[48,8,128]{2,1,0:T(8,128)(2,1)S(1)} collective-permute-done((bf16[48,8,128]{2,1,0:T(8,128)(2,1)S(1)}, bf16[48,8,128]{2,1,0:T(8,128)(2,1)S(1)}, u32[]{:S(2)}, u32[]{:S(2)}) %collective-permute-start.11) | collective-permute-done | bytes 98336 | tf_op jit(solution)/shard_map/ppermute | solution.py:519
  108.3 9.8 %fetch.1 = (bf16[1536,384]{1,0:T(8,128)(2,1)}, bf16[1536,384]{1,0:T(8,128)(2,1)}) custom-call(s32[1,3,2,512]{3,2,1,0:T(2,128)} %bitcast.19, bf16[4096,384]{1,0:T(8,128)(2,1)} %x_ref.3, bf16[4096,384]{1,0:T(8,128)(2,1)} %y_ref.3), custom_call_target="tpu_custom_call" | custom-call | bytes 6291456 | tf_op jit(solution)/shard_map/fetch/pallas_call | solution.py:93
  119.2 9.6 %visit.3 = (bf16[16,24,8,128]{3,2,1,0:T(8,128)(2,1)}, bf16[384,512]{1,0:T(8,128)(2,1)}, bf16[512,384]{1,0:T(8,128)(2,1)}, bf16[384,512]{1,0:T(8,128)(2,1)}, bf16[512,384]{1,0:T(8,128)(2,1)}) custom-call(s32[1]{0:T(128)} %bitcast.me_ref, bf16[1536,384]{1,0:T(8,128)(2,1)} %get-tuple-element.54.x_ref, bf16[1536,384]{1,0:T(8,128)(2,1)} %get-tuple-element.55.y_ref, ...), custom_call_target="tpu_custom_call" | custom-call | flops 2013265920 | bytes 4718592 | tf_op jit(solution)/shard_map/visit/pallas_call | solution.py:312
  128.8 6.4 %all-to-all-start.2 = ((bf16[16,24,8,128]{3,2,1,0:T(8,128)(2,1)}), bf16[16,24,8,128]{3,2,1,0:T(8,128)(2,1)S(1)}, u32[]{:S(2)}, u32[]{:S(2)}) async-start(bf16[16,24,8,128]{3,2,1,0:T(8,128)(2,1)} %get-tuple-element.79), calls=%async_computation.2 | async-start | bytes 1572864 | tf_op jit(solution)/shard_map/all_to_all | solution.py:512
  135.2 18.5 %all-to-all-done.2.packed_ref = bf16[16,24,8,128]{3,2,1,0:T(8,128)(2,1)S(1)} async-done(((bf16[16,24,8,128]{3,2,1,0:T(8,128)(2,1)}), bf16[16,24,8,128]{3,2,1,0:T(8,128)(2,1)S(1)}, u32[]{:S(2)}, u32[]{:S(2)}) %all-to-all-start.2) | async-done | bytes 786464 | tf_op jit(solution)/shard_map/all_to_all | solution.py:512
  153.8 1.5 reorder.3
  155.3 5.5 %all-to-all-start.3 = ((bf16[16,24,8,128]{3,2,1,0:T(8,128)(2,1)}), bf16[16,24,8,128]{3,2,1,0:T(8,128)(2,1)S(1)}, u32[]{:S(2)}, u32[]{:S(2)}) async-start(bf16[16,24,8,128]{3,2,1,0:T(8,128)(2,1)} %reorder.3), calls=%async_computation.3 | async-start | bytes 1572864 | tf_op jit(solution)/shard_map/all_to_all | solution.py:512
  160.8 5.1 %last.3 = (bf16[48,8,128]{2,1,0:T(8,128)(2,1)}, bf16[48,8,128]{2,1,0:T(8,128)(2,1)}, bf16[48,8,128]{2,1,0:T(8,128)(2,1)}, bf16[48,8,128]{2,1,0:T(8,128)(2,1)}, b...) custom-call(s32[1]{0:T(128)} %bitcast.me_ref, ...), custom_call_target="tpu_custom_call" | custom-call | flops 1006632960 | bytes 3932160 | tf_op jit(solution)/shard_map/last/pallas_call | solution.py:374
  165.9 1.4 collective-permute-start.15
  167.3 1.2 collective-permute-start.16
  168.6 2.3 collective-permute-start.18
  170.8 1.2 collective-permute-start.19
  172.1 2.9 %collective-permute-start.20 = (bf16[48,8,128]{2,1,0:T(8,128)(2,1)}, bf16[48,8,128]{2,1,0:T(8,128)(2,1)S(1)}, u32[]{:S(2)}, u32[]{:S(2)}) collective-permute-start(bf16[48,8,128]{2,1,0:T(8,128)(2,1)} %get-tuple-element.90), channel_id=1, source_target_pairs={{0,12},{1,13},{2,14},{3,15},{4,8},{5,9},{6,10},{7,11},{8,4},{9,5},... | collective-permute-start | bytes 294920 | tf_op jit(solution)/shard_map/ppermute | solution.py:519
  175.0 1.2 collective-permute-done.16.refs_2_
  176.2 3.7 %collective-permute-start.21 = (bf16[48,8,128]{2,1,0:T(8,128)(2,1)}, bf16[48,8,128]{2,1,0:T(8,128)(2,1)S(1)}, u32[]{:S(2)}, u32[]{:S(2)}) collective-permute-start(bf16[48,8,128]{2,1,0:T(8,128)(2,1)} %get-tuple-element.91), channel_id=1, source_target_pairs={{0,14},{1,15},{2,12},{3,13},{4,10},{5,11},{6,8},{7,9},{8,6},{9,7},... | collective-permute-start | bytes 294920 | tf_op jit(solution)/shard_map/ppermute | solution.py:519
  180.8 10.6 %collective-permute-done.18.refs_4_ = bf16[48,8,128]{2,1,0:T(8,128)(2,1)S(1)} collective-permute-done((bf16[48,8,128]{2,1,0:T(8,128)(2,1)}, bf16[48,8,128]{2,1,0:T(8,128)(2,1)S(1)}, u32[]{:S(2)}, u32[]{:S(2)}) %collective-permute-start.18) | collective-permute-done | bytes 98336 | tf_op jit(solution)/shard_map/ppermute | solution.py:519
  191.4 3.0 %collective-permute-done.19.refs_5_ = bf16[48,8,128]{2,1,0:T(8,128)(2,1)S(1)} collective-permute-done((bf16[48,8,128]{2,1,0:T(8,128)(2,1)}, bf16[48,8,128]{2,1,0:T(8,128)(2,1)S(1)}, u32[]{:S(2)}, u32[]{:S(2)}) %collective-permute-start.19) | collective-permute-done | bytes 98336 | tf_op jit(solution)/shard_map/ppermute | solution.py:519
  196.3 1.6 collective-permute-start.22
  197.9 1.9 collective-permute-done.22.partner_ref
  199.8 1.8 route.3
  202.0 3.9 %collective-permute-start.24 = (bf16[48,8,128]{2,1,0:T(8,128)(2,1)S(1)}, bf16[48,8,128]{2,1,0:T(8,128)(2,1)S(1)}, u32[]{:S(2)}, u32[]{:S(2)}) collective-permute-start(bf16[48,8,128]{2,1,0:T(8,128)(2,1)S(1)} %get-tuple-element.94), channel_id=1, source_target_pairs={{0,4},{1,5},{2,6},{3,7},{4,0},{5,1},{6,2},{7,3},{8,12},{9,13},{10,... | collective-permute-start | bytes 294920 | tf_op jit(solution)/shard_map/ppermute | solution.py:519
  206.8 1.5 collective-permute-start.26
  209.2 1.2 collective-permute-start.28
  210.4 2.9 %collective-permute-start.29 = (bf16[48,8,128]{2,1,0:T(8,128)(2,1)S(1)}, bf16[48,8,128]{2,1,0:T(8,128)(2,1)S(1)}, u32[]{:S(2)}, u32[]{:S(2)}) collective-permute-start(bf16[48,8,128]{2,1,0:T(8,128)(2,1)S(1)} %get-tuple-element.99), channel_id=1, source_target_pairs={{0,14},{1,15},{2,12},{3,13},{4,10},{5,11},{6,8},{7,9},{8,6},{9,7},... | collective-permute-start | bytes 294920 | tf_op jit(solution)/shard_map/ppermute | solution.py:519
  214.1 8.6 %collective-permute-done.27.refs_5_ = bf16[48,8,128]{2,1,0:T(8,128)(2,1)S(1)} collective-permute-done((bf16[48,8,128]{2,1,0:T(8,128)(2,1)S(1)}, bf16[48,8,128]{2,1,0:T(8,128)(2,1)S(1)}, u32[]{:S(2)}, u32[]{:S(2)}) %collective-permute-start.27) | collective-permute-done | bytes 98336 | tf_op jit(solution)/shard_map/ppermute | solution.py:519
  222.7 2.8 %settle.1 = (f32[384,512]{1,0:T(8,128)}, f32[512,384]{1,0:T(8,128)}, bf16[384,512]{1,0:T(8,128)(2,1)}, bf16[512,384]{1,0:T(8,128)(2,1)}) custom-call(s32[1]{0:T(128)} %bitcast.me_ref, bf16[16,24,8,128]{3,2,1,0:T(8,128)(2,1)S(1)} %all-to-all-done.3.weights_ref, bf16[48,8,128]{2,1,0:T(8,128)(2,1)S(1)} %get-tuple-element.92.refs_0_, ...), custom_call_target="tpu_custom_call" | custom-call | tf_op jit(solution)/shard_map/settle/pallas_call | solution.py:493
  (59 shorter events, 11.8 us)
Async XLA Ops:
  0.6 22.8 %copy-start.4 = (s32[2,16]{1,0:T(2,128)S(1)}, s32[2,16]{1,0:T(2,128)}, u32[]{:S(2)}) copy-start(s32[2,16]{1,0:T(2,128)} %param.11) | copy-start | bytes 388
  16.1 26.0 %all-to-all-start = ((bf16[16,24,8,128]{3,2,1,0:T(8,128)(2,1)}), bf16[16,24,8,128]{3,2,1,0:T(8,128)(2,1)S(1)}, u32[]{:S(2)}, u32[]{:S(2)}) async-start(bf16[16,24,8,128]{3,2,1,0:T(8,128)(2,1)} %get-tuple-element.56), calls=%async_computation | async-start | bytes 1572864 | tf_op jit(solution)/shard_map/all_to_all | solution.py:512
  43.6 74.6 %all-to-all-start.1 = ((bf16[16,24,8,128]{3,2,1,0:T(8,128)(2,1)}), bf16[16,24,8,128]{3,2,1,0:T(8,128)(2,1)S(1)}, u32[]{:S(2)}, u32[]{:S(2)}) async-start(bf16[16,24,8,128]{3,2,1,0:T(8,128)(2,1)} %reorder.2), calls=%async_computation.1 | async-start | bytes 1572864 | tf_op jit(solution)/shard_map/all_to_all | solution.py:512
  54.2 6.2 %collective-permute-start = (bf16[48,8,128]{2,1,0:T(8,128)(2,1)}, bf16[48,8,128]{2,1,0:T(8,128)(2,1)S(1)}, u32[]{:S(2)}, u32[]{:S(2)}) collective-permute-start(bf16[48,8,128]{2,1,0:T(8,128)(2,1)} %get-tuple-element.64), channel_id=1, source_target_pairs={{0,2},{1,3},{2,0},{3,1},{4,6},{5,7},{6,4},{7,5},{8,10},{9,11},{10,... | collective-permute-start | bytes 294920 | tf_op jit(solution)/shard_map/ppermute | solution.py:519
  55.6 8.9 %collective-permute-start.1 = (bf16[48,8,128]{2,1,0:T(8,128)(2,1)}, bf16[48,8,128]{2,1,0:T(8,128)(2,1)S(1)}, u32[]{:S(2)}, u32[]{:S(2)}) collective-permute-start(bf16[48,8,128]{2,1,0:T(8,128)(2,1)} %get-tuple-element.65), channel_id=1, source_target_pairs={{0,4},{1,5},{2,6},{3,7},{4,0},{5,1},{6,2},{7,3},{8,12},{9,13},{10,... | collective-permute-start | bytes 294920 | tf_op jit(solution)/shard_map/ppermute | solution.py:519
  56.8 12.3 %collective-permute-start.2 = (bf16[48,8,128]{2,1,0:T(8,128)(2,1)}, bf16[48,8,128]{2,1,0:T(8,128)(2,1)S(1)}, u32[]{:S(2)}, u32[]{:S(2)}) collective-permute-start(bf16[48,8,128]{2,1,0:T(8,128)(2,1)} %get-tuple-element.66), channel_id=1, source_target_pairs={{0,6},{1,7},{2,4},{3,5},{4,2},{5,3},{6,0},{7,1},{8,14},{9,15},{10,... | collective-permute-start | bytes 294920 | tf_op jit(solution)/shard_map/ppermute | solution.py:519
  56.9 22.8 %collective-permute-start.3 = (bf16[48,8,128]{2,1,0:T(8,128)(2,1)}, bf16[48,8,128]{2,1,0:T(8,128)(2,1)S(1)}, u32[]{:S(2)}, u32[]{:S(2)}) collective-permute-start(bf16[48,8,128]{2,1,0:T(8,128)(2,1)} %get-tuple-element.67), channel_id=1, source_target_pairs={{0,8},{1,9},{2,10},{3,11},{4,12},{5,13},{6,14},{7,15},{8,0},{9,1},... | collective-permute-start | bytes 294920 | tf_op jit(solution)/shard_map/ppermute | solution.py:519
  59.2 23.5 %collective-permute-start.4 = (bf16[48,8,128]{2,1,0:T(8,128)(2,1)}, bf16[48,8,128]{2,1,0:T(8,128)(2,1)S(1)}, u32[]{:S(2)}, u32[]{:S(2)}) collective-permute-start(bf16[48,8,128]{2,1,0:T(8,128)(2,1)} %get-tuple-element.68), channel_id=1, source_target_pairs={{0,10},{1,11},{2,8},{3,9},{4,14},{5,15},{6,12},{7,13},{8,2},{9,3},... | collective-permute-start | bytes 294920 | tf_op jit(solution)/shard_map/ppermute | solution.py:519
  60.5 22.2 %collective-permute-start.5 = (bf16[48,8,128]{2,1,0:T(8,128)(2,1)}, bf16[48,8,128]{2,1,0:T(8,128)(2,1)S(1)}, u32[]{:S(2)}, u32[]{:S(2)}) collective-permute-start(bf16[48,8,128]{2,1,0:T(8,128)(2,1)} %get-tuple-element.69), channel_id=1, source_target_pairs={{0,12},{1,13},{2,14},{3,15},{4,8},{5,9},{6,10},{7,11},{8,4},{9,5},... | collective-permute-start | bytes 294920 | tf_op jit(solution)/shard_map/ppermute | solution.py:519
  64.5 18.1 %collective-permute-start.6 = (bf16[48,8,128]{2,1,0:T(8,128)(2,1)}, bf16[48,8,128]{2,1,0:T(8,128)(2,1)S(1)}, u32[]{:S(2)}, u32[]{:S(2)}) collective-permute-start(bf16[48,8,128]{2,1,0:T(8,128)(2,1)} %get-tuple-element.70), channel_id=1, source_target_pairs={{0,14},{1,15},{2,12},{3,13},{4,10},{5,11},{6,8},{7,9},{8,6},{9,7},... | collective-permute-start | bytes 294920 | tf_op jit(solution)/shard_map/ppermute | solution.py:519
  82.7 0.9 copy-start
  84.6 3.5 %collective-permute-start.7 = (bf16[8,48,8,128]{3,2,1,0:T(8,128)(2,1)S(1)}, bf16[8,48,8,128]{3,2,1,0:T(8,128)(2,1)S(1)}, u32[]{:S(2)}, u32[]{:S(2)}) collective-permute-start(bf16[8,48,8,128]{3,2,1,0:T(8,128)(2,1)S(1)} %stack.2.own_ref), channel_id=1, source_target_pairs={{0,1},{1,0},{2,3},{3,2},{4,5},{5,4},{6,7},{7,6},{8,9},{9,8},{10,11... | collective-permute-start | bytes 2359304 | tf_op jit(solution)/shard_map/ppermute | solution.py:530
  90.1 0.6 copy-start.2
  90.8 10.5 %collective-permute-start.10 = (bf16[48,8,128]{2,1,0:T(8,128)(2,1)S(1)}, bf16[48,8,128]{2,1,0:T(8,128)(2,1)S(1)}, u32[]{:S(2)}, u32[]{:S(2)}) collective-permute-start(bf16[48,8,128]{2,1,0:T(8,128)(2,1)S(1)} %get-tuple-element.74), channel_id=1, source_target_pairs={{0,6},{1,7},{2,4},{3,5},{4,2},{5,3},{6,0},{7,1},{8,14},{9,15},{10,... | collective-permute-start | bytes 294920 | tf_op jit(solution)/shard_map/ppermute | solution.py:519
  94.7 13.5 %collective-permute-start.11 = (bf16[48,8,128]{2,1,0:T(8,128)(2,1)S(1)}, bf16[48,8,128]{2,1,0:T(8,128)(2,1)S(1)}, u32[]{:S(2)}, u32[]{:S(2)}) collective-permute-start(bf16[48,8,128]{2,1,0:T(8,128)(2,1)S(1)} %get-tuple-element.75), channel_id=1, source_target_pairs={{0,8},{1,9},{2,10},{3,11},{4,12},{5,13},{6,14},{7,15},{8,0},{9,1},... | collective-permute-start | bytes 294920 | tf_op jit(solution)/shard_map/ppermute | solution.py:519
  94.8 23.4 %collective-permute-start.12 = (bf16[48,8,128]{2,1,0:T(8,128)(2,1)S(1)}, bf16[48,8,128]{2,1,0:T(8,128)(2,1)S(1)}, u32[]{:S(2)}, u32[]{:S(2)}) collective-permute-start(bf16[48,8,128]{2,1,0:T(8,128)(2,1)S(1)} %get-tuple-element.76), channel_id=1, source_target_pairs={{0,10},{1,11},{2,8},{3,9},{4,14},{5,15},{6,12},{7,13},{8,2},{9,3},... | collective-permute-start | bytes 294920 | tf_op jit(solution)/shard_map/ppermute | solution.py:519
  97.9 20.2 %collective-permute-start.13 = (bf16[48,8,128]{2,1,0:T(8,128)(2,1)S(1)}, bf16[48,8,128]{2,1,0:T(8,128)(2,1)S(1)}, u32[]{:S(2)}, u32[]{:S(2)}) collective-permute-start(bf16[48,8,128]{2,1,0:T(8,128)(2,1)S(1)} %get-tuple-element.77), channel_id=1, source_target_pairs={{0,12},{1,13},{2,14},{3,15},{4,8},{5,9},{6,10},{7,11},{8,4},{9,5},... | collective-permute-start | bytes 294920 | tf_op jit(solution)/shard_map/ppermute | solution.py:519
  99.2 19.0 %collective-permute-start.14 = (bf16[48,8,128]{2,1,0:T(8,128)(2,1)S(1)}, bf16[48,8,128]{2,1,0:T(8,128)(2,1)S(1)}, u32[]{:S(2)}, u32[]{:S(2)}) collective-permute-start(bf16[48,8,128]{2,1,0:T(8,128)(2,1)S(1)} %get-tuple-element.78), channel_id=1, source_target_pairs={{0,14},{1,15},{2,12},{3,13},{4,10},{5,11},{6,8},{7,9},{8,6},{9,7},... | collective-permute-start | bytes 294920 | tf_op jit(solution)/shard_map/ppermute | solution.py:519
  101.3 16.9 %copy-start.5 = (bf16[48,8,128]{2,1,0:T(8,128)(2,1)}, bf16[48,8,128]{2,1,0:T(8,128)(2,1)S(1)}, u32[]{:S(2)}) copy-start(bf16[48,8,128]{2,1,0:T(8,128)(2,1)S(1)} %collective-permute-done.10.refs_3_) | copy-start | bytes 294916
  101.3 16.9 %collective-permute-start.8 = (bf16[48,8,128]{2,1,0:T(8,128)(2,1)S(1)}, bf16[48,8,128]{2,1,0:T(8,128)(2,1)S(1)}, u32[]{:S(2)}, u32[]{:S(2)}) collective-permute-start(bf16[48,8,128]{2,1,0:T(8,128)(2,1)S(1)} %get-tuple-element.72), channel_id=1, source_target_pairs={{0,2},{1,3},{2,0},{3,1},{4,6},{5,7},{6,4},{7,5},{8,10},{9,11},{10,... | collective-permute-start | bytes 294920 | tf_op jit(solution)/shard_map/ppermute | solution.py:519
  108.3 9.9 %copy-start.6 = (bf16[48,8,128]{2,1,0:T(8,128)(2,1)}, bf16[48,8,128]{2,1,0:T(8,128)(2,1)S(1)}, u32[]{:S(2)}) copy-start(bf16[48,8,128]{2,1,0:T(8,128)(2,1)S(1)} %collective-permute-done.11.refs_4_) | copy-start | bytes 294916
  108.3 9.9 %collective-permute-start.9 = (bf16[48,8,128]{2,1,0:T(8,128)(2,1)S(1)}, bf16[48,8,128]{2,1,0:T(8,128)(2,1)S(1)}, u32[]{:S(2)}, u32[]{:S(2)}) collective-permute-start(bf16[48,8,128]{2,1,0:T(8,128)(2,1)S(1)} %get-tuple-element.73), channel_id=1, source_target_pairs={{0,4},{1,5},{2,6},{3,7},{4,0},{5,1},{6,2},{7,3},{8,12},{9,13},{10,... | collective-permute-start | bytes 294920 | tf_op jit(solution)/shard_map/ppermute | solution.py:519
  118.1 0.6 copy-start.7
  118.2 0.7 copy-start.8
  118.2 0.7 copy-start.9
  118.2 0.7 copy-start.10
  118.2 0.7 copy-start.11
  118.2 0.9 copy-start.3
  128.8 25.0 %all-to-all-start.2 = ((bf16[16,24,8,128]{3,2,1,0:T(8,128)(2,1)}), bf16[16,24,8,128]{3,2,1,0:T(8,128)(2,1)S(1)}, u32[]{:S(2)}, u32[]{:S(2)}) async-start(bf16[16,24,8,128]{3,2,1,0:T(8,128)(2,1)} %get-tuple-element.79), calls=%async_computation.2 | async-start | bytes 1572864 | tf_op jit(solution)/shard_map/all_to_all | solution.py:512
  155.3 67.4 %all-to-all-start.3 = ((bf16[16,24,8,128]{3,2,1,0:T(8,128)(2,1)}), bf16[16,24,8,128]{3,2,1,0:T(8,128)(2,1)S(1)}, u32[]{:S(2)}, u32[]{:S(2)}) async-start(bf16[16,24,8,128]{3,2,1,0:T(8,128)(2,1)} %reorder.3), calls=%async_computation.3 | async-start | bytes 1572864 | tf_op jit(solution)/shard_map/all_to_all | solution.py:512
  165.9 6.3 %collective-permute-start.15 = (bf16[48,8,128]{2,1,0:T(8,128)(2,1)}, bf16[48,8,128]{2,1,0:T(8,128)(2,1)S(1)}, u32[]{:S(2)}, u32[]{:S(2)}) collective-permute-start(bf16[48,8,128]{2,1,0:T(8,128)(2,1)} %get-tuple-element.85), channel_id=1, source_target_pairs={{0,2},{1,3},{2,0},{3,1},{4,6},{5,7},{6,4},{7,5},{8,10},{9,11},{10,... | collective-permute-start | bytes 294920 | tf_op jit(solution)/shard_map/ppermute | solution.py:519
  167.3 9.0 %collective-permute-start.16 = (bf16[48,8,128]{2,1,0:T(8,128)(2,1)}, bf16[48,8,128]{2,1,0:T(8,128)(2,1)S(1)}, u32[]{:S(2)}, u32[]{:S(2)}) collective-permute-start(bf16[48,8,128]{2,1,0:T(8,128)(2,1)} %get-tuple-element.86), channel_id=1, source_target_pairs={{0,4},{1,5},{2,6},{3,7},{4,0},{5,1},{6,2},{7,3},{8,12},{9,13},{10,... | collective-permute-start | bytes 294920 | tf_op jit(solution)/shard_map/ppermute | solution.py:519
  168.5 12.3 %collective-permute-start.17 = (bf16[48,8,128]{2,1,0:T(8,128)(2,1)}, bf16[48,8,128]{2,1,0:T(8,128)(2,1)S(1)}, u32[]{:S(2)}, u32[]{:S(2)}) collective-permute-start(bf16[48,8,128]{2,1,0:T(8,128)(2,1)} %get-tuple-element.87), channel_id=1, source_target_pairs={{0,6},{1,7},{2,4},{3,5},{4,2},{5,3},{6,0},{7,1},{8,14},{9,15},{10,... | collective-permute-start | bytes 294920 | tf_op jit(solution)/shard_map/ppermute | solution.py:519
  168.6 22.8 %collective-permute-start.18 = (bf16[48,8,128]{2,1,0:T(8,128)(2,1)}, bf16[48,8,128]{2,1,0:T(8,128)(2,1)S(1)}, u32[]{:S(2)}, u32[]{:S(2)}) collective-permute-start(bf16[48,8,128]{2,1,0:T(8,128)(2,1)} %get-tuple-element.88), channel_id=1, source_target_pairs={{0,8},{1,9},{2,10},{3,11},{4,12},{5,13},{6,14},{7,15},{8,0},{9,1},... | collective-permute-start | bytes 294920 | tf_op jit(solution)/shard_map/ppermute | solution.py:519
  170.8 23.5 %collective-permute-start.19 = (bf16[48,8,128]{2,1,0:T(8,128)(2,1)}, bf16[48,8,128]{2,1,0:T(8,128)(2,1)S(1)}, u32[]{:S(2)}, u32[]{:S(2)}) collective-permute-start(bf16[48,8,128]{2,1,0:T(8,128)(2,1)} %get-tuple-element.89), channel_id=1, source_target_pairs={{0,10},{1,11},{2,8},{3,9},{4,14},{5,15},{6,12},{7,13},{8,2},{9,3},... | collective-permute-start | bytes 294920 | tf_op jit(solution)/shard_map/ppermute | solution.py:519
  172.1 22.2 %collective-permute-start.20 = (bf16[48,8,128]{2,1,0:T(8,128)(2,1)}, bf16[48,8,128]{2,1,0:T(8,128)(2,1)S(1)}, u32[]{:S(2)}, u32[]{:S(2)}) collective-permute-start(bf16[48,8,128]{2,1,0:T(8,128)(2,1)} %get-tuple-element.90), channel_id=1, source_target_pairs={{0,12},{1,13},{2,14},{3,15},{4,8},{5,9},{6,10},{7,11},{8,4},{9,5},... | collective-permute-start | bytes 294920 | tf_op jit(solution)/shard_map/ppermute | solution.py:519
  176.2 18.1 %collective-permute-start.21 = (bf16[48,8,128]{2,1,0:T(8,128)(2,1)}, bf16[48,8,128]{2,1,0:T(8,128)(2,1)S(1)}, u32[]{:S(2)}, u32[]{:S(2)}) collective-permute-start(bf16[48,8,128]{2,1,0:T(8,128)(2,1)} %get-tuple-element.91), channel_id=1, source_target_pairs={{0,14},{1,15},{2,12},{3,13},{4,10},{5,11},{6,8},{7,9},{8,6},{9,7},... | collective-permute-start | bytes 294920 | tf_op jit(solution)/shard_map/ppermute | solution.py:519
  194.3 0.9 copy-start.1
  196.3 3.5 %collective-permute-start.22 = (bf16[8,48,8,128]{3,2,1,0:T(8,128)(2,1)S(1)}, bf16[8,48,8,128]{3,2,1,0:T(8,128)(2,1)S(1)}, u32[]{:S(2)}, u32[]{:S(2)}) collective-permute-start(bf16[8,48,8,128]{3,2,1,0:T(8,128)(2,1)S(1)} %stack.3.own_ref), channel_id=1, source_target_pairs={{0,1},{1,0},{2,3},{3,2},{4,5},{5,4},{6,7},{7,6},{8,9},{9,8},{10,11... | collective-permute-start | bytes 2359304 | tf_op jit(solution)/shard_map/ppermute | solution.py:530
  201.6 7.6 %collective-permute-start.23 = (bf16[48,8,128]{2,1,0:T(8,128)(2,1)S(1)}, bf16[48,8,128]{2,1,0:T(8,128)(2,1)S(1)}, u32[]{:S(2)}, u32[]{:S(2)}) collective-permute-start(bf16[48,8,128]{2,1,0:T(8,128)(2,1)S(1)} %get-tuple-element.93), channel_id=1, source_target_pairs={{0,2},{1,3},{2,0},{3,1},{4,6},{5,7},{6,4},{7,5},{8,10},{9,11},{10,... | collective-permute-start | bytes 294920 | tf_op jit(solution)/shard_map/ppermute | solution.py:519
  202.0 8.4 %collective-permute-start.24 = (bf16[48,8,128]{2,1,0:T(8,128)(2,1)S(1)}, bf16[48,8,128]{2,1,0:T(8,128)(2,1)S(1)}, u32[]{:S(2)}, u32[]{:S(2)}) collective-permute-start(bf16[48,8,128]{2,1,0:T(8,128)(2,1)S(1)} %get-tuple-element.94), channel_id=1, source_target_pairs={{0,4},{1,5},{2,6},{3,7},{4,0},{5,1},{6,2},{7,3},{8,12},{9,13},{10,... | collective-permute-start | bytes 294920 | tf_op jit(solution)/shard_map/ppermute | solution.py:519
  205.9 8.2 %collective-permute-start.25 = (bf16[48,8,128]{2,1,0:T(8,128)(2,1)S(1)}, bf16[48,8,128]{2,1,0:T(8,128)(2,1)S(1)}, u32[]{:S(2)}, u32[]{:S(2)}) collective-permute-start(bf16[48,8,128]{2,1,0:T(8,128)(2,1)S(1)} %get-tuple-element.95), channel_id=1, source_target_pairs={{0,6},{1,7},{2,4},{3,5},{4,2},{5,3},{6,0},{7,1},{8,14},{9,15},{10,... | collective-permute-start | bytes 294920 | tf_op jit(solution)/shard_map/ppermute | solution.py:519
  206.8 7.3 %collective-permute-start.26 = (bf16[48,8,128]{2,1,0:T(8,128)(2,1)S(1)}, bf16[48,8,128]{2,1,0:T(8,128)(2,1)S(1)}, u32[]{:S(2)}, u32[]{:S(2)}) collective-permute-start(bf16[48,8,128]{2,1,0:T(8,128)(2,1)S(1)} %get-tuple-element.96), channel_id=1, source_target_pairs={{0,8},{1,9},{2,10},{3,11},{4,12},{5,13},{6,14},{7,15},{8,0},{9,1},... | collective-permute-start | bytes 294920 | tf_op jit(solution)/shard_map/ppermute | solution.py:519
  208.3 14.4 %collective-permute-start.27 = (bf16[48,8,128]{2,1,0:T(8,128)(2,1)S(1)}, bf16[48,8,128]{2,1,0:T(8,128)(2,1)S(1)}, u32[]{:S(2)}, u32[]{:S(2)}) collective-permute-start(bf16[48,8,128]{2,1,0:T(8,128)(2,1)S(1)} %get-tuple-element.97), channel_id=1, source_target_pairs={{0,10},{1,11},{2,8},{3,9},{4,14},{5,15},{6,12},{7,13},{8,2},{9,3},... | collective-permute-start | bytes 294920 | tf_op jit(solution)/shard_map/ppermute | solution.py:519
  209.2 13.5 %collective-permute-start.28 = (bf16[48,8,128]{2,1,0:T(8,128)(2,1)S(1)}, bf16[48,8,128]{2,1,0:T(8,128)(2,1)S(1)}, u32[]{:S(2)}, u32[]{:S(2)}) collective-permute-start(bf16[48,8,128]{2,1,0:T(8,128)(2,1)S(1)} %get-tuple-element.98), channel_id=1, source_target_pairs={{0,12},{1,13},{2,14},{3,15},{4,8},{5,9},{6,10},{7,11},{8,4},{9,5},... | collective-permute-start | bytes 294920 | tf_op jit(solution)/shard_map/ppermute | solution.py:519
  210.4 12.3 %collective-permute-start.29 = (bf16[48,8,128]{2,1,0:T(8,128)(2,1)S(1)}, bf16[48,8,128]{2,1,0:T(8,128)(2,1)S(1)}, u32[]{:S(2)}, u32[]{:S(2)}) collective-permute-start(bf16[48,8,128]{2,1,0:T(8,128)(2,1)S(1)} %get-tuple-element.99), channel_id=1, source_target_pairs={{0,14},{1,15},{2,12},{3,13},{4,10},{5,11},{6,8},{7,9},{8,6},{9,7},... | collective-permute-start | bytes 294920 | tf_op jit(solution)/shard_map/ppermute | solution.py:519

commit v7 on v6

--- a/solution.py
+++ b/solution.py
@@ -13,7 +13,7 @@
 SUB, LANE = 8, 128
 MIB = 1 << 20
 STRIDE = SUB + 1
-FETCH_BLOCKS, UNROLL = 4, 32
+FETCH_BLOCKS = 4
 FIRST_MIB, FETCH_MIB, LATER_MIB, LAST_MIB, SETTLE_MIB = 58, 58, 58, 58, 16
 F32, BF16 = jnp.float32, jnp.bfloat16
 HALF_ROOT = 0.7071067811865476
@@ -47,13 +47,14 @@
 
 
 def pick_rows(picks_ref, step, visit_index, table, picked, outs, first):
-    rows = picks_ref.shape[3]
-
-    @pl.loop(0, rows // UNROLL)
+    _, groups, _, group_rows = picks_ref.shape
+    rows = groups * group_rows
+
+    @pl.loop(0, groups)
     def _(group):
-        for offset in range(UNROLL):
-            row = group * UNROLL + offset
-            pick = picks_ref[0, step, visit_index, row]
+        for offset in range(group_rows):
+            pick = picks_ref[step, group, visit_index, offset]
+            row = group * group_rows + offset
             picked[pl.ds(row * STRIDE, SUB), :] = table[pl.ds(pick * STRIDE, SUB), :]
 
     lanes = outs[0].shape[1] // LANE
@@ -67,7 +68,7 @@
 
 def table_scratch(features, rows):
     count, width = features.shape
-    if 2 * width > SUB * LANE or count % FETCH_BLOCKS or rows % UNROLL:
+    if 2 * width > SUB * LANE or count % FETCH_BLOCKS or rows % LANE:
         raise ValueError("sizes")
     return [
         pltpu.VMEM((2, count, width), features.dtype),
@@ -78,7 +79,8 @@
 
 
 def fetch_kernel(visit_index, picks_ref, x_ref, y_ref, x_out, y_out, held, table, picked, sems):
-    _, steps, _, rows = picks_ref.shape
+    steps, groups, _, group_rows = picks_ref.shape
+    rows = groups * group_rows
     copies = table_copies(x_ref, y_ref, held, sems)
     for copy in copies:
         copy.start()
@@ -89,7 +91,7 @@
 
 def fetch(features, targets, picks, visit_index):
     count, width = features.shape
-    _, steps, _, rows = picks.shape
+    steps, rows = picks.shape[0], picks.shape[1] * picks.shape[3]
     return pl.pallas_call(
         functools.partial(fetch_kernel, visit_index),
         in_specs=[SCALARS, ANYWHERE, ANYWHERE],
@@ -310,7 +312,7 @@
     packed_shape = (2 * pieces, depth // (2 * pieces), SUB, LANE)
     shapes = [packed_shape] + [(width, hidden), (hidden, width)] * 2 + more_outs
     return pl.pallas_call(
-        functools.partial(kernel, slots, pieces, rows // 4),
+        functools.partial(kernel, slots, pieces, rows),
         grid=(steps - 1,),
         in_specs=in_specs,
         out_specs=[whole(shape) for shape in shapes],
@@ -372,7 +374,7 @@
     last = batch[0].shape[0] // rows - 1
     batch_spec = pl.BlockSpec((rows, width), lambda step: (last, 0))
     return pl.pallas_call(
-        functools.partial(last_step_kernel, slots, pieces, rows // 4),
+        functools.partial(last_step_kernel, slots, pieces, rows),
         grid=(1,),
         in_specs=[SCALARS, batch_spec, batch_spec] + [whole(part.shape) for part in kept],
         out_specs=[ANYWHERE] * pieces,
@@ -544,7 +546,7 @@
     slots = {count: tile_slots(shapes, count)[0] for count in (devices // 2, devices)}
     _, visits, steps, rows = row_index.shape
     sizes = (steps, rows, *shapes[0])
-    picks = jnp.transpose(row_index, (0, 2, 1, 3))
+    picks = row_index.reshape(visits, steps, rows // LANE, LANE).transpose(1, 2, 0, 3)
     sources = [invert(hop_order[visit_index]) for visit_index in range(visits)]
     weights, kept, batch = first_visit(features, targets, picks, model, sizes, slots)
     for visit_index in range(visits):

time: 229 us -> 221 us (0.965)
  Pallas kernels: 56.9 us -> 46.9 us
    pallas_call x4, Pallas kernels: 35.3 us -> 27.9 us  [the longest x2 19.5 us: visit(): pl.pallas_call(functools.partial(kernel, slots, pieces, rows), grid=(step...]
    pallas_call x1, Pallas kernels: 9.83 us -> 7.32 us  [fetch(): pl.pallas_call(functools.partial(fetch_kernel, visit_index), in_specs=[SC...]
  transfers between devices with their start and end apart: 34 -> 34, of which waited for: 17 -> 17; matrix products, arithmetic and copies ran while one was open for 0% -> 0% of each run, Pallas kernels for 11% -> 10%
where the time goes in v7:
time: 221 us; the launch traced here: 217 us
  waiting for transfers between devices  89.4 us (40%)
  starting transfers between devices  76.6 us (35%)
  Pallas kernels  46.9 us (21%)
  local copies, waits for them, and re-layouts  3.37 us (2%)
    ppermute x28, starting transfers between devices, spread(): lax.ppermute(parts[k], 'hop', [(i, i ^ 2 * k) for i in range(devices)])  48.7 us
    ppermute x28, waiting for transfers between devices, spread(): lax.ppermute(parts[k], 'hop', [(i, i ^ 2 * k) for i in range(devices)])  48.5 us
    all_to_all x4, waiting for transfers between devices, exchange(): lax.all_to_all(packed, 'hop', split_axis=0, concat_axis=0, tiled=True)  37 us
    all_to_all x4, starting transfers between devices, exchange(): lax.all_to_all(packed, 'hop', split_axis=0, concat_axis=0, tiled=True)  24.6 us
    pallas_call x2, Pallas kernels, visit(): pl.pallas_call(functools.partial(kernel, slots, pieces, rows), grid=(step...  19.5 us
    pallas_call x2, Pallas kernels, last_step(): pl.pallas_call(functools.partial(last_step_kernel, slots, pieces, rows),...  8.41 us
    pallas_call x1, Pallas kernels, fetch(): pl.pallas_call(functools.partial(fetch_kernel, visit_index), in_specs=[SC...  7.32 us
  transfers between devices with their start and end apart: 34, of which 17 were waited for; matrix products, arithmetic and copies ran while one was open for 0% of the time, Pallas kernels for 10%

profile of v7, /device:TPU:1, one launch (start us, length us, event | category | flops | bytes accessed | tf_op | source)
XLA Modules:
  0.0 217.5 jit_solution(2111419990254796288)
XLA Ops:
  0.6 11.6 %visit.2 = (bf16[16,24,8,128]{3,2,1,0:T(8,128)(2,1)}, bf16[384,512]{1,0:T(8,128)(2,1)}, bf16[512,384]{1,0:T(8,128)(2,1)}, bf16[384,512]{1,0:T(8,128)(2,1)}, bf16...) custom-call(s32[3,4,2,128]{3,2,1,0:T(2,128)} %bitcast.20, bf16[4096,384]{1,0:T(8,128)(2,1)} %x_ref.3, ...), custom_call_target="tpu_custom_call" | custom-call | flops 2013265920 | bytes 4718592 | tf_op jit(solution)/shard_map/visit/pallas_call | solution.py:314
  12.3 7.3 %all-to-all-start = ((bf16[16,24,8,128]{3,2,1,0:T(8,128)(2,1)}), bf16[16,24,8,128]{3,2,1,0:T(8,128)(2,1)S(1)}, u32[]{:S(2)}, u32[]{:S(2)}) async-start(bf16[16,24,8,128]{3,2,1,0:T(8,128)(2,1)} %get-tuple-element.56), calls=%async_computation | async-start | bytes 1572864 | tf_op jit(solution)/shard_map/all_to_all | solution.py:514
  19.7 18.5 %all-to-all-done.packed_ref = bf16[16,24,8,128]{3,2,1,0:T(8,128)(2,1)S(1)} async-done(((bf16[16,24,8,128]{3,2,1,0:T(8,128)(2,1)}), bf16[16,24,8,128]{3,2,1,0:T(8,128)(2,1)S(1)}, u32[]{:S(2)}, u32[]{:S(2)}) %all-to-all-start) | async-done | bytes 786464 | tf_op jit(solution)/shard_map/all_to_all | solution.py:514
  38.2 1.5 reorder.2
  39.8 5.5 %all-to-all-start.1 = ((bf16[16,24,8,128]{3,2,1,0:T(8,128)(2,1)}), bf16[16,24,8,128]{3,2,1,0:T(8,128)(2,1)S(1)}, u32[]{:S(2)}, u32[]{:S(2)}) async-start(bf16[16,24,8,128]{3,2,1,0:T(8,128)(2,1)} %reorder.2), calls=%async_computation.1 | async-start | bytes 1572864 | tf_op jit(solution)/shard_map/all_to_all | solution.py:514
  45.2 4.2 %last.2 = (bf16[48,8,128]{2,1,0:T(8,128)(2,1)}, bf16[48,8,128]{2,1,0:T(8,128)(2,1)}, bf16[48,8,128]{2,1,0:T(8,128)(2,1)}, bf16[48,8,128]{2,1,0:T(8,128)(2,1)}, b...) custom-call(s32[1]{0:T(128)} %bitcast.me_ref, ...), custom_call_target="tpu_custom_call" | custom-call | flops 1006632960 | bytes 3932160 | tf_op jit(solution)/shard_map/last/pallas_call | solution.py:376
  49.5 1.4 collective-permute-start
  50.9 1.2 collective-permute-start.1
  52.2 2.3 %collective-permute-start.3 = (bf16[48,8,128]{2,1,0:T(8,128)(2,1)}, bf16[48,8,128]{2,1,0:T(8,128)(2,1)S(1)}, u32[]{:S(2)}, u32[]{:S(2)}) collective-permute-start(bf16[48,8,128]{2,1,0:T(8,128)(2,1)} %get-tuple-element.67), channel_id=1, source_target_pairs={{0,8},{1,9},{2,10},{3,11},{4,12},{5,13},{6,14},{7,15},{8,0},{9,1},... | collective-permute-start | bytes 294920 | tf_op jit(solution)/shard_map/ppermute | solution.py:521
  54.4 1.2 collective-permute-start.4
  55.8 2.8 %collective-permute-start.5 = (bf16[48,8,128]{2,1,0:T(8,128)(2,1)}, bf16[48,8,128]{2,1,0:T(8,128)(2,1)S(1)}, u32[]{:S(2)}, u32[]{:S(2)}) collective-permute-start(bf16[48,8,128]{2,1,0:T(8,128)(2,1)} %get-tuple-element.69), channel_id=1, source_target_pairs={{0,12},{1,13},{2,14},{3,15},{4,8},{5,9},{6,10},{7,11},{8,4},{9,5},... | collective-permute-start | bytes 294920 | tf_op jit(solution)/shard_map/ppermute | solution.py:521
  58.6 2.1 collective-permute-done.1.refs_2_
  60.7 3.7 %collective-permute-start.6 = (bf16[48,8,128]{2,1,0:T(8,128)(2,1)}, bf16[48,8,128]{2,1,0:T(8,128)(2,1)S(1)}, u32[]{:S(2)}, u32[]{:S(2)}) collective-permute-start(bf16[48,8,128]{2,1,0:T(8,128)(2,1)} %get-tuple-element.70), channel_id=1, source_target_pairs={{0,14},{1,15},{2,12},{3,13},{4,10},{5,11},{6,8},{7,9},{8,6},{9,7},... | collective-permute-start | bytes 294920 | tf_op jit(solution)/shard_map/ppermute | solution.py:521
  65.2 10.6 %collective-permute-done.3.refs_4_ = bf16[48,8,128]{2,1,0:T(8,128)(2,1)S(1)} collective-permute-done((bf16[48,8,128]{2,1,0:T(8,128)(2,1)}, bf16[48,8,128]{2,1,0:T(8,128)(2,1)S(1)}, u32[]{:S(2)}, u32[]{:S(2)}) %collective-permute-start.3) | collective-permute-done | bytes 98336 | tf_op jit(solution)/shard_map/ppermute | solution.py:521
  75.8 3.0 %collective-permute-done.4.refs_5_ = bf16[48,8,128]{2,1,0:T(8,128)(2,1)S(1)} collective-permute-done((bf16[48,8,128]{2,1,0:T(8,128)(2,1)}, bf16[48,8,128]{2,1,0:T(8,128)(2,1)S(1)}, u32[]{:S(2)}, u32[]{:S(2)}) %collective-permute-start.4) | collective-permute-done | bytes 98336 | tf_op jit(solution)/shard_map/ppermute | solution.py:521
  80.8 1.6 collective-permute-start.7
  82.4 1.9 collective-permute-done.7.partner_ref
  84.3 1.8 route.2
  86.7 4.0 %collective-permute-start.10 = (bf16[48,8,128]{2,1,0:T(8,128)(2,1)S(1)}, bf16[48,8,128]{2,1,0:T(8,128)(2,1)S(1)}, u32[]{:S(2)}, u32[]{:S(2)}) collective-permute-start(bf16[48,8,128]{2,1,0:T(8,128)(2,1)S(1)} %get-tuple-element.74), channel_id=1, source_target_pairs={{0,6},{1,7},{2,4},{3,5},{4,2},{5,3},{6,0},{7,1},{8,14},{9,15},{10,... | collective-permute-start | bytes 294920 | tf_op jit(solution)/shard_map/ppermute | solution.py:521
  90.7 3.2 %collective-permute-start.12 = (bf16[48,8,128]{2,1,0:T(8,128)(2,1)S(1)}, bf16[48,8,128]{2,1,0:T(8,128)(2,1)S(1)}, u32[]{:S(2)}, u32[]{:S(2)}) collective-permute-start(bf16[48,8,128]{2,1,0:T(8,128)(2,1)S(1)} %get-tuple-element.76), channel_id=1, source_target_pairs={{0,10},{1,11},{2,8},{3,9},{4,14},{5,15},{6,12},{7,13},{8,2},{9,3},... | collective-permute-start | bytes 294920 | tf_op jit(solution)/shard_map/ppermute | solution.py:521
  93.9 1.3 collective-permute-start.13
  95.2 2.0 collective-permute-start.14
  98.4 5.9 %collective-permute-done.11.refs_4_ = bf16[48,8,128]{2,1,0:T(8,128)(2,1)S(1)} collective-permute-done((bf16[48,8,128]{2,1,0:T(8,128)(2,1)S(1)}, bf16[48,8,128]{2,1,0:T(8,128)(2,1)S(1)}, u32[]{:S(2)}, u32[]{:S(2)}) %collective-permute-start.11) | collective-permute-done | bytes 98336 | tf_op jit(solution)/shard_map/ppermute | solution.py:521
  104.2 7.3 %fetch.1 = (bf16[1536,384]{1,0:T(8,128)(2,1)}, bf16[1536,384]{1,0:T(8,128)(2,1)}) custom-call(s32[3,4,2,128]{3,2,1,0:T(2,128)} %bitcast.21, bf16[4096,384]{1,0:T(8,128)(2,1)} %x_ref.3, bf16[4096,384]{1,0:T(8,128)(2,1)} %y_ref.3), custom_call_target="tpu_custom_call" | custom-call | bytes 6291456 | tf_op jit(solution)/shard_map/fetch/pallas_call | solution.py:95
  112.6 7.9 %visit.3 = (bf16[16,24,8,128]{3,2,1,0:T(8,128)(2,1)}, bf16[384,512]{1,0:T(8,128)(2,1)}, bf16[512,384]{1,0:T(8,128)(2,1)}, bf16[384,512]{1,0:T(8,128)(2,1)}, bf16[512,384]{1,0:T(8,128)(2,1)}) custom-call(s32[1]{0:T(128)} %bitcast.me_ref, bf16[1536,384]{1,0:T(8,128)(2,1)} %get-tuple-element.54.x_ref, bf16[1536,384]{1,0:T(8,128)(2,1)} %get-tuple-element.55.y_ref, ...), custom_call_target="tpu_custom_call" | custom-call | flops 2013265920 | bytes 4718592 | tf_op jit(solution)/shard_map/visit/pallas_call | solution.py:314
  120.5 6.4 %all-to-all-start.2 = ((bf16[16,24,8,128]{3,2,1,0:T(8,128)(2,1)}), bf16[16,24,8,128]{3,2,1,0:T(8,128)(2,1)S(1)}, u32[]{:S(2)}, u32[]{:S(2)}) async-start(bf16[16,24,8,128]{3,2,1,0:T(8,128)(2,1)} %get-tuple-element.79), calls=%async_computation.2 | async-start | bytes 1572864 | tf_op jit(solution)/shard_map/all_to_all | solution.py:514
  127.0 18.5 %all-to-all-done.2.packed_ref = bf16[16,24,8,128]{3,2,1,0:T(8,128)(2,1)S(1)} async-done(((bf16[16,24,8,128]{3,2,1,0:T(8,128)(2,1)}), bf16[16,24,8,128]{3,2,1,0:T(8,128)(2,1)S(1)}, u32[]{:S(2)}, u32[]{:S(2)}) %all-to-all-start.2) | async-done | bytes 786464 | tf_op jit(solution)/shard_map/all_to_all | solution.py:514
  145.6 1.5 reorder.3
  147.1 5.5 %all-to-all-start.3 = ((bf16[16,24,8,128]{3,2,1,0:T(8,128)(2,1)}), bf16[16,24,8,128]{3,2,1,0:T(8,128)(2,1)S(1)}, u32[]{:S(2)}, u32[]{:S(2)}) async-start(bf16[16,24,8,128]{3,2,1,0:T(8,128)(2,1)} %reorder.3), calls=%async_computation.3 | async-start | bytes 1572864 | tf_op jit(solution)/shard_map/all_to_all | solution.py:514
  152.6 4.2 %last.3 = (bf16[48,8,128]{2,1,0:T(8,128)(2,1)}, bf16[48,8,128]{2,1,0:T(8,128)(2,1)}, bf16[48,8,128]{2,1,0:T(8,128)(2,1)}, bf16[48,8,128]{2,1,0:T(8,128)(2,1)}, b...) custom-call(s32[1]{0:T(128)} %bitcast.me_ref, ...), custom_call_target="tpu_custom_call" | custom-call | flops 1006632960 | bytes 3932160 | tf_op jit(solution)/shard_map/last/pallas_call | solution.py:376
  156.8 1.4 collective-permute-start.15
  158.2 1.2 collective-permute-start.16
  159.5 2.3 %collective-permute-start.18 = (bf16[48,8,128]{2,1,0:T(8,128)(2,1)}, bf16[48,8,128]{2,1,0:T(8,128)(2,1)S(1)}, u32[]{:S(2)}, u32[]{:S(2)}) collective-permute-start(bf16[48,8,128]{2,1,0:T(8,128)(2,1)} %get-tuple-element.88), channel_id=1, source_target_pairs={{0,8},{1,9},{2,10},{3,11},{4,12},{5,13},{6,14},{7,15},{8,0},{9,1},... | collective-permute-start | bytes 294920 | tf_op jit(solution)/shard_map/ppermute | solution.py:521
  161.7 1.2 collective-permute-start.19
  163.0 2.9 %collective-permute-start.20 = (bf16[48,8,128]{2,1,0:T(8,128)(2,1)}, bf16[48,8,128]{2,1,0:T(8,128)(2,1)S(1)}, u32[]{:S(2)}, u32[]{:S(2)}) collective-permute-start(bf16[48,8,128]{2,1,0:T(8,128)(2,1)} %get-tuple-element.90), channel_id=1, source_target_pairs={{0,12},{1,13},{2,14},{3,15},{4,8},{5,9},{6,10},{7,11},{8,4},{9,5},... | collective-permute-start | bytes 294920 | tf_op jit(solution)/shard_map/ppermute | solution.py:521
  165.9 2.1 collective-permute-done.16.refs_2_
  168.0 3.7 %collective-permute-start.21 = (bf16[48,8,128]{2,1,0:T(8,128)(2,1)}, bf16[48,8,128]{2,1,0:T(8,128)(2,1)S(1)}, u32[]{:S(2)}, u32[]{:S(2)}) collective-permute-start(bf16[48,8,128]{2,1,0:T(8,128)(2,1)} %get-tuple-element.91), channel_id=1, source_target_pairs={{0,14},{1,15},{2,12},{3,13},{4,10},{5,11},{6,8},{7,9},{8,6},{9,7},... | collective-permute-start | bytes 294920 | tf_op jit(solution)/shard_map/ppermute | solution.py:521
  172.5 10.6 %collective-permute-done.18.refs_4_ = bf16[48,8,128]{2,1,0:T(8,128)(2,1)S(1)} collective-permute-done((bf16[48,8,128]{2,1,0:T(8,128)(2,1)}, bf16[48,8,128]{2,1,0:T(8,128)(2,1)S(1)}, u32[]{:S(2)}, u32[]{:S(2)}) %collective-permute-start.18) | collective-permute-done | bytes 98336 | tf_op jit(solution)/shard_map/ppermute | solution.py:521
  183.2 3.0 %collective-permute-done.19.refs_5_ = bf16[48,8,128]{2,1,0:T(8,128)(2,1)S(1)} collective-permute-done((bf16[48,8,128]{2,1,0:T(8,128)(2,1)}, bf16[48,8,128]{2,1,0:T(8,128)(2,1)S(1)}, u32[]{:S(2)}, u32[]{:S(2)}) %collective-permute-start.19) | collective-permute-done | bytes 98336 | tf_op jit(solution)/shard_map/ppermute | solution.py:521
  188.1 1.6 collective-permute-start.22
  189.7 1.9 collective-permute-done.22.partner_ref
  191.6 1.8 route.3
  193.8 3.9 %collective-permute-start.24 = (bf16[48,8,128]{2,1,0:T(8,128)(2,1)S(1)}, bf16[48,8,128]{2,1,0:T(8,128)(2,1)S(1)}, u32[]{:S(2)}, u32[]{:S(2)}) collective-permute-start(bf16[48,8,128]{2,1,0:T(8,128)(2,1)S(1)} %get-tuple-element.94), channel_id=1, source_target_pairs={{0,4},{1,5},{2,6},{3,7},{4,0},{5,1},{6,2},{7,3},{8,12},{9,13},{10,... | collective-permute-start | bytes 294920 | tf_op jit(solution)/shard_map/ppermute | solution.py:521
  198.6 1.5 collective-permute-start.26
  201.0 1.2 collective-permute-start.28
  202.2 2.9 %collective-permute-start.29 = (bf16[48,8,128]{2,1,0:T(8,128)(2,1)S(1)}, bf16[48,8,128]{2,1,0:T(8,128)(2,1)S(1)}, u32[]{:S(2)}, u32[]{:S(2)}) collective-permute-start(bf16[48,8,128]{2,1,0:T(8,128)(2,1)S(1)} %get-tuple-element.99), channel_id=1, source_target_pairs={{0,14},{1,15},{2,12},{3,13},{4,10},{5,11},{6,8},{7,9},{8,6},{9,7},... | collective-permute-start | bytes 294920 | tf_op jit(solution)/shard_map/ppermute | solution.py:521
  205.9 8.6 %collective-permute-done.27.refs_5_ = bf16[48,8,128]{2,1,0:T(8,128)(2,1)S(1)} collective-permute-done((bf16[48,8,128]{2,1,0:T(8,128)(2,1)S(1)}, bf16[48,8,128]{2,1,0:T(8,128)(2,1)S(1)}, u32[]{:S(2)}, u32[]{:S(2)}) %collective-permute-start.27) | collective-permute-done | bytes 98336 | tf_op jit(solution)/shard_map/ppermute | solution.py:521
  214.5 2.8 %settle.1 = (f32[384,512]{1,0:T(8,128)}, f32[512,384]{1,0:T(8,128)}, bf16[384,512]{1,0:T(8,128)(2,1)}, bf16[512,384]{1,0:T(8,128)(2,1)}) custom-call(s32[1]{0:T(128)} %bitcast.me_ref, bf16[16,24,8,128]{3,2,1,0:T(8,128)(2,1)S(1)} %all-to-all-done.3.weights_ref, bf16[48,8,128]{2,1,0:T(8,128)(2,1)S(1)} %get-tuple-element.92.refs_0_, ...), custom_call_target="tpu_custom_call" | custom-call | tf_op jit(solution)/shard_map/settle/pallas_call | solution.py:495
  (59 shorter events, 11.9 us)
Async XLA Ops:
  0.6 19.0 %copy-start.4 = (s32[2,16]{1,0:T(2,128)S(1)}, s32[2,16]{1,0:T(2,128)}, u32[]{:S(2)}) copy-start(s32[2,16]{1,0:T(2,128)} %param.11) | copy-start | bytes 388
  12.3 26.0 %all-to-all-start = ((bf16[16,24,8,128]{3,2,1,0:T(8,128)(2,1)}), bf16[16,24,8,128]{3,2,1,0:T(8,128)(2,1)S(1)}, u32[]{:S(2)}, u32[]{:S(2)}) async-start(bf16[16,24,8,128]{3,2,1,0:T(8,128)(2,1)} %get-tuple-element.56), calls=%async_computation | async-start | bytes 1572864 | tf_op jit(solution)/shard_map/all_to_all | solution.py:514
  39.8 71.9 %all-to-all-start.1 = ((bf16[16,24,8,128]{3,2,1,0:T(8,128)(2,1)}), bf16[16,24,8,128]{3,2,1,0:T(8,128)(2,1)S(1)}, u32[]{:S(2)}, u32[]{:S(2)}) async-start(bf16[16,24,8,128]{3,2,1,0:T(8,128)(2,1)} %reorder.2), calls=%async_computation.1 | async-start | bytes 1572864 | tf_op jit(solution)/shard_map/all_to_all | solution.py:514
  49.5 6.3 %collective-permute-start = (bf16[48,8,128]{2,1,0:T(8,128)(2,1)}, bf16[48,8,128]{2,1,0:T(8,128)(2,1)S(1)}, u32[]{:S(2)}, u32[]{:S(2)}) collective-permute-start(bf16[48,8,128]{2,1,0:T(8,128)(2,1)} %get-tuple-element.64), channel_id=1, source_target_pairs={{0,2},{1,3},{2,0},{3,1},{4,6},{5,7},{6,4},{7,5},{8,10},{9,11},{10,... | collective-permute-start | bytes 294920 | tf_op jit(solution)/shard_map/ppermute | solution.py:521
  50.9 9.8 %collective-permute-start.1 = (bf16[48,8,128]{2,1,0:T(8,128)(2,1)}, bf16[48,8,128]{2,1,0:T(8,128)(2,1)S(1)}, u32[]{:S(2)}, u32[]{:S(2)}) collective-permute-start(bf16[48,8,128]{2,1,0:T(8,128)(2,1)} %get-tuple-element.65), channel_id=1, source_target_pairs={{0,4},{1,5},{2,6},{3,7},{4,0},{5,1},{6,2},{7,3},{8,12},{9,13},{10,... | collective-permute-start | bytes 294920 | tf_op jit(solution)/shard_map/ppermute | solution.py:521
  52.1 13.1 %collective-permute-start.2 = (bf16[48,8,128]{2,1,0:T(8,128)(2,1)}, bf16[48,8,128]{2,1,0:T(8,128)(2,1)S(1)}, u32[]{:S(2)}, u32[]{:S(2)}) collective-permute-start(bf16[48,8,128]{2,1,0:T(8,128)(2,1)} %get-tuple-element.66), channel_id=1, source_target_pairs={{0,6},{1,7},{2,4},{3,5},{4,2},{5,3},{6,0},{7,1},{8,14},{9,15},{10,... | collective-permute-start | bytes 294920 | tf_op jit(solution)/shard_map/ppermute | solution.py:521
  52.2 23.6 %collective-permute-start.3 = (bf16[48,8,128]{2,1,0:T(8,128)(2,1)}, bf16[48,8,128]{2,1,0:T(8,128)(2,1)S(1)}, u32[]{:S(2)}, u32[]{:S(2)}) collective-permute-start(bf16[48,8,128]{2,1,0:T(8,128)(2,1)} %get-tuple-element.67), channel_id=1, source_target_pairs={{0,8},{1,9},{2,10},{3,11},{4,12},{5,13},{6,14},{7,15},{8,0},{9,1},... | collective-permute-start | bytes 294920 | tf_op jit(solution)/shard_map/ppermute | solution.py:521
  54.4 24.4 %collective-permute-start.4 = (bf16[48,8,128]{2,1,0:T(8,128)(2,1)}, bf16[48,8,128]{2,1,0:T(8,128)(2,1)S(1)}, u32[]{:S(2)}, u32[]{:S(2)}) collective-permute-start(bf16[48,8,128]{2,1,0:T(8,128)(2,1)} %get-tuple-element.68), channel_id=1, source_target_pairs={{0,10},{1,11},{2,8},{3,9},{4,14},{5,15},{6,12},{7,13},{8,2},{9,3},... | collective-permute-start | bytes 294920 | tf_op jit(solution)/shard_map/ppermute | solution.py:521
  55.8 23.0 %collective-permute-start.5 = (bf16[48,8,128]{2,1,0:T(8,128)(2,1)}, bf16[48,8,128]{2,1,0:T(8,128)(2,1)S(1)}, u32[]{:S(2)}, u32[]{:S(2)}) collective-permute-start(bf16[48,8,128]{2,1,0:T(8,128)(2,1)} %get-tuple-element.69), channel_id=1, source_target_pairs={{0,12},{1,13},{2,14},{3,15},{4,8},{5,9},{6,10},{7,11},{8,4},{9,5},... | collective-permute-start | bytes 294920 | tf_op jit(solution)/shard_map/ppermute | solution.py:521
  60.7 18.1 %collective-permute-start.6 = (bf16[48,8,128]{2,1,0:T(8,128)(2,1)}, bf16[48,8,128]{2,1,0:T(8,128)(2,1)S(1)}, u32[]{:S(2)}, u32[]{:S(2)}) collective-permute-start(bf16[48,8,128]{2,1,0:T(8,128)(2,1)} %get-tuple-element.70), channel_id=1, source_target_pairs={{0,14},{1,15},{2,12},{3,13},{4,10},{5,11},{6,8},{7,9},{8,6},{9,7},... | collective-permute-start | bytes 294920 | tf_op jit(solution)/shard_map/ppermute | solution.py:521
  78.8 0.9 copy-start
  80.8 3.5 %collective-permute-start.7 = (bf16[8,48,8,128]{3,2,1,0:T(8,128)(2,1)S(1)}, bf16[8,48,8,128]{3,2,1,0:T(8,128)(2,1)S(1)}, u32[]{:S(2)}, u32[]{:S(2)}) collective-permute-start(bf16[8,48,8,128]{3,2,1,0:T(8,128)(2,1)S(1)} %stack.2.own_ref), channel_id=1, source_target_pairs={{0,1},{1,0},{2,3},{3,2},{4,5},{5,4},{6,7},{7,6},{8,9},{9,8},{10,11... | collective-permute-start | bytes 2359304 | tf_op jit(solution)/shard_map/ppermute | solution.py:532
  86.1 0.6 copy-start.2
  86.7 10.5 %collective-permute-start.10 = (bf16[48,8,128]{2,1,0:T(8,128)(2,1)S(1)}, bf16[48,8,128]{2,1,0:T(8,128)(2,1)S(1)}, u32[]{:S(2)}, u32[]{:S(2)}) collective-permute-start(bf16[48,8,128]{2,1,0:T(8,128)(2,1)S(1)} %get-tuple-element.74), channel_id=1, source_target_pairs={{0,6},{1,7},{2,4},{3,5},{4,2},{5,3},{6,0},{7,1},{8,14},{9,15},{10,... | collective-permute-start | bytes 294920 | tf_op jit(solution)/shard_map/ppermute | solution.py:521
  90.7 13.5 %collective-permute-start.11 = (bf16[48,8,128]{2,1,0:T(8,128)(2,1)S(1)}, bf16[48,8,128]{2,1,0:T(8,128)(2,1)S(1)}, u32[]{:S(2)}, u32[]{:S(2)}) collective-permute-start(bf16[48,8,128]{2,1,0:T(8,128)(2,1)S(1)} %get-tuple-element.75), channel_id=1, source_target_pairs={{0,8},{1,9},{2,10},{3,11},{4,12},{5,13},{6,14},{7,15},{8,0},{9,1},... | collective-permute-start | bytes 294920 | tf_op jit(solution)/shard_map/ppermute | solution.py:521
  90.7 20.9 %collective-permute-start.12 = (bf16[48,8,128]{2,1,0:T(8,128)(2,1)S(1)}, bf16[48,8,128]{2,1,0:T(8,128)(2,1)S(1)}, u32[]{:S(2)}, u32[]{:S(2)}) collective-permute-start(bf16[48,8,128]{2,1,0:T(8,128)(2,1)S(1)} %get-tuple-element.76), channel_id=1, source_target_pairs={{0,10},{1,11},{2,8},{3,9},{4,14},{5,15},{6,12},{7,13},{8,2},{9,3},... | collective-permute-start | bytes 294920 | tf_op jit(solution)/shard_map/ppermute | solution.py:521
  93.9 17.7 %collective-permute-start.13 = (bf16[48,8,128]{2,1,0:T(8,128)(2,1)S(1)}, bf16[48,8,128]{2,1,0:T(8,128)(2,1)S(1)}, u32[]{:S(2)}, u32[]{:S(2)}) collective-permute-start(bf16[48,8,128]{2,1,0:T(8,128)(2,1)S(1)} %get-tuple-element.77), channel_id=1, source_target_pairs={{0,12},{1,13},{2,14},{3,15},{4,8},{5,9},{6,10},{7,11},{8,4},{9,5},... | collective-permute-start | bytes 294920 | tf_op jit(solution)/shard_map/ppermute | solution.py:521
  95.2 16.4 %collective-permute-start.14 = (bf16[48,8,128]{2,1,0:T(8,128)(2,1)S(1)}, bf16[48,8,128]{2,1,0:T(8,128)(2,1)S(1)}, u32[]{:S(2)}, u32[]{:S(2)}) collective-permute-start(bf16[48,8,128]{2,1,0:T(8,128)(2,1)S(1)} %get-tuple-element.78), channel_id=1, source_target_pairs={{0,14},{1,15},{2,12},{3,13},{4,10},{5,11},{6,8},{7,9},{8,6},{9,7},... | collective-permute-start | bytes 294920 | tf_op jit(solution)/shard_map/ppermute | solution.py:521
  97.2 14.3 %copy-start.5 = (bf16[48,8,128]{2,1,0:T(8,128)(2,1)}, bf16[48,8,128]{2,1,0:T(8,128)(2,1)S(1)}, u32[]{:S(2)}) copy-start(bf16[48,8,128]{2,1,0:T(8,128)(2,1)S(1)} %collective-permute-done.10.refs_3_) | copy-start | bytes 294916
  97.2 14.4 %collective-permute-start.8 = (bf16[48,8,128]{2,1,0:T(8,128)(2,1)S(1)}, bf16[48,8,128]{2,1,0:T(8,128)(2,1)S(1)}, u32[]{:S(2)}, u32[]{:S(2)}) collective-permute-start(bf16[48,8,128]{2,1,0:T(8,128)(2,1)S(1)} %get-tuple-element.72), channel_id=1, source_target_pairs={{0,2},{1,3},{2,0},{3,1},{4,6},{5,7},{6,4},{7,5},{8,10},{9,11},{10,... | collective-permute-start | bytes 294920 | tf_op jit(solution)/shard_map/ppermute | solution.py:521
  104.2 7.3 %copy-start.6 = (bf16[48,8,128]{2,1,0:T(8,128)(2,1)}, bf16[48,8,128]{2,1,0:T(8,128)(2,1)S(1)}, u32[]{:S(2)}) copy-start(bf16[48,8,128]{2,1,0:T(8,128)(2,1)S(1)} %collective-permute-done.11.refs_4_) | copy-start | bytes 294916
  104.2 7.4 %collective-permute-start.9 = (bf16[48,8,128]{2,1,0:T(8,128)(2,1)S(1)}, bf16[48,8,128]{2,1,0:T(8,128)(2,1)S(1)}, u32[]{:S(2)}, u32[]{:S(2)}) collective-permute-start(bf16[48,8,128]{2,1,0:T(8,128)(2,1)S(1)} %get-tuple-element.73), channel_id=1, source_target_pairs={{0,4},{1,5},{2,6},{3,7},{4,0},{5,1},{6,2},{7,3},{8,12},{9,13},{10,... | collective-permute-start | bytes 294920 | tf_op jit(solution)/shard_map/ppermute | solution.py:521
  111.6 0.6 copy-start.7
  111.6 0.7 copy-start.8
  111.6 0.7 copy-start.9
  111.7 0.7 copy-start.10
  111.7 0.7 copy-start.11
  111.7 0.9 copy-start.3
  120.5 25.0 %all-to-all-start.2 = ((bf16[16,24,8,128]{3,2,1,0:T(8,128)(2,1)}), bf16[16,24,8,128]{3,2,1,0:T(8,128)(2,1)S(1)}, u32[]{:S(2)}, u32[]{:S(2)}) async-start(bf16[16,24,8,128]{3,2,1,0:T(8,128)(2,1)} %get-tuple-element.79), calls=%async_computation.2 | async-start | bytes 1572864 | tf_op jit(solution)/shard_map/all_to_all | solution.py:514
  147.1 67.4 %all-to-all-start.3 = ((bf16[16,24,8,128]{3,2,1,0:T(8,128)(2,1)}), bf16[16,24,8,128]{3,2,1,0:T(8,128)(2,1)S(1)}, u32[]{:S(2)}, u32[]{:S(2)}) async-start(bf16[16,24,8,128]{3,2,1,0:T(8,128)(2,1)} %reorder.3), calls=%async_computation.3 | async-start | bytes 1572864 | tf_op jit(solution)/shard_map/all_to_all | solution.py:514
  156.8 6.3 %collective-permute-start.15 = (bf16[48,8,128]{2,1,0:T(8,128)(2,1)}, bf16[48,8,128]{2,1,0:T(8,128)(2,1)S(1)}, u32[]{:S(2)}, u32[]{:S(2)}) collective-permute-start(bf16[48,8,128]{2,1,0:T(8,128)(2,1)} %get-tuple-element.85), channel_id=1, source_target_pairs={{0,2},{1,3},{2,0},{3,1},{4,6},{5,7},{6,4},{7,5},{8,10},{9,11},{10,... | collective-permute-start | bytes 294920 | tf_op jit(solution)/shard_map/ppermute | solution.py:521
  158.2 9.8 %collective-permute-start.16 = (bf16[48,8,128]{2,1,0:T(8,128)(2,1)}, bf16[48,8,128]{2,1,0:T(8,128)(2,1)S(1)}, u32[]{:S(2)}, u32[]{:S(2)}) collective-permute-start(bf16[48,8,128]{2,1,0:T(8,128)(2,1)} %get-tuple-element.86), channel_id=1, source_target_pairs={{0,4},{1,5},{2,6},{3,7},{4,0},{5,1},{6,2},{7,3},{8,12},{9,13},{10,... | collective-permute-start | bytes 294920 | tf_op jit(solution)/shard_map/ppermute | solution.py:521
  159.4 13.2 %collective-permute-start.17 = (bf16[48,8,128]{2,1,0:T(8,128)(2,1)}, bf16[48,8,128]{2,1,0:T(8,128)(2,1)S(1)}, u32[]{:S(2)}, u32[]{:S(2)}) collective-permute-start(bf16[48,8,128]{2,1,0:T(8,128)(2,1)} %get-tuple-element.87), channel_id=1, source_target_pairs={{0,6},{1,7},{2,4},{3,5},{4,2},{5,3},{6,0},{7,1},{8,14},{9,15},{10,... | collective-permute-start | bytes 294920 | tf_op jit(solution)/shard_map/ppermute | solution.py:521
  159.5 23.7 %collective-permute-start.18 = (bf16[48,8,128]{2,1,0:T(8,128)(2,1)}, bf16[48,8,128]{2,1,0:T(8,128)(2,1)S(1)}, u32[]{:S(2)}, u32[]{:S(2)}) collective-permute-start(bf16[48,8,128]{2,1,0:T(8,128)(2,1)} %get-tuple-element.88), channel_id=1, source_target_pairs={{0,8},{1,9},{2,10},{3,11},{4,12},{5,13},{6,14},{7,15},{8,0},{9,1},... | collective-permute-start | bytes 294920 | tf_op jit(solution)/shard_map/ppermute | solution.py:521
  161.7 24.4 %collective-permute-start.19 = (bf16[48,8,128]{2,1,0:T(8,128)(2,1)}, bf16[48,8,128]{2,1,0:T(8,128)(2,1)S(1)}, u32[]{:S(2)}, u32[]{:S(2)}) collective-permute-start(bf16[48,8,128]{2,1,0:T(8,128)(2,1)} %get-tuple-element.89), channel_id=1, source_target_pairs={{0,10},{1,11},{2,8},{3,9},{4,14},{5,15},{6,12},{7,13},{8,2},{9,3},... | collective-permute-start | bytes 294920 | tf_op jit(solution)/shard_map/ppermute | solution.py:521
  163.0 23.1 %collective-permute-start.20 = (bf16[48,8,128]{2,1,0:T(8,128)(2,1)}, bf16[48,8,128]{2,1,0:T(8,128)(2,1)S(1)}, u32[]{:S(2)}, u32[]{:S(2)}) collective-permute-start(bf16[48,8,128]{2,1,0:T(8,128)(2,1)} %get-tuple-element.90), channel_id=1, source_target_pairs={{0,12},{1,13},{2,14},{3,15},{4,8},{5,9},{6,10},{7,11},{8,4},{9,5},... | collective-permute-start | bytes 294920 | tf_op jit(solution)/shard_map/ppermute | solution.py:521
  168.0 18.1 %collective-permute-start.21 = (bf16[48,8,128]{2,1,0:T(8,128)(2,1)}, bf16[48,8,128]{2,1,0:T(8,128)(2,1)S(1)}, u32[]{:S(2)}, u32[]{:S(2)}) collective-permute-start(bf16[48,8,128]{2,1,0:T(8,128)(2,1)} %get-tuple-element.91), channel_id=1, source_target_pairs={{0,14},{1,15},{2,12},{3,13},{4,10},{5,11},{6,8},{7,9},{8,6},{9,7},... | collective-permute-start | bytes 294920 | tf_op jit(solution)/shard_map/ppermute | solution.py:521
  186.1 0.9 copy-start.1
  188.1 3.5 %collective-permute-start.22 = (bf16[8,48,8,128]{3,2,1,0:T(8,128)(2,1)S(1)}, bf16[8,48,8,128]{3,2,1,0:T(8,128)(2,1)S(1)}, u32[]{:S(2)}, u32[]{:S(2)}) collective-permute-start(bf16[8,48,8,128]{3,2,1,0:T(8,128)(2,1)S(1)} %stack.3.own_ref), channel_id=1, source_target_pairs={{0,1},{1,0},{2,3},{3,2},{4,5},{5,4},{6,7},{7,6},{8,9},{9,8},{10,11... | collective-permute-start | bytes 2359304 | tf_op jit(solution)/shard_map/ppermute | solution.py:532
  193.4 7.6 %collective-permute-start.23 = (bf16[48,8,128]{2,1,0:T(8,128)(2,1)S(1)}, bf16[48,8,128]{2,1,0:T(8,128)(2,1)S(1)}, u32[]{:S(2)}, u32[]{:S(2)}) collective-permute-start(bf16[48,8,128]{2,1,0:T(8,128)(2,1)S(1)} %get-tuple-element.93), channel_id=1, source_target_pairs={{0,2},{1,3},{2,0},{3,1},{4,6},{5,7},{6,4},{7,5},{8,10},{9,11},{10,... | collective-permute-start | bytes 294920 | tf_op jit(solution)/shard_map/ppermute | solution.py:521
  193.8 8.4 %collective-permute-start.24 = (bf16[48,8,128]{2,1,0:T(8,128)(2,1)S(1)}, bf16[48,8,128]{2,1,0:T(8,128)(2,1)S(1)}, u32[]{:S(2)}, u32[]{:S(2)}) collective-permute-start(bf16[48,8,128]{2,1,0:T(8,128)(2,1)S(1)} %get-tuple-element.94), channel_id=1, source_target_pairs={{0,4},{1,5},{2,6},{3,7},{4,0},{5,1},{6,2},{7,3},{8,12},{9,13},{10,... | collective-permute-start | bytes 294920 | tf_op jit(solution)/shard_map/ppermute | solution.py:521
  197.7 8.2 %collective-permute-start.25 = (bf16[48,8,128]{2,1,0:T(8,128)(2,1)S(1)}, bf16[48,8,128]{2,1,0:T(8,128)(2,1)S(1)}, u32[]{:S(2)}, u32[]{:S(2)}) collective-permute-start(bf16[48,8,128]{2,1,0:T(8,128)(2,1)S(1)} %get-tuple-element.95), channel_id=1, source_target_pairs={{0,6},{1,7},{2,4},{3,5},{4,2},{5,3},{6,0},{7,1},{8,14},{9,15},{10,... | collective-permute-start | bytes 294920 | tf_op jit(solution)/shard_map/ppermute | solution.py:521
  198.6 7.3 %collective-permute-start.26 = (bf16[48,8,128]{2,1,0:T(8,128)(2,1)S(1)}, bf16[48,8,128]{2,1,0:T(8,128)(2,1)S(1)}, u32[]{:S(2)}, u32[]{:S(2)}) collective-permute-start(bf16[48,8,128]{2,1,0:T(8,128)(2,1)S(1)} %get-tuple-element.96), channel_id=1, source_target_pairs={{0,8},{1,9},{2,10},{3,11},{4,12},{5,13},{6,14},{7,15},{8,0},{9,1},... | collective-permute-start | bytes 294920 | tf_op jit(solution)/shard_map/ppermute | solution.py:521
  200.1 14.4 %collective-permute-start.27 = (bf16[48,8,128]{2,1,0:T(8,128)(2,1)S(1)}, bf16[48,8,128]{2,1,0:T(8,128)(2,1)S(1)}, u32[]{:S(2)}, u32[]{:S(2)}) collective-permute-start(bf16[48,8,128]{2,1,0:T(8,128)(2,1)S(1)} %get-tuple-element.97), channel_id=1, source_target_pairs={{0,10},{1,11},{2,8},{3,9},{4,14},{5,15},{6,12},{7,13},{8,2},{9,3},... | collective-permute-start | bytes 294920 | tf_op jit(solution)/shard_map/ppermute | solution.py:521
  201.0 13.5 %collective-permute-start.28 = (bf16[48,8,128]{2,1,0:T(8,128)(2,1)S(1)}, bf16[48,8,128]{2,1,0:T(8,128)(2,1)S(1)}, u32[]{:S(2)}, u32[]{:S(2)}) collective-permute-start(bf16[48,8,128]{2,1,0:T(8,128)(2,1)S(1)} %get-tuple-element.98), channel_id=1, source_target_pairs={{0,12},{1,13},{2,14},{3,15},{4,8},{5,9},{6,10},{7,11},{8,4},{9,5},... | collective-permute-start | bytes 294920 | tf_op jit(solution)/shard_map/ppermute | solution.py:521
  202.2 12.3 %collective-permute-start.29 = (bf16[48,8,128]{2,1,0:T(8,128)(2,1)S(1)}, bf16[48,8,128]{2,1,0:T(8,128)(2,1)S(1)}, u32[]{:S(2)}, u32[]{:S(2)}) collective-permute-start(bf16[48,8,128]{2,1,0:T(8,128)(2,1)S(1)} %get-tuple-element.99), channel_id=1, source_target_pairs={{0,14},{1,15},{2,12},{3,13},{4,10},{5,11},{6,8},{7,9},{8,6},{9,7},... | collective-permute-start | bytes 294920 | tf_op jit(solution)/shard_map/ppermute | solution.py:521

commit v8 on v7

--- a/solution.py
+++ b/solution.py
@@ -14,7 +14,7 @@
 MIB = 1 << 20
 STRIDE = SUB + 1
 FETCH_BLOCKS = 4
-FIRST_MIB, FETCH_MIB, LATER_MIB, LAST_MIB, SETTLE_MIB = 58, 58, 58, 58, 16
+FIRST_MIB, FETCH_MIB, LATER_MIB, LAST_MIB, SETTLE_MIB = 58, 58, 53, 58, 16
 F32, BF16 = jnp.float32, jnp.bfloat16
 HALF_ROOT = 0.7071067811865476
 PDF_SCALE = 0.3989422804014327
@@ -209,23 +209,25 @@
 
 
 def hand_over(slots, pieces, state, sent):
-    packed, kept = sent[0], sent[1:5]
-    pack(state[:2], slots[2 * pieces], packed)
-    for ref, held in zip(kept, state):
-        ref[...] = held[...].astype(BF16)
+    pack(state[:2], slots[2 * pieces], sent[0])
+    for ref, held in zip(sent[1:3], state[2:]):
+        ref[...] = held[...]
 
 
 def later_visit_kernel(slots, pieces, block, me_ref, x_ref, y_ref, weights_ref, *refs):
-    moment_refs, sent, scratch = refs[:pieces], refs[pieces:][:5], refs[pieces + 5 :]
-    state, work, (packed, sems) = scratch[:4], scratch[4:7], scratch[7:9]
+    moment_refs, sent, scratch = refs[:pieces], refs[pieces:][:3], refs[pieces + 3 :]
+    state, work, (packed, sems, packed_weights, sem) = scratch[:4], scratch[4:7], scratch[7:]
     step = pl.program_id(0)
 
     @pl.when(step == 0)
     def _():
+        load = pltpu.make_async_copy(weights_ref, packed_weights, sem)
+        load.start()
         copies = collect(me_ref, moment_refs, packed, sems)
         for copy in copies:
             copy.start()
-        unpack(weights_ref, slots[2 * pieces], state[:2])
+        load.wait()
+        unpack(packed_weights, slots[2 * pieces], state[:2])
         for copy in copies:
             copy.wait()
         unpack(packed, slots[pieces], state[2:])
@@ -240,7 +242,7 @@
 
 
 def first_visit_kernel(slots, pieces, block, picks_ref, x_ref, y_ref, *refs):
-    model, sent, scratch = refs[:4], refs[4:11], refs[11:]
+    model, sent, scratch = refs[:4], refs[4:9], refs[9:]
     state, work, batch = scratch[:4], scratch[4:7], scratch[7:9]
     held, table, picked, sems, model_sems = scratch[9:]
     step = pl.program_id(0)
@@ -264,12 +266,14 @@
     @pl.when(step == pl.num_programs(0) - 1)
     def _():
         hand_over(slots, pieces, state, sent)
-        pick_rows(picks_ref, step + 1, 0, table, picked, sent[5:], 0)
+        pick_rows(picks_ref, step + 1, 0, table, picked, sent[3:], 0)
 
 
 def last_step_kernel(slots, pieces, block, me_ref, x_ref, y_ref, *refs):
-    cast_in, cast_out, min_, mout = refs[:4]
-    moment_refs, (hid, dout, dpre, new_in, new_out, packed, sems) = refs[4:-7], refs[-7:]
+    weights_ref, min_, mout = refs[:3]
+    moment_refs, (hid, dout, dpre, new_in, new_out, packed, sems) = refs[3:-9], refs[-9:-2]
+    cast_in, cast_out = refs[-2:]
+    unpack(weights_ref, slots[2 * pieces], (cast_in, cast_out))
     gradients(x_ref, y_ref, cast_in[...], cast_out[...], hid, dout, dpre, block)
     new_out[...] = momentum_out(hid, dout, mout)
     new_in[...] = momentum_in(x_ref, dpre, min_)
@@ -310,7 +314,7 @@
     pieces = min(slots)
     depth = 2 * width * hidden // (SUB * LANE)
     packed_shape = (2 * pieces, depth // (2 * pieces), SUB, LANE)
-    shapes = [packed_shape] + [(width, hidden), (hidden, width)] * 2 + more_outs
+    shapes = [packed_shape, (width, hidden), (hidden, width)] + more_outs
     return pl.pallas_call(
         functools.partial(kernel, slots, pieces, rows),
         grid=(steps - 1,),
@@ -344,7 +348,7 @@
         sizes,
         slots,
     )
-    return outs[0], outs[1:5], outs[5:]
+    return outs[0], outs[1:3], outs[3:]
 
 
 def piece_scratch(pieces, piece_shape):
@@ -357,9 +361,10 @@
     outs = visit(
         later_visit_kernel,
         (me, *batch, weights, *moments),
-        [SCALARS, batch_spec, batch_spec, whole(weights.shape)] + [ANYWHERE] * len(moments),
+        [SCALARS, batch_spec, batch_spec] + [ANYWHERE] * (1 + len(moments)),
         [],
-        piece_scratch(len(moments), moments[0].shape),
+        piece_scratch(len(moments), moments[0].shape)
+        + [pltpu.VMEM(weights.shape, BF16), pltpu.SemaphoreType.DMA],
         LATER_MIB,
         sizes,
         slots,
@@ -367,7 +372,7 @@
     return outs[0], outs[1:]
 
 
-def last_step(me, batch, kept, sizes, slots):
+def last_step(me, batch, weights, kept, sizes, slots):
     _, rows, width, hidden = sizes
     pieces = min(slots)
     piece_shape = (2 * width * hidden // (SUB * LANE) // pieces, SUB, LANE)
@@ -376,7 +381,7 @@
     return pl.pallas_call(
         functools.partial(last_step_kernel, slots, pieces, rows),
         grid=(1,),
-        in_specs=[SCALARS, batch_spec, batch_spec] + [whole(part.shape) for part in kept],
+        in_specs=[SCALARS, batch_spec, batch_spec] + [whole(part.shape) for part in (weights, *kept)],
         out_specs=[ANYWHERE] * pieces,
         out_shape=[jax.ShapeDtypeStruct(piece_shape, BF16)] * pieces,
         scratch_shapes=[
@@ -384,11 +389,13 @@
             pltpu.VMEM((width, hidden), BF16),
             pltpu.VMEM((hidden, width), BF16),
             *piece_scratch(pieces, piece_shape),
+            pltpu.VMEM((width, hidden), BF16),
+            pltpu.VMEM((hidden, width), BF16),
         ],
         cost_estimate=step_cost(1, rows, width, hidden),
         compiler_params=pltpu.CompilerParams(vmem_limit_bytes=LAST_MIB * MIB),
         name="last",
-    )(me, *batch, *kept)
+    )(me, *batch, weights, *kept)
 
 
 def reorder_kernel(source_ref, packed_ref, out_ref, sems):
@@ -478,26 +485,41 @@
 
 
 def settle_kernel(slots, pieces, me_ref, weights_ref, *refs):
-    moment_refs, outs, (packed, sems) = refs[:pieces], refs[pieces:-2], refs[-2:]
+    moment_refs, outs, scratch = refs[:pieces], refs[pieces:][:4], refs[pieces + 4 :]
+    packed, sems, packed_weights, sem, out_sems = scratch[:5]
+    made = scratch[5:]
+    load = pltpu.make_async_copy(weights_ref, packed_weights, sem)
+    load.start()
     copies = collect(me_ref, moment_refs, packed, sems)
     for copy in copies:
         copy.start()
-    unpack(weights_ref, slots[2 * pieces], outs[:2])
+    stores = [
+        pltpu.make_async_copy(ref, out, out_sems.at[index])
+        for index, (ref, out) in enumerate(zip(made, outs))
+    ]
+    load.wait()
+    unpack(packed_weights, slots[2 * pieces], made[:2])
     for copy in copies:
         copy.wait()
-    unpack(packed, slots[pieces], outs[2:])
-    for weight, moment in zip(outs[:2], outs[2:]):
-        weight[...] = stepped(weight[...], moment[...])
+    unpack(packed, slots[pieces], made[2:])
+    for side in range(2):
+        stores[2 + side].start()
+        made[side][...] = stepped(made[side][...], made[2 + side][...])
+        stores[side].start()
+    for store in stores:
+        store.wait()
 
 
 def settle(me, weights, moments, slots, outs):
-    in_vmem = pl.BlockSpec(memory_space=pltpu.VMEM)
     return pl.pallas_call(
         functools.partial(settle_kernel, slots, len(moments)),
-        in_specs=[SCALARS, in_vmem] + [ANYWHERE] * len(moments),
-        out_specs=[in_vmem] * len(outs),
+        in_specs=[SCALARS] + [ANYWHERE] * (1 + len(moments)),
+        out_specs=[ANYWHERE] * len(outs),
         out_shape=[jax.ShapeDtypeStruct(shape, dtype) for shape, dtype in outs],
-        scratch_shapes=piece_scratch(len(moments), moments[0].shape),
+        scratch_shapes=piece_scratch(len(moments), moments[0].shape)
+        + [pltpu.VMEM(weights.shape, BF16), pltpu.SemaphoreType.DMA]
+        + [pltpu.SemaphoreType.DMA((len(outs),))]
+        + [pltpu.VMEM(shape, dtype) for shape, dtype in outs],
         compiler_params=pltpu.CompilerParams(vmem_limit_bytes=SETTLE_MIB * MIB),
         name="settle",
     )(me, weights, *moments)
@@ -517,14 +539,14 @@
 def spread(parts, devices):
     moved = [None] * len(parts)
     moved[0] = parts[0]
-    for k in sorted(range(1, len(parts)), reverse=True):
+    for k in sorted(range(1, len(parts)), key=lambda k: (k >= len(parts) // 2, -k)):
         moved[k] = lax.ppermute(parts[k], "hop", [(i, i ^ (2 * k)) for i in range(devices)])
     return moved
 
 
 def move(weights, me, batch, kept, source, devices, sizes, slots):
+    moments = last_step(me, batch, weights, kept, sizes, slots)
     weights = exchange(weights)
-    moments = last_step(me, batch, kept, sizes, slots)
     moments = spread(moments, devices)
     weights = reorder(weights, source)
     weights = exchange(weights)

time: 221 us -> 217 us (0.982)
  waiting for transfers between devices: 89.4 us -> 85.6 us
    ppermute x28, waiting for transfers between devices: 48.5 us -> 44.8 us  [spread(): lax.ppermute(parts[k], 'hop', [(i, i ^ 2 * k) for i in range(devices)])]
where the time goes in v8:
time: 217 us; the launch traced here: 214 us
  waiting for transfers between devices  85.6 us (39%)
  starting transfers between devices  78.2 us (36%)
  Pallas kernels  46.2 us (21%)
  local copies, waits for them, and re-layouts  2.67 us (1%)
    ppermute x28, starting transfers between devices, spread(): lax.ppermute(parts[k], 'hop', [(i, i ^ 2 * k) for i in range(devices)])  48.6 us
    ppermute x28, waiting for transfers between devices, spread(): lax.ppermute(parts[k], 'hop', [(i, i ^ 2 * k) for i in range(devices)])  44.8 us
    all_to_all x4, waiting for transfers between devices, exchange(): lax.all_to_all(packed, 'hop', split_axis=0, concat_axis=0, tiled=True)  37 us
    all_to_all x4, starting transfers between devices, exchange(): lax.all_to_all(packed, 'hop', split_axis=0, concat_axis=0, tiled=True)  26.4 us
    pallas_call x2, Pallas kernels, visit(): pl.pallas_call(functools.partial(kernel, slots, pieces, rows), grid=(step...  18.8 us
    pallas_call x2, Pallas kernels, last_step(): pl.pallas_call(functools.partial(last_step_kernel, slots, pieces, rows),...  8.51 us
    pallas_call x1, Pallas kernels, fetch(): pl.pallas_call(functools.partial(fetch_kernel, visit_index), in_specs=[SC...  7.34 us
  transfers between devices with their start and end apart: 34, of which 17 were waited for; matrix products, arithmetic and copies ran while one was open for 0% of the time, Pallas kernels for 10%

profile of v8, /device:TPU:1, one launch (start us, length us, event | category | flops | bytes accessed | tf_op | source)
XLA Modules:
  0.0 213.9 jit_solution(3953730902000273984)
XLA Ops:
  0.6 11.3 %visit.2 = (bf16[16,24,8,128]{3,2,1,0:T(8,128)(2,1)}, bf16[384,512]{1,0:T(8,128)(2,1)}, bf16[512,384]{1,0:T(8,128)(2,1)}, bf16[512,384]{1,0:T(8,128)(2,1)}, bf16[512,384]{1,0:T(8,128)(2,1)}) custom-call(s32[3,4,2,128]{3,2,1,0:T(2,128)} %bitcast.20, bf16[4096,384]{1,0:T(8,128)(2,1)} %x_ref.3, bf16[4096,384]{1,0:T(8,128)(2,1)} %y_ref.3, f32[384,512]{1,0:T(8,128)} %bitcast.16, ...), custom_call_target="tpu_custom_call" | custom-call | flops 2013265920 | bytes 4718592 | tf_op jit(solution)/shard_map/visit/pallas_call | solution.py:318
  12.0 7.3 %all-to-all-start = ((bf16[16,24,8,128]{3,2,1,0:T(8,128)(2,1)}), bf16[16,24,8,128]{3,2,1,0:T(8,128)(2,1)S(1)}, u32[]{:S(2)}, u32[]{:S(2)}) async-start(bf16[16,24,8,128]{3,2,1,0:T(8,128)(2,1)} %get-tuple-element.52.refs_0_), calls=%async_computation | async-start | bytes 1572864 | tf_op jit(solution)/shard_map/all_to_all | solution.py:536
  19.4 18.5 %all-to-all-done.packed_ref = bf16[16,24,8,128]{3,2,1,0:T(8,128)(2,1)S(1)} async-done(((bf16[16,24,8,128]{3,2,1,0:T(8,128)(2,1)}), bf16[16,24,8,128]{3,2,1,0:T(8,128)(2,1)S(1)}, u32[]{:S(2)}, u32[]{:S(2)}) %all-to-all-start) | async-done | bytes 786464 | tf_op jit(solution)/shard_map/all_to_all | solution.py:536
  37.9 1.5 reorder.2
  39.5 5.5 %all-to-all-start.1 = ((bf16[16,24,8,128]{3,2,1,0:T(8,128)(2,1)}), bf16[16,24,8,128]{3,2,1,0:T(8,128)(2,1)S(1)}, u32[]{:S(2)}, u32[]{:S(2)}) async-start(bf16[16,24,8,128]{3,2,1,0:T(8,128)(2,1)} %reorder.2), calls=%async_computation.1 | async-start | bytes 1572864 | tf_op jit(solution)/shard_map/all_to_all | solution.py:536
  44.9 4.3 %last.2 = (bf16[48,8,128]{2,1,0:T(8,128)(2,1)}, bf16[48,8,128]{2,1,0:T(8,128)(2,1)}, bf16[48,8,128]{2,1,0:T(8,128)(2,1)}, bf16[48,8,128]{2,1,0:T(8,128)(2,1)}, b...) custom-call(s32[1]{0:T(128)} %bitcast.me_ref, ...), custom_call_target="tpu_custom_call" | custom-call | flops 1006632960 | bytes 3932160 | tf_op jit(solution)/shard_map/last/pallas_call | solution.py:381
  49.2 1.4 collective-permute-start
  50.6 1.2 collective-permute-start.1
  51.9 2.3 %collective-permute-start.3 = (bf16[48,8,128]{2,1,0:T(8,128)(2,1)}, bf16[48,8,128]{2,1,0:T(8,128)(2,1)S(1)}, u32[]{:S(2)}, u32[]{:S(2)}) collective-permute-start(bf16[48,8,128]{2,1,0:T(8,128)(2,1)} %get-tuple-element.61), channel_id=1, source_target_pairs={{0,8},{1,9},{2,10},{3,11},{4,12},{5,13},{6,14},{7,15},{8,0},{9,1},... | collective-permute-start | bytes 294920 | tf_op jit(solution)/shard_map/ppermute | solution.py:543
  54.2 1.2 collective-permute-start.4
  55.6 2.8 %collective-permute-start.5 = (bf16[48,8,128]{2,1,0:T(8,128)(2,1)}, bf16[48,8,128]{2,1,0:T(8,128)(2,1)S(1)}, u32[]{:S(2)}, u32[]{:S(2)}) collective-permute-start(bf16[48,8,128]{2,1,0:T(8,128)(2,1)} %get-tuple-element.63), channel_id=1, source_target_pairs={{0,12},{1,13},{2,14},{3,15},{4,8},{5,9},{6,10},{7,11},{8,4},{9,5},... | collective-permute-start | bytes 294920 | tf_op jit(solution)/shard_map/ppermute | solution.py:543
  58.3 2.1 collective-permute-done.1.refs_2_
  60.4 3.7 %collective-permute-start.6 = (bf16[48,8,128]{2,1,0:T(8,128)(2,1)}, bf16[48,8,128]{2,1,0:T(8,128)(2,1)S(1)}, u32[]{:S(2)}, u32[]{:S(2)}) collective-permute-start(bf16[48,8,128]{2,1,0:T(8,128)(2,1)} %get-tuple-element.64), channel_id=1, source_target_pairs={{0,14},{1,15},{2,12},{3,13},{4,10},{5,11},{6,8},{7,9},{8,6},{9,7},... | collective-permute-start | bytes 294920 | tf_op jit(solution)/shard_map/ppermute | solution.py:543
  64.9 10.6 %collective-permute-done.3.refs_4_ = bf16[48,8,128]{2,1,0:T(8,128)(2,1)S(1)} collective-permute-done((bf16[48,8,128]{2,1,0:T(8,128)(2,1)}, bf16[48,8,128]{2,1,0:T(8,128)(2,1)S(1)}, u32[]{:S(2)}, u32[]{:S(2)}) %collective-permute-start.3) | collective-permute-done | bytes 98336 | tf_op jit(solution)/shard_map/ppermute | solution.py:543
  75.5 3.0 %collective-permute-done.4.refs_5_ = bf16[48,8,128]{2,1,0:T(8,128)(2,1)S(1)} collective-permute-done((bf16[48,8,128]{2,1,0:T(8,128)(2,1)}, bf16[48,8,128]{2,1,0:T(8,128)(2,1)S(1)}, u32[]{:S(2)}, u32[]{:S(2)}) %collective-permute-start.4) | collective-permute-done | bytes 98336 | tf_op jit(solution)/shard_map/ppermute | solution.py:543
  80.5 1.6 collective-permute-start.7
  82.1 1.9 collective-permute-done.7.partner_ref
  84.0 1.8 route.2
  86.2 3.9 %collective-permute-start.9 = (bf16[48,8,128]{2,1,0:T(8,128)(2,1)S(1)}, bf16[48,8,128]{2,1,0:T(8,128)(2,1)S(1)}, u32[]{:S(2)}, u32[]{:S(2)}) collective-permute-start(bf16[48,8,128]{2,1,0:T(8,128)(2,1)S(1)} %get-tuple-element.67), channel_id=1, source_target_pairs={{0,4},{1,5},{2,6},{3,7},{4,0},{5,1},{6,2},{7,3},{8,12},{9,13},{10,... | collective-permute-start | bytes 294920 | tf_op jit(solution)/shard_map/ppermute | solution.py:543
  91.0 1.5 collective-permute-start.11
  93.4 1.2 collective-permute-start.13
  94.6 2.9 %collective-permute-start.14 = (bf16[48,8,128]{2,1,0:T(8,128)(2,1)S(1)}, bf16[48,8,128]{2,1,0:T(8,128)(2,1)S(1)}, u32[]{:S(2)}, u32[]{:S(2)}) collective-permute-start(bf16[48,8,128]{2,1,0:T(8,128)(2,1)S(1)} %get-tuple-element.72), channel_id=1, source_target_pairs={{0,14},{1,15},{2,12},{3,13},{4,10},{5,11},{6,8},{7,9},{8,6},{9,7},... | collective-permute-start | bytes 294920 | tf_op jit(solution)/shard_map/ppermute | solution.py:543
  97.5 7.3 %fetch.1 = (bf16[1536,384]{1,0:T(8,128)(2,1)}, bf16[1536,384]{1,0:T(8,128)(2,1)}) custom-call(s32[3,4,2,128]{3,2,1,0:T(2,128)} %bitcast.21, bf16[4096,384]{1,0:T(8,128)(2,1)} %x_ref.3, bf16[4096,384]{1,0:T(8,128)(2,1)} %y_ref.3), custom_call_target="tpu_custom_call" | custom-call | bytes 6291456 | tf_op jit(solution)/shard_map/fetch/pallas_call | solution.py:95
  104.9 2.0 collective-permute-done.12.refs_5_
  107.8 7.5 %visit.3 = (bf16[16,24,8,128]{3,2,1,0:T(8,128)(2,1)}, bf16[384,512]{1,0:T(8,128)(2,1)}, bf16[512,384]{1,0:T(8,128)(2,1)}) custom-call(s32[1]{0:T(128)} %bitcast.me_ref, bf16[1536,384]{1,0:T(8,128)(2,1)} %get-tuple-element.50.x_ref, bf16[1536,384]{1,0:T(8,128)(2,1)} %get-tuple-element.51.y_ref, bf16[16,24,8,128]{3,2,1,0:T(8,128)(2,1)} %copy-done.2, ...), custom_call_target="tpu_custom_call" | custom-call | flops 2013265920 | bytes 4718592 | tf_op jit(solution)/shard_map/visit/pallas_call | solution.py:318
  115.2 8.1 %all-to-all-start.2 = ((bf16[16,24,8,128]{3,2,1,0:T(8,128)(2,1)}), bf16[16,24,8,128]{3,2,1,0:T(8,128)(2,1)S(1)}, u32[]{:S(2)}, u32[]{:S(2)}) async-start(bf16[16,24,8,128]{3,2,1,0:T(8,128)(2,1)} %get-tuple-element.73.refs_0_), calls=%async_computation.2 | async-start | bytes 1572864 | tf_op jit(solution)/shard_map/all_to_all | solution.py:536
  123.5 18.5 %all-to-all-done.2.packed_ref = bf16[16,24,8,128]{3,2,1,0:T(8,128)(2,1)S(1)} async-done(((bf16[16,24,8,128]{3,2,1,0:T(8,128)(2,1)}), bf16[16,24,8,128]{3,2,1,0:T(8,128)(2,1)S(1)}, u32[]{:S(2)}, u32[]{:S(2)}) %all-to-all-start.2) | async-done | bytes 786464 | tf_op jit(solution)/shard_map/all_to_all | solution.py:536
  142.0 1.5 reorder.3
  143.5 5.5 %all-to-all-start.3 = ((bf16[16,24,8,128]{3,2,1,0:T(8,128)(2,1)}), bf16[16,24,8,128]{3,2,1,0:T(8,128)(2,1)S(1)}, u32[]{:S(2)}, u32[]{:S(2)}) async-start(bf16[16,24,8,128]{3,2,1,0:T(8,128)(2,1)} %reorder.3), calls=%async_computation.3 | async-start | bytes 1572864 | tf_op jit(solution)/shard_map/all_to_all | solution.py:536
  149.0 4.3 %last.3 = (bf16[48,8,128]{2,1,0:T(8,128)(2,1)}, bf16[48,8,128]{2,1,0:T(8,128)(2,1)}, bf16[48,8,128]{2,1,0:T(8,128)(2,1)}, bf16[48,8,128]{2,1,0:T(8,128)(2,1)}, b...) custom-call(s32[1]{0:T(128)} %bitcast.me_ref, ...), custom_call_target="tpu_custom_call" | custom-call | flops 1006632960 | bytes 3932160 | tf_op jit(solution)/shard_map/last/pallas_call | solution.py:381
  153.3 1.4 collective-permute-start.15
  154.7 1.2 collective-permute-start.16
  156.0 2.3 %collective-permute-start.18 = (bf16[48,8,128]{2,1,0:T(8,128)(2,1)}, bf16[48,8,128]{2,1,0:T(8,128)(2,1)S(1)}, u32[]{:S(2)}, u32[]{:S(2)}) collective-permute-start(bf16[48,8,128]{2,1,0:T(8,128)(2,1)} %get-tuple-element.80), channel_id=1, source_target_pairs={{0,8},{1,9},{2,10},{3,11},{4,12},{5,13},{6,14},{7,15},{8,0},{9,1},... | collective-permute-start | bytes 294920 | tf_op jit(solution)/shard_map/ppermute | solution.py:543
  158.2 1.2 collective-permute-start.19
  159.7 2.7 %collective-permute-start.20 = (bf16[48,8,128]{2,1,0:T(8,128)(2,1)}, bf16[48,8,128]{2,1,0:T(8,128)(2,1)S(1)}, u32[]{:S(2)}, u32[]{:S(2)}) collective-permute-start(bf16[48,8,128]{2,1,0:T(8,128)(2,1)} %get-tuple-element.82), channel_id=1, source_target_pairs={{0,12},{1,13},{2,14},{3,15},{4,8},{5,9},{6,10},{7,11},{8,4},{9,5},... | collective-permute-start | bytes 294920 | tf_op jit(solution)/shard_map/ppermute | solution.py:543
  162.4 2.0 collective-permute-done.16.refs_2_
  164.5 3.7 %collective-permute-start.21 = (bf16[48,8,128]{2,1,0:T(8,128)(2,1)}, bf16[48,8,128]{2,1,0:T(8,128)(2,1)S(1)}, u32[]{:S(2)}, u32[]{:S(2)}) collective-permute-start(bf16[48,8,128]{2,1,0:T(8,128)(2,1)} %get-tuple-element.83), channel_id=1, source_target_pairs={{0,14},{1,15},{2,12},{3,13},{4,10},{5,11},{6,8},{7,9},{8,6},{9,7},... | collective-permute-start | bytes 294920 | tf_op jit(solution)/shard_map/ppermute | solution.py:543
  169.0 10.6 %collective-permute-done.18.refs_4_ = bf16[48,8,128]{2,1,0:T(8,128)(2,1)S(1)} collective-permute-done((bf16[48,8,128]{2,1,0:T(8,128)(2,1)}, bf16[48,8,128]{2,1,0:T(8,128)(2,1)S(1)}, u32[]{:S(2)}, u32[]{:S(2)}) %collective-permute-start.18) | collective-permute-done | bytes 98336 | tf_op jit(solution)/shard_map/ppermute | solution.py:543
  179.6 3.0 %collective-permute-done.19.refs_5_ = bf16[48,8,128]{2,1,0:T(8,128)(2,1)S(1)} collective-permute-done((bf16[48,8,128]{2,1,0:T(8,128)(2,1)}, bf16[48,8,128]{2,1,0:T(8,128)(2,1)S(1)}, u32[]{:S(2)}, u32[]{:S(2)}) %collective-permute-start.19) | collective-permute-done | bytes 98336 | tf_op jit(solution)/shard_map/ppermute | solution.py:543
  184.5 1.6 collective-permute-start.22
  186.1 1.9 collective-permute-done.22.partner_ref
  188.1 1.8 route.3
  190.2 3.9 %collective-permute-start.24 = (bf16[48,8,128]{2,1,0:T(8,128)(2,1)S(1)}, bf16[48,8,128]{2,1,0:T(8,128)(2,1)S(1)}, u32[]{:S(2)}, u32[]{:S(2)}) collective-permute-start(bf16[48,8,128]{2,1,0:T(8,128)(2,1)S(1)} %get-tuple-element.86), channel_id=1, source_target_pairs={{0,4},{1,5},{2,6},{3,7},{4,0},{5,1},{6,2},{7,3},{8,12},{9,13},{10,... | collective-permute-start | bytes 294920 | tf_op jit(solution)/shard_map/ppermute | solution.py:543
  195.0 1.5 collective-permute-start.26
  197.4 1.2 collective-permute-start.28
  198.6 2.9 %collective-permute-start.29 = (bf16[48,8,128]{2,1,0:T(8,128)(2,1)S(1)}, bf16[48,8,128]{2,1,0:T(8,128)(2,1)S(1)}, u32[]{:S(2)}, u32[]{:S(2)}) collective-permute-start(bf16[48,8,128]{2,1,0:T(8,128)(2,1)S(1)} %get-tuple-element.91), channel_id=1, source_target_pairs={{0,14},{1,15},{2,12},{3,13},{4,10},{5,11},{6,8},{7,9},{8,6},{9,7},... | collective-permute-start | bytes 294920 | tf_op jit(solution)/shard_map/ppermute | solution.py:543
  202.3 8.6 %collective-permute-done.27.refs_5_ = bf16[48,8,128]{2,1,0:T(8,128)(2,1)S(1)} collective-permute-done((bf16[48,8,128]{2,1,0:T(8,128)(2,1)S(1)}, bf16[48,8,128]{2,1,0:T(8,128)(2,1)S(1)}, u32[]{:S(2)}, u32[]{:S(2)}) %collective-permute-start.27) | collective-permute-done | bytes 98336 | tf_op jit(solution)/shard_map/ppermute | solution.py:543
  210.9 2.8 %settle.1 = (f32[384,512]{1,0:T(8,128)}, f32[512,384]{1,0:T(8,128)}, bf16[384,512]{1,0:T(8,128)(2,1)}, bf16[512,384]{1,0:T(8,128)(2,1)}) custom-call(s32[1]{0:T(128)} %bitcast.me_ref, bf16[16,24,8,128]{3,2,1,0:T(8,128)(2,1)S(1)} %all-to-all-done.3.weights_ref, bf16[48,8,128]{2,1,0:T(8,128)(2,1)S(1)} %get-tuple-element.84.refs_0_, ...), custom_call_target="tpu_custom_call" | custom-call | tf_op jit(solution)/shard_map/settle/pallas_call | solution.py:514
  (43 shorter events, 12.3 us)
Async XLA Ops:
  0.6 18.7 %copy-start.3 = (s32[2,16]{1,0:T(2,128)S(1)}, s32[2,16]{1,0:T(2,128)}, u32[]{:S(2)}) copy-start(s32[2,16]{1,0:T(2,128)} %param.11) | copy-start | bytes 388
  12.0 26.0 %all-to-all-start = ((bf16[16,24,8,128]{3,2,1,0:T(8,128)(2,1)}), bf16[16,24,8,128]{3,2,1,0:T(8,128)(2,1)S(1)}, u32[]{:S(2)}, u32[]{:S(2)}) async-start(bf16[16,24,8,128]{3,2,1,0:T(8,128)(2,1)} %get-tuple-element.52.refs_0_), calls=%async_computation | async-start | bytes 1572864 | tf_op jit(solution)/shard_map/all_to_all | solution.py:536
  39.5 67.4 %all-to-all-start.1 = ((bf16[16,24,8,128]{3,2,1,0:T(8,128)(2,1)}), bf16[16,24,8,128]{3,2,1,0:T(8,128)(2,1)S(1)}, u32[]{:S(2)}, u32[]{:S(2)}) async-start(bf16[16,24,8,128]{3,2,1,0:T(8,128)(2,1)} %reorder.2), calls=%async_computation.1 | async-start | bytes 1572864 | tf_op jit(solution)/shard_map/all_to_all | solution.py:536
  49.2 6.4 %collective-permute-start = (bf16[48,8,128]{2,1,0:T(8,128)(2,1)}, bf16[48,8,128]{2,1,0:T(8,128)(2,1)S(1)}, u32[]{:S(2)}, u32[]{:S(2)}) collective-permute-start(bf16[48,8,128]{2,1,0:T(8,128)(2,1)} %get-tuple-element.58), channel_id=1, source_target_pairs={{0,2},{1,3},{2,0},{3,1},{4,6},{5,7},{6,4},{7,5},{8,10},{9,11},{10,... | collective-permute-start | bytes 294920 | tf_op jit(solution)/shard_map/ppermute | solution.py:543
  50.6 9.8 %collective-permute-start.1 = (bf16[48,8,128]{2,1,0:T(8,128)(2,1)}, bf16[48,8,128]{2,1,0:T(8,128)(2,1)S(1)}, u32[]{:S(2)}, u32[]{:S(2)}) collective-permute-start(bf16[48,8,128]{2,1,0:T(8,128)(2,1)} %get-tuple-element.59), channel_id=1, source_target_pairs={{0,4},{1,5},{2,6},{3,7},{4,0},{5,1},{6,2},{7,3},{8,12},{9,13},{10,... | collective-permute-start | bytes 294920 | tf_op jit(solution)/shard_map/ppermute | solution.py:543
  51.8 13.1 %collective-permute-start.2 = (bf16[48,8,128]{2,1,0:T(8,128)(2,1)}, bf16[48,8,128]{2,1,0:T(8,128)(2,1)S(1)}, u32[]{:S(2)}, u32[]{:S(2)}) collective-permute-start(bf16[48,8,128]{2,1,0:T(8,128)(2,1)} %get-tuple-element.60), channel_id=1, source_target_pairs={{0,6},{1,7},{2,4},{3,5},{4,2},{5,3},{6,0},{7,1},{8,14},{9,15},{10,... | collective-permute-start | bytes 294920 | tf_op jit(solution)/shard_map/ppermute | solution.py:543
  51.9 23.6 %collective-permute-start.3 = (bf16[48,8,128]{2,1,0:T(8,128)(2,1)}, bf16[48,8,128]{2,1,0:T(8,128)(2,1)S(1)}, u32[]{:S(2)}, u32[]{:S(2)}) collective-permute-start(bf16[48,8,128]{2,1,0:T(8,128)(2,1)} %get-tuple-element.61), channel_id=1, source_target_pairs={{0,8},{1,9},{2,10},{3,11},{4,12},{5,13},{6,14},{7,15},{8,0},{9,1},... | collective-permute-start | bytes 294920 | tf_op jit(solution)/shard_map/ppermute | solution.py:543
  54.2 24.3 %collective-permute-start.4 = (bf16[48,8,128]{2,1,0:T(8,128)(2,1)}, bf16[48,8,128]{2,1,0:T(8,128)(2,1)S(1)}, u32[]{:S(2)}, u32[]{:S(2)}) collective-permute-start(bf16[48,8,128]{2,1,0:T(8,128)(2,1)} %get-tuple-element.62), channel_id=1, source_target_pairs={{0,10},{1,11},{2,8},{3,9},{4,14},{5,15},{6,12},{7,13},{8,2},{9,3},... | collective-permute-start | bytes 294920 | tf_op jit(solution)/shard_map/ppermute | solution.py:543
  55.6 22.9 %collective-permute-start.5 = (bf16[48,8,128]{2,1,0:T(8,128)(2,1)}, bf16[48,8,128]{2,1,0:T(8,128)(2,1)S(1)}, u32[]{:S(2)}, u32[]{:S(2)}) collective-permute-start(bf16[48,8,128]{2,1,0:T(8,128)(2,1)} %get-tuple-element.63), channel_id=1, source_target_pairs={{0,12},{1,13},{2,14},{3,15},{4,8},{5,9},{6,10},{7,11},{8,4},{9,5},... | collective-permute-start | bytes 294920 | tf_op jit(solution)/shard_map/ppermute | solution.py:543
  60.4 18.1 %collective-permute-start.6 = (bf16[48,8,128]{2,1,0:T(8,128)(2,1)}, bf16[48,8,128]{2,1,0:T(8,128)(2,1)S(1)}, u32[]{:S(2)}, u32[]{:S(2)}) collective-permute-start(bf16[48,8,128]{2,1,0:T(8,128)(2,1)} %get-tuple-element.64), channel_id=1, source_target_pairs={{0,14},{1,15},{2,12},{3,13},{4,10},{5,11},{6,8},{7,9},{8,6},{9,7},... | collective-permute-start | bytes 294920 | tf_op jit(solution)/shard_map/ppermute | solution.py:543
  78.5 0.9 copy-start
  80.5 3.5 %collective-permute-start.7 = (bf16[8,48,8,128]{3,2,1,0:T(8,128)(2,1)S(1)}, bf16[8,48,8,128]{3,2,1,0:T(8,128)(2,1)S(1)}, u32[]{:S(2)}, u32[]{:S(2)}) collective-permute-start(bf16[8,48,8,128]{3,2,1,0:T(8,128)(2,1)S(1)} %stack.2.own_ref), channel_id=1, source_target_pairs={{0,1},{1,0},{2,3},{3,2},{4,5},{5,4},{6,7},{7,6},{8,9},{9,8},{10,11... | collective-permute-start | bytes 2359304 | tf_op jit(solution)/shard_map/ppermute | solution.py:554
  85.8 7.6 %collective-permute-start.8 = (bf16[48,8,128]{2,1,0:T(8,128)(2,1)S(1)}, bf16[48,8,128]{2,1,0:T(8,128)(2,1)S(1)}, u32[]{:S(2)}, u32[]{:S(2)}) collective-permute-start(bf16[48,8,128]{2,1,0:T(8,128)(2,1)S(1)} %get-tuple-element.66), channel_id=1, source_target_pairs={{0,2},{1,3},{2,0},{3,1},{4,6},{5,7},{6,4},{7,5},{8,10},{9,11},{10,... | collective-permute-start | bytes 294920 | tf_op jit(solution)/shard_map/ppermute | solution.py:543
  86.2 8.4 %collective-permute-start.9 = (bf16[48,8,128]{2,1,0:T(8,128)(2,1)S(1)}, bf16[48,8,128]{2,1,0:T(8,128)(2,1)S(1)}, u32[]{:S(2)}, u32[]{:S(2)}) collective-permute-start(bf16[48,8,128]{2,1,0:T(8,128)(2,1)S(1)} %get-tuple-element.67), channel_id=1, source_target_pairs={{0,4},{1,5},{2,6},{3,7},{4,0},{5,1},{6,2},{7,3},{8,12},{9,13},{10,... | collective-permute-start | bytes 294920 | tf_op jit(solution)/shard_map/ppermute | solution.py:543
  90.1 14.8 %collective-permute-start.10 = (bf16[48,8,128]{2,1,0:T(8,128)(2,1)S(1)}, bf16[48,8,128]{2,1,0:T(8,128)(2,1)S(1)}, u32[]{:S(2)}, u32[]{:S(2)}) collective-permute-start(bf16[48,8,128]{2,1,0:T(8,128)(2,1)S(1)} %get-tuple-element.68), channel_id=1, source_target_pairs={{0,6},{1,7},{2,4},{3,5},{4,2},{5,3},{6,0},{7,1},{8,14},{9,15},{10,... | collective-permute-start | bytes 294920 | tf_op jit(solution)/shard_map/ppermute | solution.py:543
  91.0 13.9 %collective-permute-start.11 = (bf16[48,8,128]{2,1,0:T(8,128)(2,1)S(1)}, bf16[48,8,128]{2,1,0:T(8,128)(2,1)S(1)}, u32[]{:S(2)}, u32[]{:S(2)}) collective-permute-start(bf16[48,8,128]{2,1,0:T(8,128)(2,1)S(1)} %get-tuple-element.69), channel_id=1, source_target_pairs={{0,8},{1,9},{2,10},{3,11},{4,12},{5,13},{6,14},{7,15},{8,0},{9,1},... | collective-permute-start | bytes 294920 | tf_op jit(solution)/shard_map/ppermute | solution.py:543
  92.5 14.4 %collective-permute-start.12 = (bf16[48,8,128]{2,1,0:T(8,128)(2,1)S(1)}, bf16[48,8,128]{2,1,0:T(8,128)(2,1)S(1)}, u32[]{:S(2)}, u32[]{:S(2)}) collective-permute-start(bf16[48,8,128]{2,1,0:T(8,128)(2,1)S(1)} %get-tuple-element.70), channel_id=1, source_target_pairs={{0,10},{1,11},{2,8},{3,9},{4,14},{5,15},{6,12},{7,13},{8,2},{9,3},... | collective-permute-start | bytes 294920 | tf_op jit(solution)/shard_map/ppermute | solution.py:543
  93.4 13.5 %collective-permute-start.13 = (bf16[48,8,128]{2,1,0:T(8,128)(2,1)S(1)}, bf16[48,8,128]{2,1,0:T(8,128)(2,1)S(1)}, u32[]{:S(2)}, u32[]{:S(2)}) collective-permute-start(bf16[48,8,128]{2,1,0:T(8,128)(2,1)S(1)} %get-tuple-element.71), channel_id=1, source_target_pairs={{0,12},{1,13},{2,14},{3,15},{4,8},{5,9},{6,10},{7,11},{8,4},{9,5},... | collective-permute-start | bytes 294920 | tf_op jit(solution)/shard_map/ppermute | solution.py:543
  94.6 12.3 %collective-permute-start.14 = (bf16[48,8,128]{2,1,0:T(8,128)(2,1)S(1)}, bf16[48,8,128]{2,1,0:T(8,128)(2,1)S(1)}, u32[]{:S(2)}, u32[]{:S(2)}) collective-permute-start(bf16[48,8,128]{2,1,0:T(8,128)(2,1)S(1)} %get-tuple-element.72), channel_id=1, source_target_pairs={{0,14},{1,15},{2,12},{3,13},{4,10},{5,11},{6,8},{7,9},{8,6},{9,7},... | collective-permute-start | bytes 294920 | tf_op jit(solution)/shard_map/ppermute | solution.py:543
  106.9 0.9 copy-start.2
  115.2 26.7 %all-to-all-start.2 = ((bf16[16,24,8,128]{3,2,1,0:T(8,128)(2,1)}), bf16[16,24,8,128]{3,2,1,0:T(8,128)(2,1)S(1)}, u32[]{:S(2)}, u32[]{:S(2)}) async-start(bf16[16,24,8,128]{3,2,1,0:T(8,128)(2,1)} %get-tuple-element.73.refs_0_), calls=%async_computation.2 | async-start | bytes 1572864 | tf_op jit(solution)/shard_map/all_to_all | solution.py:536
  143.5 67.4 %all-to-all-start.3 = ((bf16[16,24,8,128]{3,2,1,0:T(8,128)(2,1)}), bf16[16,24,8,128]{3,2,1,0:T(8,128)(2,1)S(1)}, u32[]{:S(2)}, u32[]{:S(2)}) async-start(bf16[16,24,8,128]{3,2,1,0:T(8,128)(2,1)} %reorder.3), calls=%async_computation.3 | async-start | bytes 1572864 | tf_op jit(solution)/shard_map/all_to_all | solution.py:536
  153.3 6.4 %collective-permute-start.15 = (bf16[48,8,128]{2,1,0:T(8,128)(2,1)}, bf16[48,8,128]{2,1,0:T(8,128)(2,1)S(1)}, u32[]{:S(2)}, u32[]{:S(2)}) collective-permute-start(bf16[48,8,128]{2,1,0:T(8,128)(2,1)} %get-tuple-element.77), channel_id=1, source_target_pairs={{0,2},{1,3},{2,0},{3,1},{4,6},{5,7},{6,4},{7,5},{8,10},{9,11},{10,... | collective-permute-start | bytes 294920 | tf_op jit(solution)/shard_map/ppermute | solution.py:543
  154.7 9.8 %collective-permute-start.16 = (bf16[48,8,128]{2,1,0:T(8,128)(2,1)}, bf16[48,8,128]{2,1,0:T(8,128)(2,1)S(1)}, u32[]{:S(2)}, u32[]{:S(2)}) collective-permute-start(bf16[48,8,128]{2,1,0:T(8,128)(2,1)} %get-tuple-element.78), channel_id=1, source_target_pairs={{0,4},{1,5},{2,6},{3,7},{4,0},{5,1},{6,2},{7,3},{8,12},{9,13},{10,... | collective-permute-start | bytes 294920 | tf_op jit(solution)/shard_map/ppermute | solution.py:543
  155.9 13.1 %collective-permute-start.17 = (bf16[48,8,128]{2,1,0:T(8,128)(2,1)}, bf16[48,8,128]{2,1,0:T(8,128)(2,1)S(1)}, u32[]{:S(2)}, u32[]{:S(2)}) collective-permute-start(bf16[48,8,128]{2,1,0:T(8,128)(2,1)} %get-tuple-element.79), channel_id=1, source_target_pairs={{0,6},{1,7},{2,4},{3,5},{4,2},{5,3},{6,0},{7,1},{8,14},{9,15},{10,... | collective-permute-start | bytes 294920 | tf_op jit(solution)/shard_map/ppermute | solution.py:543
  156.0 23.6 %collective-permute-start.18 = (bf16[48,8,128]{2,1,0:T(8,128)(2,1)}, bf16[48,8,128]{2,1,0:T(8,128)(2,1)S(1)}, u32[]{:S(2)}, u32[]{:S(2)}) collective-permute-start(bf16[48,8,128]{2,1,0:T(8,128)(2,1)} %get-tuple-element.80), channel_id=1, source_target_pairs={{0,8},{1,9},{2,10},{3,11},{4,12},{5,13},{6,14},{7,15},{8,0},{9,1},... | collective-permute-start | bytes 294920 | tf_op jit(solution)/shard_map/ppermute | solution.py:543
  158.2 24.3 %collective-permute-start.19 = (bf16[48,8,128]{2,1,0:T(8,128)(2,1)}, bf16[48,8,128]{2,1,0:T(8,128)(2,1)S(1)}, u32[]{:S(2)}, u32[]{:S(2)}) collective-permute-start(bf16[48,8,128]{2,1,0:T(8,128)(2,1)} %get-tuple-element.81), channel_id=1, source_target_pairs={{0,10},{1,11},{2,8},{3,9},{4,14},{5,15},{6,12},{7,13},{8,2},{9,3},... | collective-permute-start | bytes 294920 | tf_op jit(solution)/shard_map/ppermute | solution.py:543
  159.7 22.9 %collective-permute-start.20 = (bf16[48,8,128]{2,1,0:T(8,128)(2,1)}, bf16[48,8,128]{2,1,0:T(8,128)(2,1)S(1)}, u32[]{:S(2)}, u32[]{:S(2)}) collective-permute-start(bf16[48,8,128]{2,1,0:T(8,128)(2,1)} %get-tuple-element.82), channel_id=1, source_target_pairs={{0,12},{1,13},{2,14},{3,15},{4,8},{5,9},{6,10},{7,11},{8,4},{9,5},... | collective-permute-start | bytes 294920 | tf_op jit(solution)/shard_map/ppermute | solution.py:543
  164.5 18.1 %collective-permute-start.21 = (bf16[48,8,128]{2,1,0:T(8,128)(2,1)}, bf16[48,8,128]{2,1,0:T(8,128)(2,1)S(1)}, u32[]{:S(2)}, u32[]{:S(2)}) collective-permute-start(bf16[48,8,128]{2,1,0:T(8,128)(2,1)} %get-tuple-element.83), channel_id=1, source_target_pairs={{0,14},{1,15},{2,12},{3,13},{4,10},{5,11},{6,8},{7,9},{8,6},{9,7},... | collective-permute-start | bytes 294920 | tf_op jit(solution)/shard_map/ppermute | solution.py:543
  182.6 0.9 copy-start.1
  184.5 3.5 %collective-permute-start.22 = (bf16[8,48,8,128]{3,2,1,0:T(8,128)(2,1)S(1)}, bf16[8,48,8,128]{3,2,1,0:T(8,128)(2,1)S(1)}, u32[]{:S(2)}, u32[]{:S(2)}) collective-permute-start(bf16[8,48,8,128]{3,2,1,0:T(8,128)(2,1)S(1)} %stack.3.own_ref), channel_id=1, source_target_pairs={{0,1},{1,0},{2,3},{3,2},{4,5},{5,4},{6,7},{7,6},{8,9},{9,8},{10,11... | collective-permute-start | bytes 2359304 | tf_op jit(solution)/shard_map/ppermute | solution.py:554
  189.8 7.6 %collective-permute-start.23 = (bf16[48,8,128]{2,1,0:T(8,128)(2,1)S(1)}, bf16[48,8,128]{2,1,0:T(8,128)(2,1)S(1)}, u32[]{:S(2)}, u32[]{:S(2)}) collective-permute-start(bf16[48,8,128]{2,1,0:T(8,128)(2,1)S(1)} %get-tuple-element.85), channel_id=1, source_target_pairs={{0,2},{1,3},{2,0},{3,1},{4,6},{5,7},{6,4},{7,5},{8,10},{9,11},{10,... | collective-permute-start | bytes 294920 | tf_op jit(solution)/shard_map/ppermute | solution.py:543
  190.2 8.4 %collective-permute-start.24 = (bf16[48,8,128]{2,1,0:T(8,128)(2,1)S(1)}, bf16[48,8,128]{2,1,0:T(8,128)(2,1)S(1)}, u32[]{:S(2)}, u32[]{:S(2)}) collective-permute-start(bf16[48,8,128]{2,1,0:T(8,128)(2,1)S(1)} %get-tuple-element.86), channel_id=1, source_target_pairs={{0,4},{1,5},{2,6},{3,7},{4,0},{5,1},{6,2},{7,3},{8,12},{9,13},{10,... | collective-permute-start | bytes 294920 | tf_op jit(solution)/shard_map/ppermute | solution.py:543
  194.2 8.2 %collective-permute-start.25 = (bf16[48,8,128]{2,1,0:T(8,128)(2,1)S(1)}, bf16[48,8,128]{2,1,0:T(8,128)(2,1)S(1)}, u32[]{:S(2)}, u32[]{:S(2)}) collective-permute-start(bf16[48,8,128]{2,1,0:T(8,128)(2,1)S(1)} %get-tuple-element.87), channel_id=1, source_target_pairs={{0,6},{1,7},{2,4},{3,5},{4,2},{5,3},{6,0},{7,1},{8,14},{9,15},{10,... | collective-permute-start | bytes 294920 | tf_op jit(solution)/shard_map/ppermute | solution.py:543
  195.0 7.3 %collective-permute-start.26 = (bf16[48,8,128]{2,1,0:T(8,128)(2,1)S(1)}, bf16[48,8,128]{2,1,0:T(8,128)(2,1)S(1)}, u32[]{:S(2)}, u32[]{:S(2)}) collective-permute-start(bf16[48,8,128]{2,1,0:T(8,128)(2,1)S(1)} %get-tuple-element.88), channel_id=1, source_target_pairs={{0,8},{1,9},{2,10},{3,11},{4,12},{5,13},{6,14},{7,15},{8,0},{9,1},... | collective-permute-start | bytes 294920 | tf_op jit(solution)/shard_map/ppermute | solution.py:543
  196.6 14.4 %collective-permute-start.27 = (bf16[48,8,128]{2,1,0:T(8,128)(2,1)S(1)}, bf16[48,8,128]{2,1,0:T(8,128)(2,1)S(1)}, u32[]{:S(2)}, u32[]{:S(2)}) collective-permute-start(bf16[48,8,128]{2,1,0:T(8,128)(2,1)S(1)} %get-tuple-element.89), channel_id=1, source_target_pairs={{0,10},{1,11},{2,8},{3,9},{4,14},{5,15},{6,12},{7,13},{8,2},{9,3},... | collective-permute-start | bytes 294920 | tf_op jit(solution)/shard_map/ppermute | solution.py:543
  197.4 13.5 %collective-permute-start.28 = (bf16[48,8,128]{2,1,0:T(8,128)(2,1)S(1)}, bf16[48,8,128]{2,1,0:T(8,128)(2,1)S(1)}, u32[]{:S(2)}, u32[]{:S(2)}) collective-permute-start(bf16[48,8,128]{2,1,0:T(8,128)(2,1)S(1)} %get-tuple-element.90), channel_id=1, source_target_pairs={{0,12},{1,13},{2,14},{3,15},{4,8},{5,9},{6,10},{7,11},{8,4},{9,5},... | collective-permute-start | bytes 294920 | tf_op jit(solution)/shard_map/ppermute | solution.py:543
  198.6 12.3 %collective-permute-start.29 = (bf16[48,8,128]{2,1,0:T(8,128)(2,1)S(1)}, bf16[48,8,128]{2,1,0:T(8,128)(2,1)S(1)}, u32[]{:S(2)}, u32[]{:S(2)}) collective-permute-start(bf16[48,8,128]{2,1,0:T(8,128)(2,1)S(1)} %get-tuple-element.91), channel_id=1, source_target_pairs={{0,14},{1,15},{2,12},{3,13},{4,10},{5,11},{6,8},{7,9},{8,6},{9,7},... | collective-permute-start | bytes 294920 | tf_op jit(solution)/shard_map/ppermute | solution.py:543
